TPU v7x, 32 devices: a whole 2x2x4 slice. The times are simulated.
32 devices in a mesh: req: 4 (over y, x), seq: 8 (over z, core).
Axes of the slice: x: 2, y: 2, z: 4, core: 2. Of those that a mesh axis runs over, the one named last changes fastest.
Arguments:
- query_rows: bfloat16 [4096, 2048], P(('req', 'seq')), parts along dimension 0, may hold values from -6 to 6
- key_rows: bfloat16 [4096, 2048], P(('req', 'seq')), parts along dimension 0, may hold values from -6 to 6
- value_rows: bfloat16 [4096, 2048], P(('req', 'seq')), parts along dimension 0, may hold values from -6 to 6
- query_taps: float32 [4, 2048], replicated, may hold values from -3 to 3
- key_taps: float32 [4, 2048], replicated, may hold values from -3 to 3
- value_taps: float32 [4, 2048], replicated, may hold values from -3 to 3
- log_alpha: float32 [16, 4096], P(None, ('req', 'seq')), parts along dimension 1, may hold values from -1 to 0
- write_strength: float32 [16, 4096], P(None, ('req', 'seq')), parts along dimension 1, may hold values from 0 to 1
- tier_mixture: float32 [11, 16, 4096], P(None, None, ('req', 'seq')), parts along dimension 2, may hold values from 0.25 to 4
- output_gate: bfloat16 [4096, 2048], P(('req', 'seq')), parts along dimension 0, may hold values from -6 to 6
- norm_gain: float32 [128], replicated, may hold values from 0.1 to 1.9
Outputs:
- layer_output: bfloat16 [4096, 2048], P(('req', 'seq')), parts along dimension 0
There are 4 independent parts, one for each index of `req`. A program takes and returns all parts, laid end to end along the dimension named above; an argument that names none is the same for every part. Nothing has to cross between parts.
All inputs are finite; a program needn't handle non-finite values.
Results may differ from a plain program's by a relative error of at most 0.001.
Values may be sent and summed in bfloat16 or wider, within the bound.
No kernel may reach another device: no remote copies, remote signals or barrier semaphores. Data moves between devices by JAX's collectives and lax.ppermute only.
A program may use at most 128 MiB of HBM per device.

v0:
```python
import functools

import jax
import jax.numpy as jnp
from jax import lax
from jax.experimental import pallas as pl
from jax.experimental.pallas import tpu as pltpu
from jax.sharding import PartitionSpec as P

HEAD_DIM = 128
CHUNK = 128
CODE = 125.0
F32 = jnp.float32
BF16 = jnp.bfloat16


def split(x):
    high = x.astype(BF16)
    return high, (x - high.astype(F32)).astype(BF16)


def dot(a, b):
    return jnp.dot(a, b, preferred_element_type=F32)


def wide(b):
    row = jnp.concatenate(b, axis=1)
    return jnp.concatenate([row, row], axis=0)


def mm(a, b):
    width = b[0].shape[1]
    if width > 128:
        both = jnp.concatenate([b[0], b[0]], axis=0)
        return dot(jnp.concatenate(a, axis=1), both) + dot(a[0], b[1])
    out = dot(jnp.concatenate(a, axis=1), wide(b))
    return out[:, :width] + out[:, width:]


def silu(u):
    return u / (1.0 + jnp.exp(-u))


def encode(state):
    top = jnp.max(jnp.abs(state), axis=0, keepdims=True)
    scale = (top * 1.02 + 1e-30).astype(BF16).astype(F32)
    grade = jnp.abs(state) / scale
    level = jnp.exp2(grade * (2.0 * CODE) - CODE)
    return jnp.where(state < 0, -level, level).astype(BF16), scale


def decode(code, scale):
    grade = jnp.log2(jnp.abs(code)) * (0.5 / CODE) + 0.5
    size = grade * scale
    return jnp.where(code < 0, -size, size)


def iotas(rows, columns):
    return (
        lax.broadcasted_iota(jnp.int32, (rows, columns), 0),
        lax.broadcasted_iota(jnp.int32, (rows, columns), 1),
    )


def place():
    index = lax.axis_index("seq")
    return index % 2, index // 2


def fill(scratch, own, other, halo, core, first):
    scratch[0:8, :] = jnp.zeros((8, scratch.shape[1]), F32)
    scratch[5:8, :] = halo[first : first + 3]
    start = pl.multiple_of(8 + CHUNK * core, 8)
    scratch[pl.ds(start, CHUNK), :] = own[...].astype(F32)
    start = pl.multiple_of(8 + CHUNK * (1 - core), 8)
    scratch[pl.ds(start, CHUNK), :] = other[...].astype(F32)


def conv(scratch, taps, chunk, columns):
    total = None
    for tap in range(4):
        part = taps[tap : tap + 1, columns] * scratch[
            5 + tap + CHUNK * chunk : 5 + tap + CHUNK * chunk + CHUNK, columns
        ]
        total = part if total is None else total + part
    return silu(total)


def unit(rows):
    return rows * lax.rsqrt(jnp.sum(rows * rows, axis=-1, keepdims=True) + 1e-6)


def token_row(own, other, row, core, chunk):
    return jnp.where(core == chunk, own[pl.ds(row, 1), :], other[pl.ds(row, 1), :])


def sums(own, other, heads, core, step):
    base = 8 * core + heads * step
    rows = [
        token_row(own, other, base + head, core, chunk)
        for head in range(heads)
        for chunk in range(2)
    ]
    pad = -len(rows) % 8
    if pad:
        rows.append(jnp.zeros((pad, CHUNK), F32))
    t, j = iotas(CHUNK, CHUNK)
    upper = (t <= j).astype(F32)
    return jnp.dot(
        jnp.concatenate(rows, axis=0),
        upper,
        preferred_element_type=F32,
        precision=lax.Precision.HIGHEST,
    )


def invert(coupling, t, j):
    apart = t ^ j
    count = len(coupling)
    near = [split(jnp.where(apart < 8, -a, 0.0)) for a in coupling]
    eye = (t == j).astype(F32)
    squared = [mm(n, n) for n in near]
    grown = []
    fourth = []
    for i in range(count):
        base = eye + near[i][0].astype(F32) + near[i][1].astype(F32)
        left = split(jnp.concatenate([squared[i], base], axis=0))
        both = mm(left, split(squared[i]))
        fourth.append(both[:CHUNK])
        grown.append(base + both[CHUNK:])
    inverse = [
        grown[i] + mm(split(grown[i]), split(fourth[i])) for i in range(count)
    ]
    inverse = [split(x) for x in inverse]
    size = 8
    while size < CHUNK:
        starts = range(size, CHUNK, 2 * size)

        def pick(x):
            return jnp.concatenate([x[s : s + size] for s in starts], axis=0)

        zero = jnp.zeros((size, CHUNK), BF16)

        def spread(x):
            pieces = []
            for k in range(len(starts)):
                pieces += [zero, x[k * size : (k + 1) * size]]
            return jnp.concatenate(pieces, axis=0)

        def merge(x, rows):
            pieces = []
            for k, s in enumerate(starts):
                pieces += [x[s - size : s], rows[k * size : (k + 1) * size]]
            return jnp.concatenate(pieces, axis=0)

        mask = pick((apart >= size) & (apart < 2 * size))
        middle = []
        for i in range(count):
            lower = split(jnp.where(mask, pick(coupling[i]), 0.0))
            middle.append(split(mm(lower, inverse[i])))
        for i in range(count):
            high, low = inverse[i]
            rows = (pick(high), pick(low))
            change = mm(rows, tuple(spread(m) for m in middle[i]))
            fresh = split(rows[0].astype(F32) + rows[1].astype(F32) - change)
            inverse[i] = (merge(high, fresh[0]), merge(low, fresh[1]))
        size *= 2
    return inverse


def decay(column, row, t, j):
    return jnp.exp(jnp.where(t >= j, column - row, -1e30))


def states_kernel(
    heads,
    key_own,
    key_other,
    value_own,
    value_other,
    key_taps,
    value_taps,
    halo_one,
    halo_two,
    small_own,
    small_other,
    key_cols_out,
    inverse_out,
    write_out,
    first_state_out,
    state_out,
    transit_one_out,
    transit_out,
    code_out,
    key_scratch,
    value_scratch,
    scale_scratch,
):
    core, _ = place()
    step = pl.program_id(0)
    halo = halo_one[...].astype(F32) + halo_two[...].astype(F32)
    fill(key_scratch, key_own, key_other, halo, core, 3)
    fill(value_scratch, value_own, value_other, halo, core, 6)
    t, j = iotas(CHUNK, CHUNK)
    run = sums(small_own, small_other, heads, core, step)
    strengths = [
        token_row(small_own, small_other, 16 + 8 * core + heads * step + head, core, chunk)
        for head in range(heads)
        for chunk in range(2)
    ]
    table = jnp.concatenate([run[: 2 * heads]] + strengths, axis=0)
    pad = -table.shape[0] % 8
    if pad:
        table = jnp.concatenate([table, jnp.zeros((pad, CHUNK), F32)], axis=0)
    columns = table.T
    parts = [(head, chunk) for head in range(heads) for chunk in range(2)]
    key_cols = []
    key_units = []
    coupling = []
    for i, (head, chunk) in enumerate(parts):
        lanes = slice(head * 128, head * 128 + 128)
        key = unit(conv(key_scratch, key_taps, chunk, lanes))
        key_t = key.T
        key_cols.append(key_t)
        key_units.append(key)
        pair = split(key_t)
        key_cols_out[head, chunk, 0] = pair[0]
        key_cols_out[head, chunk, 1] = pair[1]
        gram = mm(split(key), pair)
        ratio = decay(columns[:, i : i + 1], run[i : i + 1], t, j)
        beta = columns[:, 2 * heads + i : 2 * heads + i + 1]
        coupling.append(jnp.where(t > j, gram * ratio * beta, 0.0))
    inverse = invert(coupling, t, j)
    transits = []
    states = []
    for i, (head, chunk) in enumerate(parts):
        lanes = slice(head * 128, head * 128 + 128)
        inverse_out[head, chunk, 0] = inverse[i][0]
        inverse_out[head, chunk, 1] = inverse[i][1]
        value = conv(value_scratch, value_taps, chunk, lanes)
        beta = columns[:, 2 * heads + i : 2 * heads + i + 1]
        grow = jnp.exp(columns[:, i : i + 1])
        write = jnp.concatenate([key_units[i] * (beta * grow), value * beta], axis=1)
        write = split(write)
        write_out[head, chunk, 0] = write[0]
        write_out[head, chunk, 1] = write[1]
        last = run[i : i + 1, CHUNK - 1 : CHUNK]
        tail = key_cols[i] * jnp.exp(last - run[i : i + 1])
        mixed = mm(split(tail), inverse[i])
        both = mm(split(mixed), write)
        transits.append(jnp.where(t == j, jnp.exp(last), 0.0) - both[:, :128])
        states.append(both[:, 128:])
    for head in range(heads):
        low, high = 2 * head, 2 * head + 1
        first = split(states[low])
        low_transit = split(transits[low])
        pair = split(transits[high])
        state = mm(pair, first) + states[high]
        transit = mm(pair, low_transit)
        first_state_out[head] = states[low]
        transit_one_out[head] = transits[low]
        state_out[head] = state
        transit_out[head] = transit
        code, scale = encode(state)
        index = heads * step + head
        code_out[pl.ds(pl.multiple_of(index * 128, 128), 128), :] = code
        scale_scratch[index] = scale

    @pl.when(step == pl.num_programs(0) - 1)
    def _():
        rows = [scale_scratch[h] for h in range(8)]
        rows.append(jnp.zeros((8, 128), F32))
        code_out[1024:1040, :] = jnp.concatenate(rows, axis=0).astype(BF16)


def queries_kernel(
    heads,
    near,
    query_own,
    query_other,
    query_taps,
    halo_one,
    halo_two,
    small_own,
    small_other,
    key_cols,
    inverse,
    write,
    first_state,
    transit_one,
    out,
    moved,
    query_scratch,
):
    core, _ = place()
    step = pl.program_id(0)
    halo = halo_one[...].astype(F32) + halo_two[...].astype(F32)
    fill(query_scratch, query_own, query_other, halo, core, 0)
    t, j = iotas(CHUNK, CHUNK)
    apart = t ^ j
    run = sums(small_own, small_other, heads, core, step)
    parts = [(head, chunk) for head in range(heads) for chunk in range(2)]
    rows = [run[: 2 * heads]]
    for head, chunk in parts:
        for level in range(near + 1):
            row = 32 + 16 * level + 8 * core + heads * step + head
            rows.append(token_row(small_own, small_other, row, core, chunk))
    table = jnp.concatenate(rows, axis=0)
    pad = -table.shape[0] % 8
    if pad:
        table = jnp.concatenate([table, jnp.zeros((pad, CHUNK), F32)], axis=0)
    columns = table.T
    for i, (head, chunk) in enumerate(parts):
        lanes = slice(head * 128, head * 128 + 128)
        query = unit(conv(query_scratch, query_taps, chunk, lanes))
        ratio = decay(columns[:, i : i + 1], run[i : i + 1], t, j)
        scores = mm(split(query), (key_cols[head, chunk, 0], key_cols[head, chunk, 1])) * ratio
        mixing = mm(split(scores), (inverse[head, chunk, 0], inverse[head, chunk, 1]))
        at = 2 * heads + i * (near + 1)
        level_mat = columns[:, at : at + 1]
        for level in range(1, near):
            weight = columns[:, at + level : at + level + 1]
            level_mat = jnp.where(apart >= 1 << (level - 1), weight, level_mat)
        high, low = (write[head, chunk, 0], write[head, chunk, 1])
        within = mm(split(mixing * level_mat), (high[:, 128:], low[:, 128:]))
        grow = jnp.exp(columns[:, i : i + 1])
        effective = grow * query - mm(split(mixing), (high[:, :128], low[:, :128]))
        rows = pl.ds(chunk * CHUNK, CHUNK)
        if chunk:
            pair = split(effective)
            weight = columns[:, at + near : at + near + 1]
            within = within + weight * mm(pair, split(first_state[head]))
            effective = mm(pair, split(transit_one[head]))
        out[head, rows, :] = within
        moved[head, rows, :] = effective


def received(refs, head):
    code = None
    scale = None
    for ref in refs:
        part = ref[head * 128 : head * 128 + 128, :].astype(F32)
        row = ref[1024 + head : 1025 + head, :].astype(F32)
        code = part if code is None else code + part
        scale = row if scale is None else scale + row
    return decode(code, scale)


def pack_rows(scales):
    return jnp.concatenate(scales + [jnp.zeros((8, 128), F32)], axis=0).astype(BF16)


def join_kernel(level, arrivals, with_transit, *refs):
    state_in = refs[:arrivals]
    refs = refs[arrivals:]
    transit_in = ()
    if with_transit:
        transit_in = refs[:arrivals]
        refs = refs[arrivals:]
    state, transit, refs = refs[0], refs[1], refs[2:]
    code_out, refs = refs[0], refs[1:]
    _, node = place()
    upper = (node >> level) % 2 == 1

    @pl.when(upper)
    def _():
        scales = []
        for head in range(8):
            pair = split(transit[head])
            fresh = mm(pair, split(received(state_in, head))) + state[head]
            code, scale = encode(fresh)
            code_out[head * 128 : head * 128 + 128, :] = code
            scales.append(scale)
            if with_transit:
                refs[0][head] = fresh
                refs[1][head] = mm(pair, split(received(transit_in, head)))
        code_out[1024:1040, :] = pack_rows(scales)
        if with_transit:
            scales = []
            for head in range(8):
                code, scale = encode(refs[1][head])
                refs[2][head * 128 : head * 128 + 128, :] = code
                scales.append(scale)
            refs[2][1024:1040, :] = pack_rows(scales)

    @pl.when(jnp.logical_not(upper))
    def _():
        scales = []
        for head in range(8):
            code, scale = encode(state[head])
            code_out[head * 128 : head * 128 + 128, :] = code
            scales.append(scale)
            if with_transit:
                refs[0][head] = state[head]
                refs[1][head] = transit[head]
        code_out[1024:1040, :] = pack_rows(scales)
        if with_transit:
            scales = []
            for head in range(8):
                code, scale = encode(transit[head])
                refs[2][head * 128 : head * 128 + 128, :] = code
                scales.append(scale)
            refs[2][1024:1040, :] = pack_rows(scales)


def code_kernel(value, code_out):
    scales = []
    for head in range(8):
        code, scale = encode(value[head])
        code_out[head * 128 : head * 128 + 128, :] = code
        scales.append(scale)
    code_out[1024:1040, :] = pack_rows(scales)


def level_weight(own, other, row, core):
    rows = [token_row(own, other, row, core, chunk) for chunk in range(2)]
    rows.append(jnp.zeros((6, CHUNK), F32))
    columns = jnp.concatenate(rows, axis=0).T
    return jnp.concatenate([columns[:, 0:1], columns[:, 1:2]], axis=0)


def absorb_kernel(level, weight_row, arrivals, *refs):
    state_in = refs[:arrivals]
    transit_in = refs[arrivals : 2 * arrivals]
    small_own, small_other, out_in, moved_in, out, moved = refs[2 * arrivals :]
    core, node = place()
    upper = (node >> level) % 2 == 1
    later = (node >> (level + 1)) > 0

    @pl.when(upper)
    def _():
        for head in range(8):
            pair = split(moved_in[head])
            weight = level_weight(small_own, small_other, weight_row + 8 * core + head, core)
            gain = mm(pair, split(received(state_in, head)))
            out[head] = out_in[head] + weight * gain

    @pl.when(jnp.logical_not(upper))
    def _():
        out[...] = out_in[...]

    @pl.when(upper & later)
    def _():
        for head in range(8):
            moved[head] = mm(split(moved_in[head]), split(received(transit_in, head)))

    @pl.when(jnp.logical_not(upper & later))
    def _():
        moved[...] = moved_in[...]


def finish_kernel(level, weight_row, arrivals, *refs):
    state_in = refs[:arrivals]
    (small_own, small_other, out_in, moved_in, gate_own, gate_other, gain, out, total) = refs[
        arrivals:
    ]
    core, node = place()
    upper = (node >> level) % 2 == 1

    @pl.when(upper)
    def _():
        for head in range(8):
            weight = level_weight(small_own, small_other, weight_row + 8 * core + head, core)
            extra = mm(split(moved_in[head]), split(received(state_in, head)))
            total[head] = out_in[head] + weight * extra

    @pl.when(jnp.logical_not(upper))
    def _():
        total[...] = out_in[...]

    for head in range(8):
        lanes = slice(head * 128, head * 128 + 128)
        attended = total[head]
        scale = lax.rsqrt(jnp.mean(attended * attended, axis=-1, keepdims=True) + 1e-5)
        normed = attended * scale * gain[...]
        total[head] = normed
        for source, chunk in ((gate_own, core), (gate_other, 1 - core)):
            rows = pl.ds(pl.multiple_of(chunk * CHUNK, CHUNK), CHUNK)
            gated = total[head, rows, :] * silu(source[:, lanes].astype(F32))
            out[rows, lanes] = gated.astype(BF16)


def halo_kernel(query, key, value, out):
    rows = [x[13:16, :].astype(F32) for x in (query, key, value)]
    rows.append(jnp.zeros((7, query.shape[1]), F32))
    out[...] = jnp.concatenate(rows, axis=0).astype(BF16)


def swap_kernel(own, other, out):
    core, _ = place()
    width = own.shape[1]
    start = pl.multiple_of(core * width, width)
    out[:, pl.ds(start, width)] = own[pl.ds(pl.multiple_of(core * CHUNK, CHUNK), CHUNK), :]
    start = pl.multiple_of((1 - core) * width, width)
    out[:, pl.ds(start, width)] = other[...]


def struct(shape, dtype=F32):
    return jax.ShapeDtypeStruct(shape, dtype)


PARAMS = pltpu.CompilerParams(vmem_limit_bytes=48 << 20)


def per_device(
    query_rows,
    key_rows,
    value_rows,
    query_taps,
    key_taps,
    value_taps,
    log_alpha,
    write_strength,
    tier_mixture,
    output_gate,
    norm_gain,
):
    rows, width = query_rows.shape
    half = width // 2
    size = lax.axis_size("seq")
    nodes = size // 2
    level_total = tier_mixture.shape[0]
    near = CHUNK.bit_length()
    cores = [(i, i ^ 1) for i in range(size)]
    small = jnp.concatenate(
        [log_alpha, write_strength, tier_mixture.reshape(level_total * 16, rows)], axis=0
    )
    halo = pl.pallas_call(
        halo_kernel,
        grid=(1,),
        in_specs=[pl.BlockSpec((16, width), lambda i: (rows // 16 - 1, 0))] * 3,
        out_specs=pl.BlockSpec((16, width), lambda i: (0, 0)),
        out_shape=struct((16, width), BF16),
        name="halo",
    )(query_rows, key_rows, value_rows)
    halo_one = lax.ppermute(halo, "seq", [(i, i + 1) for i in range(1, size - 1, 2)])
    halo_two = lax.ppermute(halo, "seq", [(i, i + 2) for i in range(1, size - 1, 2)])
    key_other = lax.ppermute(key_rows, "seq", cores)
    value_other = lax.ppermute(value_rows, "seq", cores)
    small_other = lax.ppermute(small, "seq", cores)
    query_other = lax.ppermute(query_rows, "seq", cores)
    gate_other = lax.ppermute(output_gate, "seq", cores)

    heads = 2
    steps = 8 // heads
    lanes = heads * 128

    def feature(row_count):
        return pl.BlockSpec(
            (row_count, lanes), lambda g: (0, (lax.axis_index("seq") % 2) * steps + g)
        )

    def whole(shape):
        return pl.BlockSpec(shape, lambda g: (0,) * len(shape))

    def by_head(*tail):
        return pl.BlockSpec((heads,) + tail, lambda g: (g,) + (0,) * len(tail))

    small_spec = whole(small.shape)
    pair = (2, 2, 128, 128)
    pair_wide = (2, 2, 128, 256)
    square = (128, 128)
    (key_cols, inverse, write, first_state, state, transit_one, transit, code) = pl.pallas_call(
        functools.partial(states_kernel, heads),
        grid=(steps,),
        in_specs=[feature(rows)] * 4
        + [feature(4)] * 2
        + [feature(16)] * 2
        + [small_spec, small_spec],
        out_specs=[
            by_head(*pair),
            by_head(*pair),
            by_head(*pair_wide),
            by_head(*square),
            by_head(*square),
            by_head(*square),
            by_head(*square),
            whole((1040, 128)),
        ],
        out_shape=[
            struct((8,) + pair, BF16),
            struct((8,) + pair, BF16),
            struct((8,) + pair_wide, BF16),
            struct((8,) + square),
            struct((8,) + square),
            struct((8,) + square),
            struct((8,) + square),
            struct((1040, 128), BF16),
        ],
        scratch_shapes=[
            pltpu.VMEM((8 + 2 * CHUNK, lanes), F32),
            pltpu.VMEM((8 + 2 * CHUNK, lanes), F32),
            pltpu.VMEM((8, 1, 128), F32),
        ],
        compiler_params=PARAMS,
        cost_estimate=pl.CostEstimate(
            flops=8_000_000_000, bytes_accessed=12_000_000, transcendentals=0
        ),
        name="states",
    )(
        key_rows,
        key_other,
        value_rows,
        value_other,
        key_taps,
        value_taps,
        halo_one,
        halo_two,
        small,
        small_other,
    )

    shard_bits = nodes.bit_length() - 1

    def fan(value, level, keep):
        span = 1 << level
        results = []
        for offset in range(span):
            route = []
            for low in range(0, nodes, 2 * span):
                source, target = low + span - 1, low + span + offset
                if keep(target):
                    route += [(2 * source + c, 2 * target + c) for c in range(2)]
            results.append(lax.ppermute(value, "seq", route))
        return results

    arrived = fan(code, 0, lambda target: True) if shard_bits else []

    moved_shape = struct((8, 2 * CHUNK, 128))
    out, moved = pl.pallas_call(
        functools.partial(queries_kernel, heads, near),
        grid=(steps,),
        in_specs=[feature(rows)] * 2
        + [feature(4)]
        + [feature(16)] * 2
        + [small_spec, small_spec]
        + [
            by_head(*pair),
            by_head(*pair),
            by_head(*pair_wide),
            by_head(*square),
            by_head(*square),
        ],
        out_specs=[by_head(2 * CHUNK, 128)] * 2,
        out_shape=[moved_shape, moved_shape],
        scratch_shapes=[pltpu.VMEM((8 + 2 * CHUNK, lanes), F32)],
        compiler_params=PARAMS,
        cost_estimate=pl.CostEstimate(
            flops=6_000_000_000, bytes_accessed=10_000_000, transcendentals=0
        ),
        name="queries",
    )(
        query_rows,
        query_other,
        query_taps,
        halo_one,
        halo_two,
        small,
        small_other,
        key_cols,
        inverse,
        write,
        first_state,
        transit_one,
    )

    transit_code = None
    if shard_bits > 1:
        transit_code = pl.pallas_call(
            code_kernel,
            out_shape=struct((1040, 128), BF16),
            compiler_params=PARAMS,
            name="code",
        )(transit)
    for level in range(shard_bits - 1):
        keeps = level < shard_bits - 2
        transit_arrived = fan(
            transit_code, level, lambda target: keeps or target >> (level + 1) > 0
        )
        shapes = [struct((1040, 128), BF16)]
        operands = list(arrived)
        if keeps:
            shapes += [struct((8, 128, 128)), struct((8, 128, 128)), struct((1040, 128), BF16)]
            operands += transit_arrived
        joined = pl.pallas_call(
            functools.partial(join_kernel, level, len(arrived), keeps),
            out_shape=shapes,
            compiler_params=PARAMS,
            cost_estimate=pl.CostEstimate(
                flops=300_000_000, bytes_accessed=2_000_000, transcendentals=0
            ),
            name="join",
        )(*operands, state, transit)
        code = joined[0]
        following = fan(code, level + 1, lambda target: True)
        if keeps:
            state, transit, transit_code = joined[1:]
        out, moved = pl.pallas_call(
            functools.partial(
                absorb_kernel, level, 32 + 16 * (near + 1 + level), len(arrived)
            ),
            out_shape=[moved_shape, moved_shape],
            compiler_params=PARAMS,
            cost_estimate=pl.CostEstimate(
                flops=1_500_000_000, bytes_accessed=6_000_000, transcendentals=0
            ),
            name="absorb",
        )(*arrived, *transit_arrived, small, small_other, out, moved)
        arrived = following

    level = max(shard_bits - 1, 0)
    core_half = pl.BlockSpec((rows, half), lambda i: (0, lax.axis_index("seq") % 2))
    full = lambda x: pl.BlockSpec(x.shape, lambda i: (0,) * x.ndim)
    gain = norm_gain.reshape(1, 128)
    operands = list(arrived) + [small, small_other, out, moved]
    result = pl.pallas_call(
        functools.partial(finish_kernel, level, 32 + 16 * (near + 1 + level), len(arrived)),
        grid=(1,),
        in_specs=[full(x) for x in operands] + [core_half, core_half, full(gain)],
        out_specs=pl.BlockSpec((2 * rows, half), lambda i: (0, 0)),
        out_shape=struct((2 * rows, half), BF16),
        scratch_shapes=[pltpu.VMEM((8, 2 * CHUNK, 128), F32)],
        compiler_params=PARAMS,
        name="finish",
    )(*operands, output_gate, gate_other, gain)
    core = lax.axis_index("seq") % 2
    leaving = lax.dynamic_slice(result, ((1 - core) * rows, 0), (rows, half))
    coming = lax.ppermute(leaving, "seq", cores)
    return pl.pallas_call(
        swap_kernel,
        out_shape=struct((rows, width), BF16),
        compiler_params=PARAMS,
        name="swap",
    )(result, coming)


def solution(mesh):
    placed = (
        P(("req", "seq"), None),
        P(("req", "seq"), None),
        P(("req", "seq"), None),
        P(),
        P(),
        P(),
        P(None, ("req", "seq")),
        P(None, ("req", "seq")),
        P(None, None, ("req", "seq")),
        P(("req", "seq"), None),
        P(),
    )
    return jax.shard_map(
        per_device, mesh=mesh, in_specs=placed, out_specs=P(("req", "seq"), None), check_vma=False
    )
```

profile of v0, /device:TPU:11, one launch (start us, length us, event | category | flops | bytes accessed | tf_op | source)
XLA Modules:
  0.0 63.5 jit_solution(2971568646353571054)
XLA Ops:
  0.7 0.9 %pad_maximum_fusion.small_own.refs_2_ = f32[208,128]{1,0:T(8,128)S(1)} fusion(f32[176,128]{1,0:T(8,128)} %bitcast.3, f32[16,128]{1,0:T(8,128)} %param.18, f32[16,128]{1,0:T(8,128)} %param.17), kind=kLoop, calls=%fused_computation | loop fusion | flops 53248 | bytes 212992 | tf_op jit(solution)/shard_map/concatenate | solution.py:525
  2.2 1.6 %halo.1 = bf16[16,2048]{1,0:T(8,128)(2,1)} custom-call(bf16[128,2048]{1,0:T(8,128)(2,1)} %query_own.1, bf16[128,2048]{1,0:T(8,128)(2,1)} %key_own.1, bf16[128,2048]{1,0:T(8,128)(2,1)} %value_own.1), custom_call_target="tpu_custom_call" | custom-call | tf_op jit(solution)/shard_map/halo/pallas_call | solution.py:528
  3.8 3.1 %collective-permute-start.2 = (bf16[16,2048]{1,0:T(8,128)(2,1)}, bf16[16,2048]{1,0:T(8,128)(2,1)S(1)}, u32[]{:S(2)}, u32[]{:S(2)}) collective-permute-start(bf16[16,2048]{1,0:T(8,128)(2,1)} %halo.1), channel_id=1, source_target_pairs={{1,2},{3,4},{5,6},{9,10},{11,12},{13,14},{17,18},{19,20},{21,22},{... | collective-permute-start | bytes 196616 | tf_op jit(solution)/shard_map/ppermute | solution.py:536
  6.9 3.2 %collective-permute-start.3 = (bf16[16,2048]{1,0:T(8,128)(2,1)}, bf16[16,2048]{1,0:T(8,128)(2,1)S(1)}, u32[]{:S(2)}, u32[]{:S(2)}) collective-permute-start(bf16[16,2048]{1,0:T(8,128)(2,1)} %halo.1), channel_id=1, source_target_pairs={{1,3},{3,5},{5,7},{9,11},{11,13},{13,15},{17,19},{19,21},{21,23},{... | collective-permute-start | bytes 196616 | tf_op jit(solution)/shard_map/ppermute | solution.py:537
  10.2 1.9 %collective-permute-done.3.halo_two = bf16[16,2048]{1,0:T(8,128)(2,1)S(1)} collective-permute-done((bf16[16,2048]{1,0:T(8,128)(2,1)}, bf16[16,2048]{1,0:T(8,128)(2,1)S(1)}, u32[]{:S(2)}, u32[]{:S(2)}) %collective-permute-start.3) | collective-permute-done | bytes 65568 | tf_op jit(solution)/shard_map/ppermute | solution.py:537
  12.1 1.0 %copy-done = bf16[128,2048]{1,0:T(8,128)(2,1)S(1)} copy-done((bf16[128,2048]{1,0:T(8,128)(2,1)S(1)}, bf16[128,2048]{1,0:T(8,128)(2,1)}, u32[]{:S(2)}) %copy-start) | copy-done | bytes 524312
  13.2 1.0 %copy-done.1 = bf16[128,2048]{1,0:T(8,128)(2,1)S(1)} copy-done((bf16[128,2048]{1,0:T(8,128)(2,1)S(1)}, bf16[128,2048]{1,0:T(8,128)(2,1)}, u32[]{:S(2)}) %copy-start.1) | copy-done | bytes 524312
  14.2 0.8 %copy-done.5 = f32[4,2048]{1,0:T(4,128)S(1)} copy-done((f32[4,2048]{1,0:T(4,128)S(1)}, f32[4,2048]{1,0:T(4,128)}, u32[]{:S(2)}) %copy-start.5) | copy-done | bytes 32792
  15.0 0.8 %copy-done.6 = f32[4,2048]{1,0:T(4,128)S(1)} copy-done((f32[4,2048]{1,0:T(4,128)S(1)}, f32[4,2048]{1,0:T(4,128)}, u32[]{:S(2)}) %copy-start.6) | copy-done | bytes 32792
  15.7 15.5 %states.1 = (bf16[8,2,2,128,128]{4,3,2,1,0:T(8,128)(2,1)S(1)}, bf16[8,2,2,128,128]{4,3,2,1,0:T(8,128)(2,1)}, bf16[8,2,2,128,256]{4,3,2,1,0:T(8,128)(2,1)}, f32[8...) custom-call(bf16[128,2048]{1,0:T(8,128)(2,1)S(1)} %copy-done, ...), custom_call_target="tpu_custom_call" | custom-call | flops 8000000000 | bytes 12000000 | tf_op jit(solution)/shard_map/states/pallas_call | solution.py:563
  31.3 1.0 %copy-done.8 = bf16[8,2,2,128,128]{4,3,2,1,0:T(8,128)(2,1)} copy-done((bf16[8,2,2,128,128]{4,3,2,1,0:T(8,128)(2,1)}, bf16[8,2,2,128,128]{4,3,2,1,0:T(8,128)(2,1)S(1)}, u32[]{:S(2)}) %copy-start.8) | copy-done | bytes 1048600
  32.2 0.8 %copy-done.10 = f32[8,128,128]{2,1,0:T(8,128)} copy-done((f32[8,128,128]{2,1,0:T(8,128)}, f32[8,128,128]{2,1,0:T(8,128)S(1)}, u32[]{:S(2)}) %copy-start.10) | copy-done | bytes 524312
  33.0 0.8 %copy-done.12 = f32[8,128,128]{2,1,0:T(8,128)} copy-done((f32[8,128,128]{2,1,0:T(8,128)}, f32[8,128,128]{2,1,0:T(8,128)S(1)}, u32[]{:S(2)}) %copy-start.12) | copy-done | bytes 524312
  33.8 1.4 %collective-permute-start.5 = (bf16[1040,128]{1,0:T(8,128)(2,1)S(1)}, bf16[1040,128]{1,0:T(8,128)(2,1)S(1)}, u32[]{:S(2)}, u32[]{:S(2)}) collective-permute-start(bf16[1040,128]{1,0:T(8,128)(2,1)S(1)} %get-tuple-element.17), channel_id=1, source_target_pairs={{0,2},{1,3},{4,6},{5,7},{8,10},{9,11},{12,14},{13,15},{16,18},{17,... | collective-permute-start | bytes 798728 | tf_op jit(solution)/shard_map/ppermute | solution.py:624
  35.6 0.8 %collective-permute-start.8 = (bf16[1040,128]{1,0:T(8,128)(2,1)S(1)}, bf16[1040,128]{1,0:T(8,128)(2,1)S(1)}, u32[]{:S(2)}, u32[]{:S(2)}) collective-permute-start(bf16[1040,128]{1,0:T(8,128)(2,1)S(1)} %code.1), channel_id=1, source_target_pairs={{4,6},{5,7},{12,14},{13,15},{20,22},{21,23},{28,30},{29,31}} | collective-permute-start | bytes 798728 | tf_op jit(solution)/shard_map/ppermute | solution.py:624
  36.4 6.6 %collective-permute-done.5.refs_0_ = bf16[1040,128]{1,0:T(8,128)(2,1)S(1)} collective-permute-done((bf16[1040,128]{1,0:T(8,128)(2,1)S(1)}, bf16[1040,128]{1,0:T(8,128)(2,1)S(1)}, u32[]{:S(2)}, u32[]{:S(2)}) %collective-permute-start.5) | collective-permute-done | bytes 266272 | tf_op jit(solution)/shard_map/ppermute | solution.py:624
  43.6 1.9 %collective-permute-start.6 = (bf16[1040,128]{1,0:T(8,128)(2,1)S(1)}, bf16[1040,128]{1,0:T(8,128)(2,1)S(1)}, u32[]{:S(2)}, u32[]{:S(2)}) collective-permute-start(bf16[1040,128]{1,0:T(8,128)(2,1)S(1)} %join.1), channel_id=1, source_target_pairs={{2,4},{3,5},{10,12},{11,13},{18,20},{19,21},{26,28},{27,29}} | collective-permute-start | bytes 798728 | tf_op jit(solution)/shard_map/ppermute | solution.py:624
  45.4 3.0 %collective-permute-start.7 = (bf16[1040,128]{1,0:T(8,128)(2,1)S(1)}, bf16[1040,128]{1,0:T(8,128)(2,1)S(1)}, u32[]{:S(2)}, u32[]{:S(2)}) collective-permute-start(bf16[1040,128]{1,0:T(8,128)(2,1)S(1)} %join.1), channel_id=1, source_target_pairs={{2,6},{3,7},{10,14},{11,15},{18,22},{19,23},{26,30},{27,31}} | collective-permute-start | bytes 798728 | tf_op jit(solution)/shard_map/ppermute | solution.py:624
  48.5 1.0 %copy-done.13 = f32[8,128,128]{2,1,0:T(8,128)S(1)} copy-done((f32[8,128,128]{2,1,0:T(8,128)S(1)}, f32[8,128,128]{2,1,0:T(8,128)}, u32[]{:S(2)}) %copy-start.13) | copy-done | bytes 524312
  49.5 9.4 %queries.1 = (f32[8,256,128]{2,1,0:T(8,128)S(1)}, f32[8,256,128]{2,1,0:T(8,128)S(1)}) custom-call(bf16[128,2048]{1,0:T(8,128)(2,1)S(1)} %copy-done.2, bf16[128,2048]{1,0:T(8,128)(2,1)} %collective-permute-done.9.query_other, f32[4,2048]{1,0:T(4,128)S(1)} %copy-done.7, bf16[16,2048]{1,0:T(8,128)(2,1)S(1)} %collective-permute-done.2.halo_one, ...), custom_call_target="tpu_custom_call" | custom-call | flops 6000000000 | bytes 10000000 | tf_op jit(solution)/shard_map/queries/pallas_call | solution.py:630
  59.0 1.0 %absorb.1 = (f32[8,256,128]{2,1,0:T(8,128)S(1)}, f32[8,256,128]{2,1,0:T(8,128)S(1)}) custom-call(bf16[1040,128]{1,0:T(8,128)(2,1)S(1)} %collective-permute-done.5.refs_0_, bf16[1040,128]{1,0:T(8,128)(2,1)S(1)} %collective-permute-done.8.refs_1_, f32[208,128]{1,0:T(8,128)S(1)} %pad_maximum_fusion.small_own.refs_2_, ...), custom_call_target="tpu_custom_call" | custom-call | flops 1500000000 | bytes 6000000 | tf_op jit(solution)/shard_map/absorb/pallas_call | solution.py:698
  60.0 0.9 %finish.1.own = bf16[256,1024]{1,0:T(8,128)(2,1)S(1)} custom-call(bf16[1040,128]{1,0:T(8,128)(2,1)S(1)} %collective-permute-done.6.refs_0_, bf16[1040,128]{1,0:T(8,128)(2,1)S(1)} %collective-permute-done.7.refs_1_, f32[208,128]{1,0:T(8,128)S(1)} %pad_maximum_fusion.small_own.refs_2_, f32[208,128]{1,0:T(8,128)S(1)} %collective-permute-done.4.small_other.refs_3_, ...), custom_call_target="tpu_custom_call" | custom-call | tf_op jit(solution)/shard_map/finish/pallas_call | solution.py:716
  61.1 1.5 %collective-permute-done.11.other = bf16[128,1024]{1,0:T(8,128)(2,1)S(1)} collective-permute-done((bf16[128,1024]{1,0:T(8,128)(2,1)S(1)}, bf16[128,1024]{1,0:T(8,128)(2,1)S(1)}, u32[]{:S(2)}, u32[]{:S(2)}) %collective-permute-start.11) | collective-permute-done | bytes 262176 | tf_op jit(solution)/shard_map/ppermute | solution.py:728
  62.6 0.8 %swap.1 = bf16[128,2048]{1,0:T(8,128)(2,1)} custom-call(bf16[256,1024]{1,0:T(8,128)(2,1)S(1)} %finish.1.own, bf16[128,1024]{1,0:T(8,128)(2,1)S(1)} %collective-permute-done.11.other), custom_call_target="tpu_custom_call" | custom-call | tf_op jit(solution)/shard_map/swap/pallas_call | solution.py:729
  (38 shorter events, 2.4 us)
Async XLA Ops:
  0.0 12.1 %collective-permute-start = (bf16[128,2048]{1,0:T(8,128)(2,1)}, bf16[128,2048]{1,0:T(8,128)(2,1)S(1)}, u32[]{:S(2)}, u32[]{:S(2)}) collective-permute-start(bf16[128,2048]{1,0:T(8,128)(2,1)} %key_own.1), channel_id=1, source_target_pairs={{0,1},{1,0},{2,3},{3,2},{4,5},{5,4},{6,7},{7,6},{8,9},{9,8},{10,11... | collective-permute-start | bytes 1572872 | tf_op jit(solution)/shard_map/ppermute | solution.py:538
  0.7 11.4 %collective-permute-start.1 = (bf16[128,2048]{1,0:T(8,128)(2,1)}, bf16[128,2048]{1,0:T(8,128)(2,1)S(1)}, u32[]{:S(2)}, u32[]{:S(2)}) collective-permute-start(bf16[128,2048]{1,0:T(8,128)(2,1)} %value_own.1), channel_id=1, source_target_pairs={{0,1},{1,0},{2,3},{3,2},{4,5},{5,4},{6,7},{7,6},{8,9},{9,8},{10,11... | collective-permute-start | bytes 1572872 | tf_op jit(solution)/shard_map/ppermute | solution.py:539
  1.6 10.5 %collective-permute-start.4 = (f32[208,128]{1,0:T(8,128)S(1)}, f32[208,128]{1,0:T(8,128)S(1)}, u32[]{:S(2)}, u32[]{:S(2)}) collective-permute-start(f32[208,128]{1,0:T(8,128)S(1)} %pad_maximum_fusion.small_own.refs_2_), channel_id=1, source_target_pairs={{0,1},{1,0},{2,3},{3,2},{4,5},{5,4},{6,7},{7,6},{8,9},{9,8},{10,11... | collective-permute-start | bytes 319496 | tf_op jit(solution)/shard_map/ppermute | solution.py:540
  2.2 33.1 %copy-start.3 = (bf16[128,2048]{1,0:T(8,128)(2,1)S(1)}, bf16[128,2048]{1,0:T(8,128)(2,1)}, u32[]{:S(2)}) copy-start(bf16[128,2048]{1,0:T(8,128)(2,1)} %refs_6_.1) | copy-start | bytes 1572868
  3.8 6.3 %collective-permute-start.2 = (bf16[16,2048]{1,0:T(8,128)(2,1)}, bf16[16,2048]{1,0:T(8,128)(2,1)S(1)}, u32[]{:S(2)}, u32[]{:S(2)}) collective-permute-start(bf16[16,2048]{1,0:T(8,128)(2,1)} %halo.1), channel_id=1, source_target_pairs={{1,2},{3,4},{5,6},{9,10},{11,12},{13,14},{17,18},{19,20},{21,22},{... | collective-permute-start | bytes 196616 | tf_op jit(solution)/shard_map/ppermute | solution.py:536
  6.9 5.2 %collective-permute-start.3 = (bf16[16,2048]{1,0:T(8,128)(2,1)}, bf16[16,2048]{1,0:T(8,128)(2,1)S(1)}, u32[]{:S(2)}, u32[]{:S(2)}) collective-permute-start(bf16[16,2048]{1,0:T(8,128)(2,1)} %halo.1), channel_id=1, source_target_pairs={{1,3},{3,5},{5,7},{9,11},{11,13},{13,15},{17,19},{19,21},{21,23},{... | collective-permute-start | bytes 196616 | tf_op jit(solution)/shard_map/ppermute | solution.py:537
  10.1 38.3 %collective-permute-start.9 = (bf16[128,2048]{1,0:T(8,128)(2,1)}, bf16[128,2048]{1,0:T(8,128)(2,1)}, u32[]{:S(2)}, u32[]{:S(2)}) collective-permute-start(bf16[128,2048]{1,0:T(8,128)(2,1)} %query_own.1), channel_id=1, source_target_pairs={{0,1},{1,0},{2,3},{3,2},{4,5},{5,4},{6,7},{7,6},{8,9},{9,8},{10,11... | collective-permute-start | bytes 1572872 | tf_op jit(solution)/shard_map/ppermute | solution.py:541
  12.1 1.0 %copy-start = (bf16[128,2048]{1,0:T(8,128)(2,1)S(1)}, bf16[128,2048]{1,0:T(8,128)(2,1)}, u32[]{:S(2)}) copy-start(bf16[128,2048]{1,0:T(8,128)(2,1)} %key_own.1) | copy-start | bytes 1572868
  13.2 1.0 %copy-start.1 = (bf16[128,2048]{1,0:T(8,128)(2,1)S(1)}, bf16[128,2048]{1,0:T(8,128)(2,1)}, u32[]{:S(2)}) copy-start(bf16[128,2048]{1,0:T(8,128)(2,1)} %value_own.1) | copy-start | bytes 1572868
  31.3 1.0 %copy-start.8 = (bf16[8,2,2,128,128]{4,3,2,1,0:T(8,128)(2,1)}, bf16[8,2,2,128,128]{4,3,2,1,0:T(8,128)(2,1)S(1)}, u32[]{:S(2)}) copy-start(bf16[8,2,2,128,128]{4,3,2,1,0:T(8,128)(2,1)S(1)} %get-tuple-element.20.key_cols) | copy-start | bytes 3145732
  32.2 0.8 %copy-start.10 = (f32[8,128,128]{2,1,0:T(8,128)}, f32[8,128,128]{2,1,0:T(8,128)S(1)}, u32[]{:S(2)}) copy-start(f32[8,128,128]{2,1,0:T(8,128)S(1)} %get-tuple-element.23.first_state) | copy-start | bytes 1572868
  33.0 0.8 %copy-start.12 = (f32[8,128,128]{2,1,0:T(8,128)}, f32[8,128,128]{2,1,0:T(8,128)S(1)}, u32[]{:S(2)}) copy-start(f32[8,128,128]{2,1,0:T(8,128)S(1)} %get-tuple-element.24.transit_one) | copy-start | bytes 1572868
  33.8 14.6 %copy-start.2 = (bf16[128,2048]{1,0:T(8,128)(2,1)S(1)}, bf16[128,2048]{1,0:T(8,128)(2,1)}, u32[]{:S(2)}) copy-start(bf16[128,2048]{1,0:T(8,128)(2,1)} %query_own.1) | copy-start | bytes 1572868
  33.8 14.7 %copy-start.7 = (f32[4,2048]{1,0:T(4,128)S(1)}, f32[4,2048]{1,0:T(4,128)}, u32[]{:S(2)}) copy-start(f32[4,2048]{1,0:T(4,128)} %query_taps.1) | copy-start | bytes 98308
  33.8 9.2 %collective-permute-start.5 = (bf16[1040,128]{1,0:T(8,128)(2,1)S(1)}, bf16[1040,128]{1,0:T(8,128)(2,1)S(1)}, u32[]{:S(2)}, u32[]{:S(2)}) collective-permute-start(bf16[1040,128]{1,0:T(8,128)(2,1)S(1)} %get-tuple-element.17), channel_id=1, source_target_pairs={{0,2},{1,3},{4,6},{5,7},{8,10},{9,11},{12,14},{13,15},{16,18},{17,... | collective-permute-start | bytes 798728 | tf_op jit(solution)/shard_map/ppermute | solution.py:624
  35.2 24.8 %collective-permute-start.10 = (bf16[128,2048]{1,0:T(8,128)(2,1)S(1)}, bf16[128,2048]{1,0:T(8,128)(2,1)S(1)}, u32[]{:S(2)}, u32[]{:S(2)}) collective-permute-start(bf16[128,2048]{1,0:T(8,128)(2,1)S(1)} %copy-done.3), channel_id=1, source_target_pairs={{0,1},{1,0},{2,3},{3,2},{4,5},{5,4},{6,7},{7,6},{8,9},{9,8},{10,11... | collective-permute-start | bytes 1572872 | tf_op jit(solution)/shard_map/ppermute | solution.py:542
  35.3 13.1 %copy-start.9 = (bf16[8,2,2,128,128]{4,3,2,1,0:T(8,128)(2,1)S(1)}, bf16[8,2,2,128,128]{4,3,2,1,0:T(8,128)(2,1)}, u32[]{:S(2)}) copy-start(bf16[8,2,2,128,128]{4,3,2,1,0:T(8,128)(2,1)} %copy-done.8) | copy-start | bytes 3145732
  35.3 13.1 %copy-start.11 = (f32[8,128,128]{2,1,0:T(8,128)S(1)}, f32[8,128,128]{2,1,0:T(8,128)}, u32[]{:S(2)}) copy-start(f32[8,128,128]{2,1,0:T(8,128)} %copy-done.10) | copy-start | bytes 1572868
  35.6 23.4 %collective-permute-start.8 = (bf16[1040,128]{1,0:T(8,128)(2,1)S(1)}, bf16[1040,128]{1,0:T(8,128)(2,1)S(1)}, u32[]{:S(2)}, u32[]{:S(2)}) collective-permute-start(bf16[1040,128]{1,0:T(8,128)(2,1)S(1)} %code.1), channel_id=1, source_target_pairs={{4,6},{5,7},{12,14},{13,15},{20,22},{21,23},{28,30},{29,31}} | collective-permute-start | bytes 798728 | tf_op jit(solution)/shard_map/ppermute | solution.py:624
  43.6 16.4 %collective-permute-start.6 = (bf16[1040,128]{1,0:T(8,128)(2,1)S(1)}, bf16[1040,128]{1,0:T(8,128)(2,1)S(1)}, u32[]{:S(2)}, u32[]{:S(2)}) collective-permute-start(bf16[1040,128]{1,0:T(8,128)(2,1)S(1)} %join.1), channel_id=1, source_target_pairs={{2,4},{3,5},{10,12},{11,13},{18,20},{19,21},{26,28},{27,29}} | collective-permute-start | bytes 798728 | tf_op jit(solution)/shard_map/ppermute | solution.py:624
  45.4 14.6 %collective-permute-start.7 = (bf16[1040,128]{1,0:T(8,128)(2,1)S(1)}, bf16[1040,128]{1,0:T(8,128)(2,1)S(1)}, u32[]{:S(2)}, u32[]{:S(2)}) collective-permute-start(bf16[1040,128]{1,0:T(8,128)(2,1)S(1)} %join.1), channel_id=1, source_target_pairs={{2,6},{3,7},{10,14},{11,15},{18,22},{19,23},{26,30},{27,31}} | collective-permute-start | bytes 798728 | tf_op jit(solution)/shard_map/ppermute | solution.py:624
  48.5 1.0 %copy-start.13 = (f32[8,128,128]{2,1,0:T(8,128)S(1)}, f32[8,128,128]{2,1,0:T(8,128)}, u32[]{:S(2)}) copy-start(f32[8,128,128]{2,1,0:T(8,128)} %copy-done.12) | copy-start | bytes 1572868
  59.0 1.1 %copy-start.4 = (f32[128]{0:T(128)S(1)}, f32[128]{0:T(128)}, u32[]{:S(2)}) copy-start(f32[128]{0:T(128)} %param.21) | copy-start | bytes 1540
  61.0 1.6 %collective-permute-start.11 = (bf16[128,1024]{1,0:T(8,128)(2,1)S(1)}, bf16[128,1024]{1,0:T(8,128)(2,1)S(1)}, u32[]{:S(2)}, u32[]{:S(2)}) collective-permute-start(bf16[128,1024]{1,0:T(8,128)(2,1)S(1)} %constant_dynamic-slice_fusion), channel_id=1, source_target_pairs={{0,1},{1,0},{2,3},{3,2},{4,5},{5,4},{6,7},{7,6},{8,9},{9,8},{10,11... | collective-permute-start | bytes 786440 | tf_op jit(solution)/shard_map/ppermute | solution.py:728
  (2 other events, 1.5 us)
where the time goes:
time: 64 us; the launch traced here: 63.5 us
  Pallas kernels  30.2 us (47%)
  starting transfers between devices  14.8 us (23%)
  waiting for transfers between devices  10.1 us (16%)
  local copies, waits for them, and re-layouts  7.23 us (11%)
  other arithmetic  0.9 us (1%)
    pallas_call x1, Pallas kernels, per_device(): pl.pallas_call(functools.partial(states_kernel, heads), grid=(steps,), in...  15.5 us
    pallas_call x1, Pallas kernels, per_device(): pl.pallas_call(functools.partial(queries_kernel, heads, near), grid=(step...  9.43 us
    unnamed x28, local copies, waits for them, and re-layouts  7.21 us
    ppermute x4, starting transfers between devices, fan(): results.append(lax.ppermute(value, 'seq', route))  7.06 us
    ppermute x4, waiting for transfers between devices, fan(): results.append(lax.ppermute(value, 'seq', route))  6.6 us
    ppermute x1, starting transfers between devices, per_device(): lax.ppermute(halo, 'seq', [(i, i + 2) for i in range(1, size - 1, 2)])  3.2 us
    ppermute x1, starting transfers between devices, per_device(): lax.ppermute(halo, 'seq', [(i, i + 1) for i in range(1, size - 1, 2)])  3.1 us
    ppermute x1, waiting for transfers between devices, per_device(): lax.ppermute(halo, 'seq', [(i, i + 2) for i in range(1, size - 1, 2)])  1.92 us
  transfers between devices with their start and end apart: 12, of which 3 were waited for; matrix products, arithmetic and copies ran while one was open for 1% of the time, Pallas kernels for 45%

commit v1 on v0

v1 whole, which is shorter than its diff:
```python
import functools

import jax
import jax.numpy as jnp
from jax import lax
from jax.experimental import pallas as pl
from jax.experimental.pallas import tpu as pltpu
from jax.sharding import PartitionSpec as P

HEAD_DIM = 128
CHUNK = 128
CODE = 125.0
F32 = jnp.float32
BF16 = jnp.bfloat16


def split(x):
    high = x.astype(BF16)
    return high, (x - high.astype(F32)).astype(BF16)


def dot(a, b):
    return jnp.dot(a, b, preferred_element_type=F32)


def wide(b):
    row = jnp.concatenate(b, axis=1)
    return jnp.concatenate([row, row], axis=0)


def mm(a, b):
    width = b[0].shape[1]
    if width > 128:
        both = jnp.concatenate([b[0], b[0]], axis=0)
        return dot(jnp.concatenate(a, axis=1), both) + dot(a[0], b[1])
    out = dot(jnp.concatenate(a, axis=1), wide(b))
    return out[:, :width] + out[:, width:]


def silu(u):
    return u / (1.0 + jnp.exp(-u))


def encode(state):
    top = jnp.max(jnp.abs(state), axis=0, keepdims=True)
    scale = (top * 1.02 + 1e-30).astype(BF16).astype(F32)
    grade = jnp.abs(state) / scale
    level = jnp.exp2(grade * (2.0 * CODE) - CODE)
    return jnp.where(state < 0, -level, level).astype(BF16), scale


def decode(code, scale):
    grade = jnp.log2(jnp.abs(code)) * (0.5 / CODE) + 0.5
    size = grade * scale
    return jnp.where(code < 0, -size, size)


def iotas(rows, columns):
    return (
        lax.broadcasted_iota(jnp.int32, (rows, columns), 0),
        lax.broadcasted_iota(jnp.int32, (rows, columns), 1),
    )


def place():
    index = lax.axis_index("seq")
    return index % 2, index // 2


def fill(scratch, own, other, halo, core, group, first):
    lanes = scratch.shape[1]
    start = pl.multiple_of(core * 8 * HEAD_DIM + group * lanes, lanes)
    rows = halo[0][:, pl.ds(start, lanes)].astype(F32) + halo[1][:, pl.ds(start, lanes)].astype(F32)
    scratch[5:8, :] = rows[first : first + 3]
    place_own = pl.multiple_of(8 + CHUNK * core, 8)
    scratch[pl.ds(place_own, CHUNK), :] = own[:, group * lanes : (group + 1) * lanes].astype(F32)
    place_other = pl.multiple_of(8 + CHUNK * (1 - core), 8)
    scratch[pl.ds(place_other, CHUNK), :] = other[:, pl.ds(start, lanes)].astype(F32)


def conv(scratch, taps, chunk, columns, taps_columns):
    total = None
    for tap in range(4):
        part = taps[tap : tap + 1, taps_columns] * scratch[
            5 + tap + CHUNK * chunk : 5 + tap + CHUNK * chunk + CHUNK, columns
        ]
        total = part if total is None else total + part
    return silu(total)


def unit(rows):
    return rows * lax.rsqrt(jnp.sum(rows * rows, axis=-1, keepdims=True) + 1e-6)


def token_row(own, other, row, core, chunk):
    return jnp.where(core == chunk, own[pl.ds(row, 1), :], other[pl.ds(row, 1), :])


def rows_table(rows):
    pad = -len(rows) % 8
    if pad:
        rows = rows + [jnp.zeros((pad, CHUNK), F32)]
    return jnp.concatenate(rows, axis=0)


def sums(own, other, base, parts, core):
    rows = [token_row(own, other, base + head, core, chunk) for head, chunk in parts]
    t, j = iotas(CHUNK, CHUNK)
    upper = (t <= j).astype(F32)
    run = jnp.dot(
        rows_table(rows), upper, preferred_element_type=F32, precision=lax.Precision.HIGHEST
    )
    return [run[i : i + 1] for i in range(len(parts))]


def invert(coupling, t, j):
    apart = t ^ j
    count = len(coupling)
    near = [split(jnp.where(apart < 8, -a, 0.0)) for a in coupling]
    eye = (t == j).astype(F32)
    squared = [mm(n, n) for n in near]
    grown = []
    fourth = []
    for i in range(count):
        base = eye + near[i][0].astype(F32) + near[i][1].astype(F32)
        left = split(jnp.concatenate([squared[i], base], axis=0))
        both = mm(left, split(squared[i]))
        fourth.append(both[:CHUNK])
        grown.append(base + both[CHUNK:])
    inverse = [
        grown[i] + mm(split(grown[i]), split(fourth[i])) for i in range(count)
    ]
    inverse = [split(x) for x in inverse]
    size = 8
    while size < CHUNK:
        starts = range(size, CHUNK, 2 * size)

        def pick(x):
            return jnp.concatenate([x[s : s + size] for s in starts], axis=0)

        zero = jnp.zeros((size, CHUNK), BF16)

        def spread(x):
            pieces = []
            for k in range(len(starts)):
                pieces += [zero, x[k * size : (k + 1) * size]]
            return jnp.concatenate(pieces, axis=0)

        def merge(x, rows):
            pieces = []
            for k, s in enumerate(starts):
                pieces += [x[s - size : s], rows[k * size : (k + 1) * size]]
            return jnp.concatenate(pieces, axis=0)

        mask = pick((apart >= size) & (apart < 2 * size))
        middle = []
        for i in range(count):
            lower = split(jnp.where(mask, pick(coupling[i]), 0.0))
            middle.append(split(mm(lower, inverse[i])))
        for i in range(count):
            high, low = inverse[i]
            rows = (pick(high), pick(low))
            change = mm(rows, tuple(spread(m) for m in middle[i]))
            fresh = split(rows[0].astype(F32) + rows[1].astype(F32) - change)
            inverse[i] = (merge(high, fresh[0]), merge(low, fresh[1]))
        size *= 2
    return inverse


def decay(column, row, t, j):
    return jnp.exp(jnp.where(t >= j, column - row, -1e30))


def prepare_kernel(query, key, value, gate, log_alpha, strength, mixture, query_taps, key_taps,
                   value_taps, query_half, key_half, value_half, gate_half, query_taps_half,
                   key_taps_half, value_taps_half, halo, small, tails, sems):
    core, _ = place()
    rows, half = query_half.shape
    lanes = pl.ds(pl.multiple_of(core * half, half), half)
    copies = []

    def copy(source, target):
        made = pltpu.make_async_copy(source, target, sems.at[len(copies)])
        made.start()
        copies.append(made)

    for i, x in enumerate((query, key, value)):
        copy(x.at[rows - 16 : rows, :], tails.at[i])
    copy(log_alpha, small.at[0:16])
    copy(strength, small.at[16:32])
    copy(mixture, small.at[32 : small.shape[0]])
    for x, y in (
        (key, key_half),
        (value, value_half),
        (key_taps, key_taps_half),
        (value_taps, value_taps_half),
        (query_taps, query_taps_half),
        (query, query_half),
        (gate, gate_half),
    ):
        copy(x.at[:, lanes], y)
    for made in copies:
        made.wait()
    message = [tails[i][13:16, :].astype(F32) for i in range(3)]
    message.append(jnp.zeros((7, 2 * half), F32))
    halo[...] = jnp.concatenate(message, axis=0).astype(BF16)


def states_kernel(
    group,
    heads,
    key_own,
    key_other,
    value_own,
    value_other,
    key_taps,
    value_taps,
    halo_one,
    halo_two,
    small_own,
    small_other,
    key_cols_out,
    inverse_out,
    write_out,
    first_state_out,
    state_out,
    transit_one_out,
    transit_out,
    code_out,
    key_scratch,
    value_scratch,
):
    core, _ = place()
    fill(key_scratch, key_own, key_other, (halo_one, halo_two), core, group, 3)
    fill(value_scratch, value_own, value_other, (halo_one, halo_two), core, group, 6)
    t, j = iotas(CHUNK, CHUNK)
    parts = [(head, chunk) for head in range(heads) for chunk in range(2)]
    count = len(parts)
    base = 8 * core + heads * group
    run = sums(small_own, small_other, base, parts, core)
    strengths = [
        token_row(small_own, small_other, 16 + base + head, core, chunk) for head, chunk in parts
    ]
    columns = rows_table(run + strengths).T

    def lanes(head):
        return slice(head * 128, head * 128 + 128)

    def taps_lanes(head):
        return lanes(group * heads + head)

    def beta(i):
        return columns[:, count + i : count + i + 1]

    keys = [
        unit(conv(key_scratch, key_taps, chunk, lanes(head), taps_lanes(head)))
        for head, chunk in parts
    ]
    keys_t = [key.T for key in keys]
    coupling = []
    for i, (head, chunk) in enumerate(parts):
        pair = split(keys_t[i])
        key_cols_out[head, chunk, 0] = pair[0]
        key_cols_out[head, chunk, 1] = pair[1]
        gram = mm(split(keys[i]), pair)
        ratio = decay(columns[:, i : i + 1], run[i], t, j)
        coupling.append(jnp.where(t > j, gram * ratio * beta(i), 0.0))
    inverse = invert(coupling, t, j)
    mixed = []
    for i, (head, chunk) in enumerate(parts):
        inverse_out[head, chunk, 0] = inverse[i][0]
        inverse_out[head, chunk, 1] = inverse[i][1]
        last = run[i][:, CHUNK - 1 : CHUNK]
        tail = keys_t[i] * jnp.exp(last - run[i])
        mixed.append(mm(split(tail), inverse[i]))
    transits = []
    states = []
    for i, (head, chunk) in enumerate(parts):
        value = conv(value_scratch, value_taps, chunk, lanes(head), taps_lanes(head))
        grow = jnp.exp(columns[:, i : i + 1])
        write = jnp.concatenate([keys[i] * (beta(i) * grow), value * beta(i)], axis=1)
        write = split(write)
        write_out[head, chunk, 0] = write[0]
        write_out[head, chunk, 1] = write[1]
        last = run[i][:, CHUNK - 1 : CHUNK]
        both = mm(split(mixed[i]), write)
        transits.append(jnp.where(t == j, jnp.exp(last), 0.0) - both[:, :128])
        states.append(both[:, 128:])
    scales = []
    for head in range(heads):
        low, high = 2 * head, 2 * head + 1
        pair = split(transits[high])
        state = mm(pair, split(states[low])) + states[high]
        first_state_out[head] = states[low]
        transit_one_out[head] = transits[low]
        state_out[head] = state
        transit_out[head] = mm(pair, split(transits[low]))
        code, scale = encode(state)
        code_out[head * 128 : head * 128 + 128, :] = code
        scales.append(scale)
    code_out[heads * 128 : heads * 128 + 16, :] = pack_rows(scales)


def queries_kernel(
    group,
    heads,
    first,
    count,
    near,
    query_own,
    query_other,
    query_taps,
    halo_one,
    halo_two,
    small_own,
    small_other,
    key_cols,
    inverse,
    write,
    first_state,
    transit_one,
    out,
    moved,
    query_scratch,
):
    core, _ = place()
    piece = (group * heads + first) // count
    fill(query_scratch, query_own, query_other, (halo_one, halo_two), core, piece, 0)
    t, j = iotas(CHUNK, CHUNK)
    apart = t ^ j
    parts = [(head, chunk) for head in range(count) for chunk in range(2)]
    base = 8 * core + heads * group + first
    run = sums(small_own, small_other, base, parts, core)
    rows = list(run)
    for head, chunk in parts:
        for level in range(near + 1):
            row = 32 + 16 * level + base + head
            rows.append(token_row(small_own, small_other, row, core, chunk))
    columns = rows_table(rows).T
    mixings = []
    queries = []
    for i, (head, chunk) in enumerate(parts):
        lanes = slice(head * 128, head * 128 + 128)
        full = group * heads + first + head
        taps_lanes = slice(full * 128, full * 128 + 128)
        query = unit(conv(query_scratch, query_taps, chunk, lanes, taps_lanes))
        queries.append(query)
        at = first + head
        ratio = decay(columns[:, i : i + 1], run[i], t, j)
        scores = mm(split(query), (key_cols[at, chunk, 0], key_cols[at, chunk, 1])) * ratio
        mixings.append(mm(split(scores), (inverse[at, chunk, 0], inverse[at, chunk, 1])))
    for i, (head, chunk) in enumerate(parts):
        at = len(parts) + i * (near + 1)
        level_mat = columns[:, at : at + 1]
        for level in range(1, near):
            weight = columns[:, at + level : at + level + 1]
            level_mat = jnp.where(apart >= 1 << (level - 1), weight, level_mat)
        high, low = (write[first + head, chunk, 0], write[first + head, chunk, 1])
        within = mm(split(mixings[i] * level_mat), (high[:, 128:], low[:, 128:]))
        grow = jnp.exp(columns[:, i : i + 1])
        effective = grow * queries[i] - mm(split(mixings[i]), (high[:, :128], low[:, :128]))
        rows = slice(chunk * CHUNK, chunk * CHUNK + CHUNK)
        if chunk:
            pair = split(effective)
            weight = columns[:, at + near : at + near + 1]
            within = within + weight * mm(pair, split(first_state[first + head]))
            effective = mm(pair, split(transit_one[first + head]))
        out[head, rows, :] = within
        moved[head, rows, :] = effective


def received(refs, head):
    code = None
    scale = None
    for ref in refs:
        tail = ref.shape[0] - 16 + head
        part = ref[head * 128 : head * 128 + 128, :].astype(F32)
        row = ref[tail : tail + 1, :].astype(F32)
        code = part if code is None else code + part
        scale = row if scale is None else scale + row
    return decode(code, scale)


def pack_rows(scales):
    zeros = jnp.zeros((16 - len(scales), 128), F32)
    return jnp.concatenate(scales + [zeros], axis=0).astype(BF16)


def encode_all(values, code_out):
    scales = []
    for head, value in enumerate(values):
        code, scale = encode(value)
        code_out[head * 128 : head * 128 + 128, :] = code
        scales.append(scale)
    head = len(values)
    code_out[head * 128 : head * 128 + 16, :] = pack_rows(scales)


def join_kernel(level, arrivals, with_transit, *refs):
    state_in = refs[:arrivals]
    refs = refs[arrivals:]
    transit_in = ()
    if with_transit:
        transit_in = refs[:arrivals]
        refs = refs[arrivals:]
    state, transit, code_out = refs[:3]
    refs = refs[3:]
    heads = state.shape[0]
    _, node = place()
    upper = (node >> level) % 2 == 1

    @pl.when(upper)
    def _():
        fresh = []
        for head in range(heads):
            pair = split(transit[head])
            fresh.append(mm(pair, split(received(state_in, head))) + state[head])
            if with_transit:
                refs[0][head] = fresh[head]
                refs[1][head] = mm(pair, split(received(transit_in, head)))
        encode_all(fresh, code_out)
        if with_transit:
            encode_all([refs[1][head] for head in range(heads)], refs[2])

    @pl.when(jnp.logical_not(upper))
    def _():
        encode_all([state[head] for head in range(heads)], code_out)
        if with_transit:
            for head in range(heads):
                refs[0][head] = state[head]
                refs[1][head] = transit[head]
            encode_all([transit[head] for head in range(heads)], refs[2])


def code_kernel(value, code_out):
    encode_all([value[head] for head in range(value.shape[0])], code_out)


def level_weight(own, other, row, core):
    rows = [token_row(own, other, row, core, chunk) for chunk in range(2)]
    columns = rows_table(rows).T
    return jnp.concatenate([columns[:, 0:1], columns[:, 1:2]], axis=0)


def absorb_kernel(level, weight_row, group, heads, arrivals, pieces, *refs):
    state_in = refs[:arrivals]
    transit_in = refs[arrivals : 2 * arrivals]
    refs = refs[2 * arrivals :]
    small_own, small_other = refs[:2]
    outs_in = refs[2 : 2 + pieces]
    moved_in = refs[2 + pieces : 2 + 2 * pieces]
    out, moved = refs[2 + 2 * pieces :]
    core, node = place()
    upper = (node >> level) % 2 == 1
    later = (node >> (level + 1)) > 0
    each = heads // pieces

    @pl.when(upper)
    def _():
        for head in range(heads):
            pair = split(moved_in[head // each][head % each])
            row = weight_row + 8 * core + heads * group + head
            weight = level_weight(small_own, small_other, row, core)
            gain = mm(pair, split(received(state_in, head)))
            out[head] = outs_in[head // each][head % each] + weight * gain

    @pl.when(jnp.logical_not(upper))
    def _():
        for head in range(heads):
            out[head] = outs_in[head // each][head % each]

    @pl.when(upper & later)
    def _():
        for head in range(heads):
            pair = split(moved_in[head // each][head % each])
            moved[head] = mm(pair, split(received(transit_in, head)))

    @pl.when(jnp.logical_not(upper & later))
    def _():
        for head in range(heads):
            moved[head] = moved_in[head // each][head % each]


def finish_kernel(level, weight_row, group, heads, arrivals, pieces, *refs):
    state_in = refs[:arrivals]
    refs = refs[arrivals:]
    small_own, small_other, gate_own, gate_other, gain = refs[:5]
    outs_in = refs[5 : 5 + pieces]
    moved_in = refs[5 + pieces : 5 + 2 * pieces]
    stay, leave, total = refs[5 + 2 * pieces :]
    core, node = place()
    upper = (node >> level) % 2 == 1
    each = heads // pieces

    @pl.when(upper)
    def _():
        for head in range(heads):
            row = weight_row + 8 * core + heads * group + head
            weight = level_weight(small_own, small_other, row, core)
            extra = mm(split(moved_in[head // each][head % each]), split(received(state_in, head)))
            total[head] = outs_in[head // each][head % each] + weight * extra

    @pl.when(jnp.logical_not(upper))
    def _():
        for head in range(heads):
            total[head] = outs_in[head // each][head % each]

    lanes_all = heads * 128
    start = pl.multiple_of(core * 8 * HEAD_DIM + group * lanes_all, lanes_all)
    gates = (
        gate_own[:, group * lanes_all : (group + 1) * lanes_all],
        gate_other[:, pl.ds(start, lanes_all)],
    )
    for head in range(heads):
        lanes = slice(head * 128, head * 128 + 128)
        for gate, chunk, target in ((gates[0], core, stay), (gates[1], 1 - core, leave)):
            rows = pl.ds(pl.multiple_of(chunk * CHUNK, CHUNK), CHUNK)
            attended = total[head, rows, :]
            scale = lax.rsqrt(jnp.mean(attended * attended, axis=-1, keepdims=True) + 1e-5)
            gated = attended * scale * gain[...] * silu(gate[:, lanes].astype(F32))
            target[:, lanes] = gated.astype(BF16)


def swap_kernel(*refs):
    out = refs[-1]
    count = (len(refs) - 1) // 2
    core, _ = place()
    half = out.shape[1] // 2
    width = half // count
    for i in range(count):
        start = pl.multiple_of(core * half + i * width, width)
        out[:, pl.ds(start, width)] = refs[i][...]
        start = pl.multiple_of((1 - core) * half + i * width, width)
        out[:, pl.ds(start, width)] = refs[count + i][...]


def struct(shape, dtype=F32):
    return jax.ShapeDtypeStruct(shape, dtype)


def params(mib):
    return pltpu.CompilerParams(vmem_limit_bytes=mib << 20)


def cost(flops):
    return pl.CostEstimate(flops=flops, bytes_accessed=1_000_000, transcendentals=0)


GROUPS = 2
PIECES = 2


def per_device(
    query_rows,
    key_rows,
    value_rows,
    query_taps,
    key_taps,
    value_taps,
    log_alpha,
    write_strength,
    tier_mixture,
    output_gate,
    norm_gain,
):
    rows, width = query_rows.shape
    half = width // 2
    size = lax.axis_size("seq")
    nodes = size // 2
    level_total = tier_mixture.shape[0]
    near = CHUNK.bit_length()
    heads = 8 // GROUPS
    lanes = heads * 128
    shard_bits = nodes.bit_length() - 1
    cores = [(i, i ^ 1) for i in range(size)]
    small_rows = 16 * (2 + level_total)
    key_other = lax.ppermute(key_rows, "seq", cores)
    value_other = lax.ppermute(value_rows, "seq", cores)
    half_shape = struct((rows, half), BF16)
    taps_shape = struct((4, half))
    (
        query_half,
        key_half,
        value_half,
        gate_half,
        query_taps_half,
        key_taps_half,
        value_taps_half,
        halo,
        small,
    ) = pl.pallas_call(
        prepare_kernel,
        in_specs=[pl.BlockSpec(memory_space=pltpu.HBM)] * 10,
        out_shape=[half_shape] * 4
        + [taps_shape] * 3
        + [struct((16, width), BF16), struct((small_rows, 128))],
        scratch_shapes=[pltpu.VMEM((3, 16, width), BF16), pltpu.SemaphoreType.DMA((13,))],
        compiler_params=params(8),
        name="prepare",
    )(
        *[
            pltpu.with_memory_space_constraint(x, pltpu.HBM)
            for x in (
                query_rows,
                key_rows,
                value_rows,
                output_gate,
                log_alpha,
                write_strength,
                tier_mixture.reshape(level_total * 16, rows),
                query_taps,
                key_taps,
                value_taps,
            )
        ]
    )
    halo_one = lax.ppermute(halo, "seq", [(i, i + 1) for i in range(1, size - 1, 2)])
    halo_two = lax.ppermute(halo, "seq", [(i, i + 2) for i in range(1, size - 1, 2)])
    small_other = lax.ppermute(small, "seq", cores)
    query_other = lax.ppermute(query_rows, "seq", cores)
    gate_other = lax.ppermute(output_gate, "seq", cores)

    def fan(value, level, keep):
        span = 1 << level
        results = []
        for offset in reversed(range(span)):
            route = []
            for low in range(0, nodes, 2 * span):
                source, target = low + span - 1, low + span + offset
                if keep(target):
                    route += [(2 * source + c, 2 * target + c) for c in range(2)]
            results.append(lax.ppermute(value, "seq", route))
        return results

    square = (heads, 128, 128)
    pair = struct((heads, 2, 2, 128, 128), BF16)
    code_shape = struct((heads * 128 + 16, 128), BF16)
    local = []
    arrived = []
    for group in range(GROUPS):
        local.append(
            pl.pallas_call(
                functools.partial(states_kernel, group, heads),
                out_shape=[
                    pair,
                    pair,
                    struct((heads, 2, 2, 128, 256), BF16),
                    struct(square),
                    struct(square),
                    struct(square),
                    struct(square),
                    code_shape,
                ],
                scratch_shapes=[pltpu.VMEM((8 + 2 * CHUNK, lanes), F32)] * 2,
                compiler_params=params(24),
                cost_estimate=cost(4_000_000_000),
                name="states",
            )(
                key_half,
                key_other,
                value_half,
                value_other,
                key_taps_half,
                value_taps_half,
                halo_one,
                halo_two,
                small,
                small_other,
            )
        )
        arrived.append(fan(local[group][7], 0, lambda target: True) if shard_bits else [])
    state = [x[4] for x in local]
    transit = [x[6] for x in local]
    transit_code = [None] * GROUPS
    outs = [None] * GROUPS
    moved = [None] * GROUPS

    def ask(group):
        key_cols, inverse, write, first_state, _, transit_one, _, _ = local[group]
        outs[group] = []
        moved[group] = []
        count = heads // PIECES
        shape = struct((count, 2 * CHUNK, 128))
        for piece in range(PIECES):
            first = piece * count
            out, move = pl.pallas_call(
                functools.partial(queries_kernel, group, heads, first, count, near),
                out_shape=[shape, shape],
                scratch_shapes=[pltpu.VMEM((8 + 2 * CHUNK, count * 128), F32)],
                compiler_params=params(16),
                cost_estimate=cost(1_500_000_000),
                name="queries",
            )(
                query_half,
                query_other,
                query_taps_half,
                halo_one,
                halo_two,
                small,
                small_other,
                key_cols,
                inverse,
                write,
                first_state,
                transit_one,
            )
            outs[group].append(out)
            moved[group].append(move)

    def encoded(value):
        return pl.pallas_call(
            code_kernel,
            out_shape=code_shape,
            compiler_params=params(8),
            name="code",
        )(value)

    moved_shape = struct((heads, 2 * CHUNK, 128))
    if shard_bits > 1:
        transit_code = [encoded(x) for x in transit]
    if shard_bits < 2:
        for group in range(GROUPS):
            ask(group)
    for level in range(shard_bits - 1):
        keeps = level < shard_bits - 2
        following = []
        for group in range(GROUPS):
            transit_arrived = fan(
                transit_code[group], level, lambda target: keeps or target >> (level + 1) > 0
            )
            shapes = [code_shape]
            operands = list(arrived[group])
            if keeps:
                shapes += [struct(square), struct(square), code_shape]
                operands += transit_arrived
            joined = pl.pallas_call(
                functools.partial(join_kernel, level, len(arrived[group]), keeps),
                out_shape=shapes,
                compiler_params=params(12),
                cost_estimate=cost(300_000_000),
                name="join",
            )(*operands, state[group], transit[group])
            following.append(fan(joined[0], level + 1, lambda target: True))
            if keeps:
                state[group], transit[group], transit_code[group] = joined[1:]
            if level == 0:
                ask(group)
            arrivals = len(arrived[group])
            out, move = pl.pallas_call(
                functools.partial(
                    absorb_kernel,
                    level,
                    32 + 16 * (near + 1 + level),
                    group,
                    heads,
                    arrivals,
                    len(outs[group]),
                ),
                out_shape=[moved_shape, moved_shape],
                compiler_params=params(12),
                cost_estimate=cost(800_000_000),
                name="absorb",
            )(
                *arrived[group],
                *transit_arrived,
                small,
                small_other,
                *outs[group],
                *moved[group],
            )
            outs[group], moved[group] = [out], [move]
        arrived = following

    level = max(shard_bits - 1, 0)
    gain = norm_gain.reshape(1, 128)
    stays = []
    comes = []
    for group in range(GROUPS):
        stay, leave = pl.pallas_call(
            functools.partial(
                finish_kernel,
                level,
                32 + 16 * (near + 1 + level),
                group,
                heads,
                len(arrived[group]),
                len(outs[group]),
            ),
            out_shape=[struct((rows, lanes), BF16)] * 2,
            scratch_shapes=[pltpu.VMEM((heads, 2 * CHUNK, 128), F32)],
            compiler_params=params(12),
            cost_estimate=cost(600_000_000),
            name="finish",
        )(
            *arrived[group],
            small,
            small_other,
            gate_half,
            gate_other,
            gain,
            *outs[group],
            *moved[group],
        )
        stays.append(stay)
        comes.append(lax.ppermute(leave, "seq", cores))
    return pl.pallas_call(
        swap_kernel,
        out_shape=struct((rows, width), BF16),
        compiler_params=params(4),
        name="swap",
    )(*stays, *comes)


def solution(mesh):
    placed = (
        P(("req", "seq"), None),
        P(("req", "seq"), None),
        P(("req", "seq"), None),
        P(),
        P(),
        P(),
        P(None, ("req", "seq")),
        P(None, ("req", "seq")),
        P(None, None, ("req", "seq")),
        P(("req", "seq"), None),
        P(),
    )
    return jax.shard_map(
        per_device, mesh=mesh, in_specs=placed, out_specs=P(("req", "seq"), None), check_vma=False
    )
```

time: 64 us -> 52 us (0.81)
  the two profiles are of different devices: /device:TPU:11 before, /device:TPU:17 now
where the time goes in v1:
time: 52 us; the launch traced here: 51.7 us
  starting transfers between devices  20.4 us (39%)
  Pallas kernels  20.4 us (39%)
  waiting for transfers between devices  9.97 us (19%)
  local copies, waits for them, and re-layouts  0.66 us (1%)
    ppermute x8, starting transfers between devices, fan(): results.append(lax.ppermute(value, 'seq', route))  9.92 us
    pallas_call x2, Pallas kernels, per_device(): pl.pallas_call(functools.partial(states_kernel, group, heads), out_shape=...  9.53 us
    ppermute x8, waiting for transfers between devices, fan(): results.append(lax.ppermute(value, 'seq', route))  6.45 us
    pallas_call x4, Pallas kernels, ask(): pl.pallas_call(functools.partial(queries_kernel, group, heads, first, cou...  6.05 us
    ppermute x2, starting transfers between devices, per_device(): comes.append(lax.ppermute(leave, 'seq', cores))  3.72 us
    ppermute x1, starting transfers between devices, per_device(): lax.ppermute(halo, 'seq', [(i, i + 1) for i in range(1, size - 1, 2)])  3.1 us
    ppermute x1, waiting for transfers between devices, per_device(): lax.ppermute(halo, 'seq', [(i, i + 2) for i in range(1, size - 1, 2)])  2.52 us
    ppermute x1, starting transfers between devices, per_device(): lax.ppermute(halo, 'seq', [(i, i + 2) for i in range(1, size - 1, 2)])  1.92 us
  transfers between devices with their start and end apart: 17, of which 4 were waited for; matrix products, arithmetic and copies ran while one was open for 0% of the time, Pallas kernels for 38%

profile of v1, /device:TPU:17, one launch (start us, length us, event | category | flops | bytes accessed | tf_op | source)
XLA Modules:
  0.0 51.7 jit_solution(1261351124530022141)
XLA Ops:
  0.7 1.6 %prepare.1 = (bf16[128,1024]{1,0:T(8,128)(2,1)S(1)}, bf16[128,1024]{1,0:T(8,128)(2,1)S(1)}, bf16[128,1024]{1,0:T(8,128)(2,1)S(1)}, bf16[128,1024]{1,0:T(8,128)(2...) custom-call(bf16[128,2048]{1,0:T(8,128)(2,1)} %query.1, ...), custom_call_target="tpu_custom_call" | custom-call | tf_op jit(solution)/shard_map/prepare/pallas_call | solution.py:591
  2.9 3.1 %collective-permute-start.2 = (bf16[16,2048]{1,0:T(8,128)(2,1)S(1)}, bf16[16,2048]{1,0:T(8,128)(2,1)S(1)}, u32[]{:S(2)}, u32[]{:S(2)}) collective-permute-start(bf16[16,2048]{1,0:T(8,128)(2,1)S(1)} %get-tuple-element.50), channel_id=1, source_target_pairs={{1,2},{3,4},{5,6},{9,10},{11,12},{13,14},{17,18},{19,20},{21,22},{... | collective-permute-start | bytes 196616 | tf_op jit(solution)/shard_map/ppermute | solution.py:617
  6.0 1.9 %collective-permute-start.3 = (bf16[16,2048]{1,0:T(8,128)(2,1)S(1)}, bf16[16,2048]{1,0:T(8,128)(2,1)S(1)}, u32[]{:S(2)}, u32[]{:S(2)}) collective-permute-start(bf16[16,2048]{1,0:T(8,128)(2,1)S(1)} %get-tuple-element.50), channel_id=1, source_target_pairs={{1,3},{3,5},{5,7},{9,11},{11,13},{13,15},{17,19},{19,21},{21,23},{... | collective-permute-start | bytes 196616 | tf_op jit(solution)/shard_map/ppermute | solution.py:618
  8.5 2.5 %collective-permute-done.3.halo_two = bf16[16,2048]{1,0:T(8,128)(2,1)S(1)} collective-permute-done((bf16[16,2048]{1,0:T(8,128)(2,1)S(1)}, bf16[16,2048]{1,0:T(8,128)(2,1)S(1)}, u32[]{:S(2)}, u32[]{:S(2)}) %collective-permute-start.3) | collective-permute-done | bytes 65568 | tf_op jit(solution)/shard_map/ppermute | solution.py:618
  11.0 4.8 %states.3 = (bf16[4,2,2,128,128]{4,3,2,1,0:T(8,128)(2,1)S(1)}, bf16[4,2,2,128,128]{4,3,2,1,0:T(8,128)(2,1)S(1)}, bf16[4,2,2,128,256]{4,3,2,1,0:T(8,128)(2,1)S(1)...) custom-call(bf16[128,1024]{1,0:T(8,128)(2,1)S(1)} %get-tuple-element, ...), custom_call_target="tpu_custom_call" | custom-call | flops 4000000000 | bytes 1000000 | tf_op jit(solution)/shard_map/states/pallas_call | solution.py:642
  15.9 1.9 %collective-permute-start.14 = (bf16[528,128]{1,0:T(8,128)(2,1)S(1)}, bf16[528,128]{1,0:T(8,128)(2,1)S(1)}, u32[]{:S(2)}, u32[]{:S(2)}) collective-permute-start(bf16[528,128]{1,0:T(8,128)(2,1)S(1)} %code.3), channel_id=1, source_target_pairs={{4,6},{5,7},{12,14},{13,15},{20,22},{21,23},{28,30},{29,31}} | collective-permute-start | bytes 405512 | tf_op jit(solution)/shard_map/ppermute | solution.py:632
  17.8 1.3 %collective-permute-start.11 = (bf16[528,128]{1,0:T(8,128)(2,1)S(1)}, bf16[528,128]{1,0:T(8,128)(2,1)S(1)}, u32[]{:S(2)}, u32[]{:S(2)}) collective-permute-start(bf16[528,128]{1,0:T(8,128)(2,1)S(1)} %get-tuple-element.70), channel_id=1, source_target_pairs={{0,2},{1,3},{4,6},{5,7},{8,10},{9,11},{12,14},{13,15},{16,18},{17,... | collective-permute-start | bytes 405512 | tf_op jit(solution)/shard_map/ppermute | solution.py:632
  19.1 4.8 %states.2 = (bf16[4,2,2,128,128]{4,3,2,1,0:T(8,128)(2,1)S(1)}, bf16[4,2,2,128,128]{4,3,2,1,0:T(8,128)(2,1)S(1)}, bf16[4,2,2,128,256]{4,3,2,1,0:T(8,128)(2,1)S(1)...) custom-call(bf16[128,1024]{1,0:T(8,128)(2,1)S(1)} %get-tuple-element, ...), custom_call_target="tpu_custom_call" | custom-call | flops 4000000000 | bytes 1000000 | tf_op jit(solution)/shard_map/states/pallas_call | solution.py:642
  24.0 1.3 %collective-permute-start.9 = (bf16[528,128]{1,0:T(8,128)(2,1)S(1)}, bf16[528,128]{1,0:T(8,128)(2,1)S(1)}, u32[]{:S(2)}, u32[]{:S(2)}) collective-permute-start(bf16[528,128]{1,0:T(8,128)(2,1)S(1)} %code.2), channel_id=1, source_target_pairs={{4,6},{5,7},{12,14},{13,15},{20,22},{21,23},{28,30},{29,31}} | collective-permute-start | bytes 405512 | tf_op jit(solution)/shard_map/ppermute | solution.py:632
  25.3 1.5 %collective-permute-start.5 = (bf16[528,128]{1,0:T(8,128)(2,1)S(1)}, bf16[528,128]{1,0:T(8,128)(2,1)S(1)}, u32[]{:S(2)}, u32[]{:S(2)}) collective-permute-start(bf16[528,128]{1,0:T(8,128)(2,1)S(1)} %get-tuple-element.52), channel_id=1, source_target_pairs={{0,2},{1,3},{4,6},{5,7},{8,10},{9,11},{12,14},{13,15},{16,18},{17,... | collective-permute-start | bytes 405512 | tf_op jit(solution)/shard_map/ppermute | solution.py:632
  26.8 1.5 %queries.7 = (f32[2,256,128]{2,1,0:T(8,128)S(1)}, f32[2,256,128]{2,1,0:T(8,128)S(1)}) custom-call(bf16[128,1024]{1,0:T(8,128)(2,1)S(1)} %get-tuple-element.56.query_own, bf16[128,2048]{1,0:T(8,128)(2,1)S(1)} %collective-permute-done.10.query_other, f32[4,1024]{1,0:T(4,128)S(1)} %get-tuple-element.57.query_taps, ...), custom_call_target="tpu_custom_call" | custom-call | flops 1500000000 | bytes 1000000 | tf_op jit(solution)/shard_map/queries/pallas_call | solution.py:686
  28.3 1.5 %queries.6 = (f32[2,256,128]{2,1,0:T(8,128)S(1)}, f32[2,256,128]{2,1,0:T(8,128)S(1)}) custom-call(bf16[128,1024]{1,0:T(8,128)(2,1)S(1)} %get-tuple-element.56.query_own, bf16[128,2048]{1,0:T(8,128)(2,1)S(1)} %collective-permute-done.10.query_other, f32[4,1024]{1,0:T(4,128)S(1)} %get-tuple-element.57.query_taps, ...), custom_call_target="tpu_custom_call" | custom-call | flops 1500000000 | bytes 1000000 | tf_op jit(solution)/shard_map/queries/pallas_call | solution.py:686
  29.9 1.5 %queries.5 = (f32[2,256,128]{2,1,0:T(8,128)S(1)}, f32[2,256,128]{2,1,0:T(8,128)S(1)}) custom-call(bf16[128,1024]{1,0:T(8,128)(2,1)S(1)} %get-tuple-element.56.query_own, bf16[128,2048]{1,0:T(8,128)(2,1)S(1)} %collective-permute-done.10.query_other, f32[4,1024]{1,0:T(4,128)S(1)} %get-tuple-element.57.query_taps, ...), custom_call_target="tpu_custom_call" | custom-call | flops 1500000000 | bytes 1000000 | tf_op jit(solution)/shard_map/queries/pallas_call | solution.py:686
  31.4 1.5 %queries.4 = (f32[2,256,128]{2,1,0:T(8,128)S(1)}, f32[2,256,128]{2,1,0:T(8,128)S(1)}) custom-call(bf16[128,1024]{1,0:T(8,128)(2,1)S(1)} %get-tuple-element.56.query_own, bf16[128,2048]{1,0:T(8,128)(2,1)S(1)} %collective-permute-done.10.query_other, f32[4,1024]{1,0:T(4,128)S(1)} %get-tuple-element.57.query_taps, ...), custom_call_target="tpu_custom_call" | custom-call | flops 1500000000 | bytes 1000000 | tf_op jit(solution)/shard_map/queries/pallas_call | solution.py:686
  33.7 1.3 %collective-permute-start.13 = (bf16[528,128]{1,0:T(8,128)(2,1)S(1)}, bf16[528,128]{1,0:T(8,128)(2,1)S(1)}, u32[]{:S(2)}, u32[]{:S(2)}) collective-permute-start(bf16[528,128]{1,0:T(8,128)(2,1)S(1)} %join.3), channel_id=1, source_target_pairs={{2,4},{3,5},{10,12},{11,13},{18,20},{19,21},{26,28},{27,29}} | collective-permute-start | bytes 405512 | tf_op jit(solution)/shard_map/ppermute | solution.py:632
  35.9 1.3 %collective-permute-start.7 = (bf16[528,128]{1,0:T(8,128)(2,1)S(1)}, bf16[528,128]{1,0:T(8,128)(2,1)S(1)}, u32[]{:S(2)}, u32[]{:S(2)}) collective-permute-start(bf16[528,128]{1,0:T(8,128)(2,1)S(1)} %join.2), channel_id=1, source_target_pairs={{2,4},{3,5},{10,12},{11,13},{18,20},{19,21},{26,28},{27,29}} | collective-permute-start | bytes 405512 | tf_op jit(solution)/shard_map/ppermute | solution.py:632
  37.4 4.5 %collective-permute-done.13.refs_1_ = bf16[528,128]{1,0:T(8,128)(2,1)S(1)} collective-permute-done((bf16[528,128]{1,0:T(8,128)(2,1)S(1)}, bf16[528,128]{1,0:T(8,128)(2,1)S(1)}, u32[]{:S(2)}, u32[]{:S(2)}) %collective-permute-start.13) | collective-permute-done | bytes 135200 | tf_op jit(solution)/shard_map/ppermute | solution.py:632
  42.5 0.8 %finish.3 = (bf16[128,512]{1,0:T(8,128)(2,1)S(1)}, bf16[128,512]{1,0:T(8,128)(2,1)S(1)}) custom-call(bf16[528,128]{1,0:T(8,128)(2,1)S(1)} %collective-permute-done.12.refs_0_, bf16[528,128]{1,0:T(8,128)(2,1)S(1)} %collective-permute-done.13.refs_1_, f32[208,128]{1,0:T(8,128)S(1)} %get-tuple-element.51.small_own.refs_2_, ...), custom_call_target="tpu_custom_call" | custom-call | flops 600000000 | bytes 1000000 | tf_op jit(solution)/shard_map/finish/pallas_call | solution.py:779
  43.4 2.3 %collective-permute-start.16 = (bf16[128,512]{1,0:T(8,128)(2,1)S(1)}, bf16[128,512]{1,0:T(8,128)(2,1)S(1)}, u32[]{:S(2)}, u32[]{:S(2)}) collective-permute-start(bf16[128,512]{1,0:T(8,128)(2,1)S(1)} %get-tuple-element.86), channel_id=1, source_target_pairs={{0,1},{1,0},{2,3},{3,2},{4,5},{5,4},{6,7},{7,6},{8,9},{9,8},{10,11... | collective-permute-start | bytes 393224 | tf_op jit(solution)/shard_map/ppermute | solution.py:805
  45.7 2.0 %collective-permute-done.7.refs_1_ = bf16[528,128]{1,0:T(8,128)(2,1)S(1)} collective-permute-done((bf16[528,128]{1,0:T(8,128)(2,1)S(1)}, bf16[528,128]{1,0:T(8,128)(2,1)S(1)}, u32[]{:S(2)}, u32[]{:S(2)}) %collective-permute-start.7) | collective-permute-done | bytes 135200 | tf_op jit(solution)/shard_map/ppermute | solution.py:632
  47.7 0.8 %finish.2 = (bf16[128,512]{1,0:T(8,128)(2,1)S(1)}, bf16[128,512]{1,0:T(8,128)(2,1)S(1)}) custom-call(bf16[528,128]{1,0:T(8,128)(2,1)S(1)} %collective-permute-done.6.refs_0_, bf16[528,128]{1,0:T(8,128)(2,1)S(1)} %collective-permute-done.7.refs_1_, f32[208,128]{1,0:T(8,128)S(1)} %get-tuple-element.51.small_own.refs_2_, ...), custom_call_target="tpu_custom_call" | custom-call | flops 600000000 | bytes 1000000 | tf_op jit(solution)/shard_map/finish/pallas_call | solution.py:779
  48.5 1.4 %collective-permute-start.15 = (bf16[128,512]{1,0:T(8,128)(2,1)S(1)}, bf16[128,512]{1,0:T(8,128)(2,1)S(1)}, u32[]{:S(2)}, u32[]{:S(2)}) collective-permute-start(bf16[128,512]{1,0:T(8,128)(2,1)S(1)} %get-tuple-element.85), channel_id=1, source_target_pairs={{0,1},{1,0},{2,3},{3,2},{4,5},{5,4},{6,7},{7,6},{8,9},{9,8},{10,11... | collective-permute-start | bytes 393224 | tf_op jit(solution)/shard_map/ppermute | solution.py:805
  49.9 1.0 %collective-permute-done.15.refs_2_ = bf16[128,512]{1,0:T(8,128)(2,1)S(1)} collective-permute-done((bf16[128,512]{1,0:T(8,128)(2,1)S(1)}, bf16[128,512]{1,0:T(8,128)(2,1)S(1)}, u32[]{:S(2)}, u32[]{:S(2)}) %collective-permute-start.15) | collective-permute-done | bytes 131104 | tf_op jit(solution)/shard_map/ppermute | solution.py:805
  50.9 0.8 %swap.1 = bf16[128,2048]{1,0:T(8,128)(2,1)} custom-call(bf16[128,512]{1,0:T(8,128)(2,1)S(1)} %get-tuple-element.69.refs_0_, bf16[128,512]{1,0:T(8,128)(2,1)S(1)} %get-tuple-element.84.refs_1_, bf16[128,512]{1,0:T(8,128)(2,1)S(1)} %collective-permute-done.15.refs_2_, bf16[128,512]{1,0:T(8,128)(2,1)S(1)} %collective-permute-done.16.refs_3_), custom_call_target="tpu_custom_call" | custom-call | tf_op jit(solution)/shard_map/swap/pallas_call | solution.py:806
  (32 shorter events, 4.5 us)
Async XLA Ops:
  0.0 11.0 %collective-permute-start = (bf16[128,2048]{1,0:T(8,128)(2,1)}, bf16[128,2048]{1,0:T(8,128)(2,1)S(1)}, u32[]{:S(2)}, u32[]{:S(2)}) collective-permute-start(bf16[128,2048]{1,0:T(8,128)(2,1)} %key.1), channel_id=1, source_target_pairs={{0,1},{1,0},{2,3},{3,2},{4,5},{5,4},{6,7},{7,6},{8,9},{9,8},{10,11... | collective-permute-start | bytes 1572872 | tf_op jit(solution)/shard_map/ppermute | solution.py:577
  0.7 10.3 %collective-permute-start.1 = (bf16[128,2048]{1,0:T(8,128)(2,1)}, bf16[128,2048]{1,0:T(8,128)(2,1)S(1)}, u32[]{:S(2)}, u32[]{:S(2)}) collective-permute-start(bf16[128,2048]{1,0:T(8,128)(2,1)} %value.1), channel_id=1, source_target_pairs={{0,1},{1,0},{2,3},{3,2},{4,5},{5,4},{6,7},{7,6},{8,9},{9,8},{10,11... | collective-permute-start | bytes 1572872 | tf_op jit(solution)/shard_map/ppermute | solution.py:578
  0.7 7.2 %copy-start.1 = (bf16[128,2048]{1,0:T(8,128)(2,1)S(1)}, bf16[128,2048]{1,0:T(8,128)(2,1)}, u32[]{:S(2)}) copy-start(bf16[128,2048]{1,0:T(8,128)(2,1)} %query.1) | copy-start | bytes 1572868
  0.7 10.3 %copy-start.2 = (bf16[128,2048]{1,0:T(8,128)(2,1)S(1)}, bf16[128,2048]{1,0:T(8,128)(2,1)}, u32[]{:S(2)}) copy-start(bf16[128,2048]{1,0:T(8,128)(2,1)} %gate.1) | copy-start | bytes 1572868
  2.3 8.7 %collective-permute-start.4 = (f32[208,128]{1,0:T(8,128)S(1)}, f32[208,128]{1,0:T(8,128)S(1)}, u32[]{:S(2)}, u32[]{:S(2)}) collective-permute-start(f32[208,128]{1,0:T(8,128)S(1)} %get-tuple-element.51.small_own.refs_2_), channel_id=1, source_target_pairs={{0,1},{1,0},{2,3},{3,2},{4,5},{5,4},{6,7},{7,6},{8,9},{9,8},{10,11... | collective-permute-start | bytes 319496 | tf_op jit(solution)/shard_map/ppermute | solution.py:619
  2.9 5.0 %collective-permute-start.2 = (bf16[16,2048]{1,0:T(8,128)(2,1)S(1)}, bf16[16,2048]{1,0:T(8,128)(2,1)S(1)}, u32[]{:S(2)}, u32[]{:S(2)}) collective-permute-start(bf16[16,2048]{1,0:T(8,128)(2,1)S(1)} %get-tuple-element.50), channel_id=1, source_target_pairs={{1,2},{3,4},{5,6},{9,10},{11,12},{13,14},{17,18},{19,20},{21,22},{... | collective-permute-start | bytes 196616 | tf_op jit(solution)/shard_map/ppermute | solution.py:617
  6.0 5.0 %collective-permute-start.3 = (bf16[16,2048]{1,0:T(8,128)(2,1)S(1)}, bf16[16,2048]{1,0:T(8,128)(2,1)S(1)}, u32[]{:S(2)}, u32[]{:S(2)}) collective-permute-start(bf16[16,2048]{1,0:T(8,128)(2,1)S(1)} %get-tuple-element.50), channel_id=1, source_target_pairs={{1,3},{3,5},{5,7},{9,11},{11,13},{13,15},{17,19},{19,21},{21,23},{... | collective-permute-start | bytes 196616 | tf_op jit(solution)/shard_map/ppermute | solution.py:618
  7.9 17.4 %collective-permute-start.10 = (bf16[128,2048]{1,0:T(8,128)(2,1)S(1)}, bf16[128,2048]{1,0:T(8,128)(2,1)S(1)}, u32[]{:S(2)}, u32[]{:S(2)}) collective-permute-start(bf16[128,2048]{1,0:T(8,128)(2,1)S(1)} %copy-done.1), channel_id=1, source_target_pairs={{0,1},{1,0},{2,3},{3,2},{4,5},{5,4},{6,7},{7,6},{8,9},{9,8},{10,11... | collective-permute-start | bytes 1572872 | tf_op jit(solution)/shard_map/ppermute | solution.py:620
  11.0 26.4 %collective-permute-start.8 = (bf16[128,2048]{1,0:T(8,128)(2,1)S(1)}, bf16[128,2048]{1,0:T(8,128)(2,1)S(1)}, u32[]{:S(2)}, u32[]{:S(2)}) collective-permute-start(bf16[128,2048]{1,0:T(8,128)(2,1)S(1)} %copy-done.2), channel_id=1, source_target_pairs={{0,1},{1,0},{2,3},{3,2},{4,5},{5,4},{6,7},{7,6},{8,9},{9,8},{10,11... | collective-permute-start | bytes 1572872 | tf_op jit(solution)/shard_map/ppermute | solution.py:621
  15.9 19.3 %collective-permute-start.14 = (bf16[528,128]{1,0:T(8,128)(2,1)S(1)}, bf16[528,128]{1,0:T(8,128)(2,1)S(1)}, u32[]{:S(2)}, u32[]{:S(2)}) collective-permute-start(bf16[528,128]{1,0:T(8,128)(2,1)S(1)} %code.3), channel_id=1, source_target_pairs={{4,6},{5,7},{12,14},{13,15},{20,22},{21,23},{28,30},{29,31}} | collective-permute-start | bytes 405512 | tf_op jit(solution)/shard_map/ppermute | solution.py:632
  17.8 15.1 %collective-permute-start.11 = (bf16[528,128]{1,0:T(8,128)(2,1)S(1)}, bf16[528,128]{1,0:T(8,128)(2,1)S(1)}, u32[]{:S(2)}, u32[]{:S(2)}) collective-permute-start(bf16[528,128]{1,0:T(8,128)(2,1)S(1)} %get-tuple-element.70), channel_id=1, source_target_pairs={{0,2},{1,3},{4,6},{5,7},{8,10},{9,11},{12,14},{13,15},{16,18},{17,... | collective-permute-start | bytes 405512 | tf_op jit(solution)/shard_map/ppermute | solution.py:632
  24.0 11.8 %collective-permute-start.9 = (bf16[528,128]{1,0:T(8,128)(2,1)S(1)}, bf16[528,128]{1,0:T(8,128)(2,1)S(1)}, u32[]{:S(2)}, u32[]{:S(2)}) collective-permute-start(bf16[528,128]{1,0:T(8,128)(2,1)S(1)} %code.2), channel_id=1, source_target_pairs={{4,6},{5,7},{12,14},{13,15},{20,22},{21,23},{28,30},{29,31}} | collective-permute-start | bytes 405512 | tf_op jit(solution)/shard_map/ppermute | solution.py:632
  25.3 8.4 %collective-permute-start.5 = (bf16[528,128]{1,0:T(8,128)(2,1)S(1)}, bf16[528,128]{1,0:T(8,128)(2,1)S(1)}, u32[]{:S(2)}, u32[]{:S(2)}) collective-permute-start(bf16[528,128]{1,0:T(8,128)(2,1)S(1)} %get-tuple-element.52), channel_id=1, source_target_pairs={{0,2},{1,3},{4,6},{5,7},{8,10},{9,11},{12,14},{13,15},{16,18},{17,... | collective-permute-start | bytes 405512 | tf_op jit(solution)/shard_map/ppermute | solution.py:632
  33.1 4.4 %collective-permute-start.12 = (bf16[528,128]{1,0:T(8,128)(2,1)S(1)}, bf16[528,128]{1,0:T(8,128)(2,1)S(1)}, u32[]{:S(2)}, u32[]{:S(2)}) collective-permute-start(bf16[528,128]{1,0:T(8,128)(2,1)S(1)} %join.3), channel_id=1, source_target_pairs={{2,6},{3,7},{10,14},{11,15},{18,22},{19,23},{26,30},{27,31}} | collective-permute-start | bytes 405512 | tf_op jit(solution)/shard_map/ppermute | solution.py:632
  33.7 8.1 %collective-permute-start.13 = (bf16[528,128]{1,0:T(8,128)(2,1)S(1)}, bf16[528,128]{1,0:T(8,128)(2,1)S(1)}, u32[]{:S(2)}, u32[]{:S(2)}) collective-permute-start(bf16[528,128]{1,0:T(8,128)(2,1)S(1)} %join.3), channel_id=1, source_target_pairs={{2,4},{3,5},{10,12},{11,13},{18,20},{19,21},{26,28},{27,29}} | collective-permute-start | bytes 405512 | tf_op jit(solution)/shard_map/ppermute | solution.py:632
  35.2 10.5 %collective-permute-start.6 = (bf16[528,128]{1,0:T(8,128)(2,1)S(1)}, bf16[528,128]{1,0:T(8,128)(2,1)S(1)}, u32[]{:S(2)}, u32[]{:S(2)}) collective-permute-start(bf16[528,128]{1,0:T(8,128)(2,1)S(1)} %join.2), channel_id=1, source_target_pairs={{2,6},{3,7},{10,14},{11,15},{18,22},{19,23},{26,30},{27,31}} | collective-permute-start | bytes 405512 | tf_op jit(solution)/shard_map/ppermute | solution.py:632
  35.9 11.8 %collective-permute-start.7 = (bf16[528,128]{1,0:T(8,128)(2,1)S(1)}, bf16[528,128]{1,0:T(8,128)(2,1)S(1)}, u32[]{:S(2)}, u32[]{:S(2)}) collective-permute-start(bf16[528,128]{1,0:T(8,128)(2,1)S(1)} %join.2), channel_id=1, source_target_pairs={{2,4},{3,5},{10,12},{11,13},{18,20},{19,21},{26,28},{27,29}} | collective-permute-start | bytes 405512 | tf_op jit(solution)/shard_map/ppermute | solution.py:632
  41.9 0.7 %copy-start = (f32[128]{0:T(128)S(1)}, f32[128]{0:T(128)}, u32[]{:S(2)}) copy-start(f32[128]{0:T(128)} %param.21) | copy-start | bytes 1540
  43.4 6.5 %collective-permute-start.16 = (bf16[128,512]{1,0:T(8,128)(2,1)S(1)}, bf16[128,512]{1,0:T(8,128)(2,1)S(1)}, u32[]{:S(2)}, u32[]{:S(2)}) collective-permute-start(bf16[128,512]{1,0:T(8,128)(2,1)S(1)} %get-tuple-element.86), channel_id=1, source_target_pairs={{0,1},{1,0},{2,3},{3,2},{4,5},{5,4},{6,7},{7,6},{8,9},{9,8},{10,11... | collective-permute-start | bytes 393224 | tf_op jit(solution)/shard_map/ppermute | solution.py:805
  48.5 2.4 %collective-permute-start.15 = (bf16[128,512]{1,0:T(8,128)(2,1)S(1)}, bf16[128,512]{1,0:T(8,128)(2,1)S(1)}, u32[]{:S(2)}, u32[]{:S(2)}) collective-permute-start(bf16[128,512]{1,0:T(8,128)(2,1)S(1)} %get-tuple-element.85), channel_id=1, source_target_pairs={{0,1},{1,0},{2,3},{3,2},{4,5},{5,4},{6,7},{7,6},{8,9},{9,8},{10,11... | collective-permute-start | bytes 393224 | tf_op jit(solution)/shard_map/ppermute | solution.py:805

commit v2 on v1

--- a/solution.py
+++ b/solution.py
@@ -67,23 +67,25 @@
     return index % 2, index // 2
 
 
-def fill(scratch, own, other, halo, core, group, first):
+def fill(scratch, own, other, before, core, chunk, first_lane):
     lanes = scratch.shape[1]
-    start = pl.multiple_of(core * 8 * HEAD_DIM + group * lanes, lanes)
-    rows = halo[0][:, pl.ds(start, lanes)].astype(F32) + halo[1][:, pl.ds(start, lanes)].astype(F32)
-    scratch[5:8, :] = rows[first : first + 3]
-    place_own = pl.multiple_of(8 + CHUNK * core, 8)
-    scratch[pl.ds(place_own, CHUNK), :] = own[:, group * lanes : (group + 1) * lanes].astype(F32)
-    place_other = pl.multiple_of(8 + CHUNK * (1 - core), 8)
-    scratch[pl.ds(place_other, CHUNK), :] = other[:, pl.ds(start, lanes)].astype(F32)
-
-
-def conv(scratch, taps, chunk, columns, taps_columns):
+    start = pl.multiple_of(core * 8 * HEAD_DIM + first_lane, 128)
+    mine = own[:, first_lane : first_lane + lanes]
+    theirs = other[:, pl.ds(start, lanes)]
+    if before is None:
+        last = jnp.where(core == 1, theirs[CHUNK - 16 :], mine[CHUNK - 16 :]).astype(F32)[13:16]
+    else:
+        one, two, first = before
+        rows = one[:, pl.ds(start, lanes)].astype(F32) + two[:, pl.ds(start, lanes)].astype(F32)
+        last = rows[first : first + 3]
+    scratch[5:8, :] = last
+    scratch[8 : 8 + CHUNK, :] = jnp.where(core == chunk, mine, theirs).astype(F32)
+
+
+def conv(scratch, taps, columns, taps_columns):
     total = None
     for tap in range(4):
-        part = taps[tap : tap + 1, taps_columns] * scratch[
-            5 + tap + CHUNK * chunk : 5 + tap + CHUNK * chunk + CHUNK, columns
-        ]
+        part = taps[tap : tap + 1, taps_columns] * scratch[5 + tap : 5 + tap + CHUNK, columns]
         total = part if total is None else total + part
     return silu(total)
 
@@ -172,8 +174,8 @@
 
 
 def prepare_kernel(query, key, value, gate, log_alpha, strength, mixture, query_taps, key_taps,
-                   value_taps, query_half, key_half, value_half, gate_half, query_taps_half,
-                   key_taps_half, value_taps_half, halo, small, tails, sems):
+                   value_taps, gain, query_half, key_half, value_half, gate_half, query_taps_half,
+                   key_taps_half, value_taps_half, halo, small, gain_out, tails, sems):
     core, _ = place()
     rows, half = query_half.shape
     lanes = pl.ds(pl.multiple_of(core * half, half), half)
@@ -199,6 +201,7 @@
         (gate, gate_half),
     ):
         copy(x.at[:, lanes], y)
+    copy(gain, gain_out)
     for made in copies:
         made.wait()
     message = [tails[i][13:16, :].astype(F32) for i in range(3)]
@@ -206,7 +209,113 @@
     halo[...] = jnp.concatenate(message, axis=0).astype(BF16)
 
 
-def states_kernel(
+def chunk_states(
+    chunk,
+    first,
+    heads,
+    key_taps,
+    value_taps,
+    small_own,
+    small_other,
+    key_cols_out,
+    inverse_out,
+    write_out,
+    key_scratch,
+    value_scratch,
+):
+    core, _ = place()
+    t, j = iotas(CHUNK, CHUNK)
+    base = 8 * core + first
+    parts = [(head, chunk) for head in range(heads)]
+    run = sums(small_own, small_other, base, parts, core)
+    strengths = [
+        token_row(small_own, small_other, 16 + base + head, core, chunk) for head in range(heads)
+    ]
+    columns = rows_table(run + strengths).T
+
+    def lanes(head):
+        return slice(head * 128, head * 128 + 128)
+
+    def beta(head):
+        return columns[:, heads + head : heads + head + 1]
+
+    keys = [
+        unit(conv(key_scratch, key_taps, lanes(head), lanes(first + head)))
+        for head in range(heads)
+    ]
+    keys_t = [key.T for key in keys]
+    coupling = []
+    for head in range(heads):
+        pair = split(keys_t[head])
+        key_cols_out[head, 0] = pair[0]
+        key_cols_out[head, 1] = pair[1]
+        gram = mm(split(keys[head]), pair)
+        ratio = decay(columns[:, head : head + 1], run[head], t, j)
+        coupling.append(jnp.where(t > j, gram * ratio * beta(head), 0.0))
+    inverse = invert(coupling, t, j)
+    mixed = []
+    for head in range(heads):
+        inverse_out[head, 0] = inverse[head][0]
+        inverse_out[head, 1] = inverse[head][1]
+        last = run[head][:, CHUNK - 1 : CHUNK]
+        tail = keys_t[head] * jnp.exp(last - run[head])
+        mixed.append(mm(split(tail), inverse[head]))
+    transits = []
+    states = []
+    for head in range(heads):
+        value = conv(value_scratch, value_taps, lanes(head), lanes(first + head))
+        grow = jnp.exp(columns[:, head : head + 1])
+        write = jnp.concatenate([keys[head] * (beta(head) * grow), value * beta(head)], axis=1)
+        write = split(write)
+        write_out[head, 0] = write[0]
+        write_out[head, 1] = write[1]
+        last = run[head][:, CHUNK - 1 : CHUNK]
+        both = mm(split(mixed[head]), write)
+        transits.append(jnp.where(t == j, jnp.exp(last), 0.0) - both[:, :128])
+        states.append(both[:, 128:])
+    return transits, states
+
+
+def upper_kernel(
+    key_own,
+    key_other,
+    value_own,
+    value_other,
+    key_taps,
+    value_taps,
+    small_own,
+    small_other,
+    key_cols_out,
+    inverse_out,
+    write_out,
+    transit_out,
+    state_out,
+    key_scratch,
+    value_scratch,
+):
+    core, _ = place()
+    fill(key_scratch, key_own, key_other, None, core, 1, 0)
+    fill(value_scratch, value_own, value_other, None, core, 1, 0)
+    transits, states = chunk_states(
+        1,
+        0,
+        8,
+        key_taps,
+        value_taps,
+        small_own,
+        small_other,
+        key_cols_out,
+        inverse_out,
+        write_out,
+        key_scratch,
+        value_scratch,
+    )
+    for head in range(8):
+        transit_out[head] = transits[head]
+        state_out[head] = states[head]
+
+
+def lower_kernel(
     group,
     heads,
     key_own,
@@ -219,6 +328,8 @@
     halo_two,
     small_own,
     small_other,
+    upper_transit,
+    upper_state,
     key_cols_out,
     inverse_out,
     write_out,
@@ -231,74 +342,33 @@
     value_scratch,
 ):
     core, _ = place()
-    fill(key_scratch, key_own, key_other, (halo_one, halo_two), core, group, 3)
-    fill(value_scratch, value_own, value_other, (halo_one, halo_two), core, group, 6)
-    t, j = iotas(CHUNK, CHUNK)
-    parts = [(head, chunk) for head in range(heads) for chunk in range(2)]
-    count = len(parts)
-    base = 8 * core + heads * group
-    run = sums(small_own, small_other, base, parts, core)
-    strengths = [
-        token_row(small_own, small_other, 16 + base + head, core, chunk) for head, chunk in parts
-    ]
-    columns = rows_table(run + strengths).T
-
-    def lanes(head):
-        return slice(head * 128, head * 128 + 128)
-
-    def taps_lanes(head):
-        return lanes(group * heads + head)
-
-    def beta(i):
-        return columns[:, count + i : count + i + 1]
-
-    keys = [
-        unit(conv(key_scratch, key_taps, chunk, lanes(head), taps_lanes(head)))
-        for head, chunk in parts
-    ]
-    keys_t = [key.T for key in keys]
-    coupling = []
-    for i, (head, chunk) in enumerate(parts):
-        pair = split(keys_t[i])
-        key_cols_out[head, chunk, 0] = pair[0]
-        key_cols_out[head, chunk, 1] = pair[1]
-        gram = mm(split(keys[i]), pair)
-        ratio = decay(columns[:, i : i + 1], run[i], t, j)
-        coupling.append(jnp.where(t > j, gram * ratio * beta(i), 0.0))
-    inverse = invert(coupling, t, j)
-    mixed = []
-    for i, (head, chunk) in enumerate(parts):
-        inverse_out[head, chunk, 0] = inverse[i][0]
-        inverse_out[head, chunk, 1] = inverse[i][1]
-        last = run[i][:, CHUNK - 1 : CHUNK]
-        tail = keys_t[i] * jnp.exp(last - run[i])
-        mixed.append(mm(split(tail), inverse[i]))
-    transits = []
-    states = []
-    for i, (head, chunk) in enumerate(parts):
-        value = conv(value_scratch, value_taps, chunk, lanes(head), taps_lanes(head))
-        grow = jnp.exp(columns[:, i : i + 1])
-        write = jnp.concatenate([keys[i] * (beta(i) * grow), value * beta(i)], axis=1)
-        write = split(write)
-        write_out[head, chunk, 0] = write[0]
-        write_out[head, chunk, 1] = write[1]
-        last = run[i][:, CHUNK - 1 : CHUNK]
-        both = mm(split(mixed[i]), write)
-        transits.append(jnp.where(t == j, jnp.exp(last), 0.0) - both[:, :128])
-        states.append(both[:, 128:])
-    scales = []
+    first = group * heads
+    fill(key_scratch, key_own, key_other, (halo_one, halo_two, 3), core, 0, first * 128)
+    fill(value_scratch, value_own, value_other, (halo_one, halo_two, 6), core, 0, first * 128)
+    transits, states = chunk_states(
+        0,
+        first,
+        heads,
+        key_taps,
+        value_taps,
+        small_own,
+        small_other,
+        key_cols_out,
+        inverse_out,
+        write_out,
+        key_scratch,
+        value_scratch,
+    )
+    joined = []
+    pairs = [split(upper_transit[first + head]) for head in range(heads)]
     for head in range(heads):
-        low, high = 2 * head, 2 * head + 1
-        pair = split(transits[high])
-        state = mm(pair, split(states[low])) + states[high]
-        first_state_out[head] = states[low]
-        transit_one_out[head] = transits[low]
-        state_out[head] = state
-        transit_out[head] = mm(pair, split(transits[low]))
-        code, scale = encode(state)
-        code_out[head * 128 : head * 128 + 128, :] = code
-        scales.append(scale)
-    code_out[heads * 128 : heads * 128 + 16, :] = pack_rows(scales)
+        joined.append(mm(pairs[head], split(states[head])) + upper_state[first + head])
+    encode_all(joined, code_out)
+    for head in range(heads):
+        first_state_out[head] = states[head]
+        transit_one_out[head] = transits[head]
+        state_out[head] = joined[head]
+        transit_out[head] = mm(pairs[head], split(transits[head]))
 
 
 def queries_kernel(
@@ -314,22 +384,27 @@
     halo_two,
     small_own,
     small_other,
-    key_cols,
-    inverse,
-    write,
+    key_cols_one,
+    inverse_one,
+    write_one,
+    key_cols_two,
+    inverse_two,
+    write_two,
     first_state,
     transit_one,
     out,
     moved,
-    query_scratch,
+    scratch_one,
+    scratch_two,
 ):
     core, _ = place()
-    piece = (group * heads + first) // count
-    fill(query_scratch, query_own, query_other, (halo_one, halo_two), core, piece, 0)
+    start = group * heads + first
+    fill(scratch_one, query_own, query_other, (halo_one, halo_two, 0), core, 0, start * 128)
+    fill(scratch_two, query_own, query_other, None, core, 1, start * 128)
     t, j = iotas(CHUNK, CHUNK)
     apart = t ^ j
     parts = [(head, chunk) for head in range(count) for chunk in range(2)]
-    base = 8 * core + heads * group + first
+    base = 8 * core + start
     run = sums(small_own, small_other, base, parts, core)
     rows = list(run)
     for head, chunk in parts:
@@ -337,25 +412,30 @@
             row = 32 + 16 * level + base + head
             rows.append(token_row(small_own, small_other, row, core, chunk))
     columns = rows_table(rows).T
+
+    def held(one, two, head, chunk):
+        if chunk:
+            return two[start + head, 0], two[start + head, 1]
+        return one[first + head, 0], one[first + head, 1]
+
     mixings = []
     queries = []
     for i, (head, chunk) in enumerate(parts):
         lanes = slice(head * 128, head * 128 + 128)
-        full = group * heads + first + head
-        taps_lanes = slice(full * 128, full * 128 + 128)
-        query = unit(conv(query_scratch, query_taps, chunk, lanes, taps_lanes))
+        taps_lanes = slice((start + head) * 128, (start + head) * 128 + 128)
+        scratch = scratch_two if chunk else scratch_one
+        query = unit(conv(scratch, query_taps, lanes, taps_lanes))
         queries.append(query)
-        at = first + head
         ratio = decay(columns[:, i : i + 1], run[i], t, j)
-        scores = mm(split(query), (key_cols[at, chunk, 0], key_cols[at, chunk, 1])) * ratio
-        mixings.append(mm(split(scores), (inverse[at, chunk, 0], inverse[at, chunk, 1])))
+        scores = mm(split(query), held(key_cols_one, key_cols_two, head, chunk)) * ratio
+        mixings.append(mm(split(scores), held(inverse_one, inverse_two, head, chunk)))
     for i, (head, chunk) in enumerate(parts):
         at = len(parts) + i * (near + 1)
         level_mat = columns[:, at : at + 1]
         for level in range(1, near):
             weight = columns[:, at + level : at + level + 1]
             level_mat = jnp.where(apart >= 1 << (level - 1), weight, level_mat)
-        high, low = (write[first + head, chunk, 0], write[first + head, chunk, 1])
+        high, low = held(write_one, write_two, head, chunk)
         within = mm(split(mixings[i] * level_mat), (high[:, 128:], low[:, 128:]))
         grow = jnp.exp(columns[:, i : i + 1])
         effective = grow * queries[i] - mm(split(mixings[i]), (high[:, :128], low[:, :128]))
@@ -396,7 +476,7 @@
     code_out[head * 128 : head * 128 + 16, :] = pack_rows(scales)
 
 
-def join_kernel(level, arrivals, with_transit, *refs):
+def join_kernel(level, arrivals, with_transit, shift, *refs):
     state_in = refs[:arrivals]
     refs = refs[arrivals:]
     transit_in = ()
@@ -408,6 +488,8 @@
     heads = state.shape[0]
     _, node = place()
     upper = (node >> level) % 2 == 1
+    if not with_transit:
+        upper = upper & ((node >> (level + 1)) % 2 == 0)
 
     @pl.when(upper)
     def _():
@@ -417,23 +499,25 @@
             fresh.append(mm(pair, split(received(state_in, head))) + state[head])
             if with_transit:
                 refs[0][head] = fresh[head]
-                refs[1][head] = mm(pair, split(received(transit_in, head)))
+                refs[1][head] = mm(pair, split(received(transit_in, shift + head)))
         encode_all(fresh, code_out)
         if with_transit:
             encode_all([refs[1][head] for head in range(heads)], refs[2])
 
-    @pl.when(jnp.logical_not(upper))
-    def _():
-        encode_all([state[head] for head in range(heads)], code_out)
-        if with_transit:
+    if with_transit:
+
+        @pl.when(jnp.logical_not(upper))
+        def _():
+            encode_all([state[head] for head in range(heads)], code_out)
             for head in range(heads):
                 refs[0][head] = state[head]
                 refs[1][head] = transit[head]
             encode_all([transit[head] for head in range(heads)], refs[2])
 
 
-def code_kernel(value, code_out):
-    encode_all([value[head] for head in range(value.shape[0])], code_out)
+def code_kernel(*refs):
+    values = [ref[head] for ref in refs[:-1] for head in range(ref.shape[0])]
+    encode_all(values, refs[-1])
 
 
 def level_weight(own, other, row, core):
@@ -442,23 +526,37 @@
     return jnp.concatenate([columns[:, 0:1], columns[:, 1:2]], axis=0)
 
 
-def absorb_kernel(level, weight_row, group, heads, arrivals, pieces, *refs):
+def absorb_kernel(level, weight_row, group, heads, arrivals, passed, pieces, *refs):
     state_in = refs[:arrivals]
-    transit_in = refs[arrivals : 2 * arrivals]
-    refs = refs[2 * arrivals :]
+    transit_in = refs[arrivals : arrivals + passed]
+    refs = refs[arrivals + passed :]
     small_own, small_other = refs[:2]
     outs_in = refs[2 : 2 + pieces]
     moved_in = refs[2 + pieces : 2 + 2 * pieces]
     out, moved = refs[2 + 2 * pieces :]
     core, node = place()
     upper = (node >> level) % 2 == 1
-    later = (node >> (level + 1)) > 0
     each = heads // pieces
+    behind = jnp.bool_(False)
+    if passed:
+        behind = ((node >> (level - 1)) % 2 == 1) & ((node >> level) > 0)
+
+        @pl.when(behind)
+        def _():
+            shift = group * heads if level == 1 else 0
+            for head in range(heads):
+                pair = split(moved_in[head // each][head % each])
+                moved[head] = mm(pair, split(received(transit_in, shift + head)))
+
+    @pl.when(jnp.logical_not(behind))
+    def _():
+        for head in range(heads):
+            moved[head] = moved_in[head // each][head % each]
 
     @pl.when(upper)
     def _():
         for head in range(heads):
-            pair = split(moved_in[head // each][head % each])
+            pair = split(moved[head])
             row = weight_row + 8 * core + heads * group + head
             weight = level_weight(small_own, small_other, row, core)
             gain = mm(pair, split(received(state_in, head)))
@@ -469,21 +567,62 @@
         for head in range(heads):
             out[head] = outs_in[head // each][head % each]
 
-    @pl.when(upper & later)
-    def _():
-        for head in range(heads):
-            pair = split(moved_in[head // each][head % each])
-            moved[head] = mm(pair, split(received(transit_in, head)))
-
-    @pl.when(jnp.logical_not(upper & later))
-    def _():
-        for head in range(heads):
-            moved[head] = moved_in[head // each][head % each]
-
-
-def finish_kernel(level, weight_row, group, heads, arrivals, pieces, *refs):
+
+def tail_kernel(level, weight_row, groups, heads, count, pending, near, arrivals, *refs):
+    state_in = [refs[g * arrivals : (g + 1) * arrivals] for g in range(groups)]
+    refs = refs[groups * arrivals :]
+    query_refs, refs = refs[:7], refs[7:]
+    uppers, refs = refs[:3], refs[3:]
+    lowers = {}
+    for group in sorted({group for group, _ in pending}):
+        lowers[group], refs = refs[:5], refs[5:]
+    pieces = heads // count
+    outs_in = {}
+    for group in range(groups):
+        for piece in range(pieces):
+            if (group, piece) not in pending:
+                outs_in[group, piece], refs = refs[:2], refs[2:]
+    outs, refs = refs[: 2 * groups], refs[2 * groups :]
+    scratch, refs = refs[:2], refs[2:]
+    for group, piece in pending:
+        temporary, refs = refs[:2], refs[2:]
+        made = lowers[group]
+        queries_kernel(
+            group,
+            heads,
+            piece * count,
+            count,
+            near,
+            *query_refs,
+            *made[:3],
+            *uppers,
+            *made[3:],
+            *temporary,
+            *scratch,
+        )
+        outs_in[group, piece] = temporary
+    for group in range(groups):
+        absorb_kernel(
+            level,
+            weight_row,
+            group,
+            heads,
+            arrivals,
+            0,
+            pieces,
+            *state_in[group],
+            *query_refs[5:7],
+            *[outs_in[group, piece][0] for piece in range(pieces)],
+            *[outs_in[group, piece][1] for piece in range(pieces)],
+            outs[2 * group],
+            outs[2 * group + 1],
+        )
+
+
+def finish_kernel(level, weight_row, group, heads, arrivals, passed, pieces, *refs):
     state_in = refs[:arrivals]
-    refs = refs[arrivals:]
+    transit_in = refs[arrivals : arrivals + passed]
+    refs = refs[arrivals + passed :]
     small_own, small_other, gate_own, gate_other, gain = refs[:5]
     outs_in = refs[5 : 5 + pieces]
     moved_in = refs[5 + pieces : 5 + 2 * pieces]
@@ -492,13 +631,33 @@
     upper = (node >> level) % 2 == 1
     each = heads // pieces
 
-    @pl.when(upper)
-    def _():
+    def add(through):
+        states = [received(state_in, head) for head in range(heads)]
+        if through:
+            shift = group * heads if level == 1 else 0
+            states = [
+                mm(split(received(transit_in, shift + head)), split(states[head]))
+                for head in range(heads)
+            ]
         for head in range(heads):
             row = weight_row + 8 * core + heads * group + head
             weight = level_weight(small_own, small_other, row, core)
-            extra = mm(split(moved_in[head // each][head % each]), split(received(state_in, head)))
+            extra = mm(split(moved_in[head // each][head % each]), split(states[head]))
             total[head] = outs_in[head // each][head % each] + weight * extra
+
+    through = jnp.bool_(False)
+    if passed:
+        through = (node >> (level - 1)) % 2 == 1
+
+    @pl.when(upper & jnp.logical_not(through))
+    def _():
+        add(False)
+
+    if passed:
+
+        @pl.when(upper & through)
+        def _():
+            add(True)
 
     @pl.when(jnp.logical_not(upper))
     def _():
@@ -547,7 +706,7 @@
 
 
 GROUPS = 2
-PIECES = 2
+PIECES = 1
 
 
 def per_device(
@@ -588,13 +747,14 @@
         value_taps_half,
         halo,
         small,
+        gain,
     ) = pl.pallas_call(
         prepare_kernel,
-        in_specs=[pl.BlockSpec(memory_space=pltpu.HBM)] * 10,
+        in_specs=[pl.BlockSpec(memory_space=pltpu.HBM)] * 11,
         out_shape=[half_shape] * 4
         + [taps_shape] * 3
-        + [struct((16, width), BF16), struct((small_rows, 128))],
-        scratch_shapes=[pltpu.VMEM((3, 16, width), BF16), pltpu.SemaphoreType.DMA((13,))],
+        + [struct((16, width), BF16), struct((small_rows, 128)), struct((1, 128))],
+        scratch_shapes=[pltpu.VMEM((3, 16, width), BF16), pltpu.SemaphoreType.DMA((14,))],
         compiler_params=params(8),
         name="prepare",
     )(
@@ -611,14 +771,13 @@
                 query_taps,
                 key_taps,
                 value_taps,
+                norm_gain.reshape(1, 128),
             )
         ]
     )
+    small_other = lax.ppermute(small, "seq", cores)
     halo_one = lax.ppermute(halo, "seq", [(i, i + 1) for i in range(1, size - 1, 2)])
     halo_two = lax.ppermute(halo, "seq", [(i, i + 2) for i in range(1, size - 1, 2)])
-    small_other = lax.ppermute(small, "seq", cores)
-    query_other = lax.ppermute(query_rows, "seq", cores)
-    gate_other = lax.ppermute(output_gate, "seq", cores)
 
     def fan(value, level, keep):
         span = 1 << level
@@ -632,147 +791,218 @@
             results.append(lax.ppermute(value, "seq", route))
         return results
 
+    def held(count):
+        return [
+            struct((count, 2, 128, 128), BF16),
+            struct((count, 2, 128, 128), BF16),
+            struct((count, 2, 128, 256), BF16),
+        ]
+
     square = (heads, 128, 128)
-    pair = struct((heads, 2, 2, 128, 128), BF16)
     code_shape = struct((heads * 128 + 16, 128), BF16)
+    upper = pl.pallas_call(
+        upper_kernel,
+        out_shape=held(8) + [struct((8, 128, 128))] * 2,
+        scratch_shapes=[pltpu.VMEM((8 + CHUNK, half), F32)] * 2,
+        compiler_params=params(24),
+        cost_estimate=cost(4_000_000_000),
+        name="upper",
+    )(
+        key_half,
+        key_other,
+        value_half,
+        value_other,
+        key_taps_half,
+        value_taps_half,
+        small,
+        small_other,
+    )
     local = []
     arrived = []
+    after = upper[4]
     for group in range(GROUPS):
-        local.append(
-            pl.pallas_call(
-                functools.partial(states_kernel, group, heads),
-                out_shape=[
-                    pair,
-                    pair,
-                    struct((heads, 2, 2, 128, 256), BF16),
-                    struct(square),
-                    struct(square),
-                    struct(square),
-                    struct(square),
-                    code_shape,
-                ],
-                scratch_shapes=[pltpu.VMEM((8 + 2 * CHUNK, lanes), F32)] * 2,
-                compiler_params=params(24),
-                cost_estimate=cost(4_000_000_000),
-                name="states",
-            )(
-                key_half,
-                key_other,
-                value_half,
-                value_other,
-                key_taps_half,
-                value_taps_half,
-                halo_one,
-                halo_two,
-                small,
-                small_other,
-            )
+        after, halo_first = lax.optimization_barrier((after, halo_one))
+        made = pl.pallas_call(
+            functools.partial(lower_kernel, group, heads),
+            out_shape=held(heads)
+            + [struct(square), struct(square), struct(square), struct(square), code_shape],
+            scratch_shapes=[pltpu.VMEM((8 + CHUNK, lanes), F32)] * 2,
+            compiler_params=params(24),
+            cost_estimate=cost(2_500_000_000),
+            name="lower",
+        )(
+            key_half,
+            key_other,
+            value_half,
+            value_other,
+            key_taps_half,
+            value_taps_half,
+            halo_first,
+            halo_two,
+            small,
+            small_other,
+            upper[3],
+            upper[4],
         )
-        arrived.append(fan(local[group][7], 0, lambda target: True) if shard_bits else [])
+        local.append(made)
+        after = made[7]
+        arrived.append(fan(made[7], 0, lambda target: True) if shard_bits else [])
+    after, query_late, gate_late = lax.optimization_barrier((after, query_rows, output_gate))
+    query_other = lax.ppermute(query_late, "seq", cores)
+    gate_other = lax.ppermute(gate_late, "seq", cores)
+    after, query_other, gate_other = lax.optimization_barrier((after, query_other, gate_other))
     state = [x[4] for x in local]
     transit = [x[6] for x in local]
-    transit_code = [None] * GROUPS
-    outs = [None] * GROUPS
-    moved = [None] * GROUPS
-
-    def ask(group):
-        key_cols, inverse, write, first_state, _, transit_one, _, _ = local[group]
-        outs[group] = []
-        moved[group] = []
-        count = heads // PIECES
+    count = heads // PIECES
+    outs = [[] for _ in range(GROUPS)]
+    moved = [[] for _ in range(GROUPS)]
+    pending = [(group, piece) for group in range(GROUPS) for piece in range(PIECES)]
+
+    def ask(after):
+        group, piece = pending.pop(0)
+        made = local[group]
         shape = struct((count, 2 * CHUNK, 128))
-        for piece in range(PIECES):
-            first = piece * count
-            out, move = pl.pallas_call(
-                functools.partial(queries_kernel, group, heads, first, count, near),
-                out_shape=[shape, shape],
-                scratch_shapes=[pltpu.VMEM((8 + 2 * CHUNK, count * 128), F32)],
-                compiler_params=params(16),
-                cost_estimate=cost(1_500_000_000),
-                name="queries",
-            )(
-                query_half,
-                query_other,
-                query_taps_half,
-                halo_one,
-                halo_two,
-                small,
-                small_other,
-                key_cols,
-                inverse,
-                write,
-                first_state,
-                transit_one,
-            )
-            outs[group].append(out)
-            moved[group].append(move)
-
-    def encoded(value):
+        after, small_here = lax.optimization_barrier((after, small))
+        out, move = pl.pallas_call(
+            functools.partial(queries_kernel, group, heads, piece * count, count, near),
+            out_shape=[shape, shape],
+            scratch_shapes=[pltpu.VMEM((8 + CHUNK, count * 128), F32)] * 2,
+            compiler_params=params(16),
+            cost_estimate=cost(4_000_000_000),
+            name="queries",
+        )(
+            query_half,
+            query_other,
+            query_taps_half,
+            halo_one,
+            halo_two,
+            small_here,
+            small_other,
+            *made[:3],
+            *upper[:3],
+            made[3],
+            made[5],
+        )
+        outs[group].append(out)
+        moved[group].append(move)
+        return out
+
+    moved_shape = struct((heads, 2 * CHUNK, 128))
+    transit_codes = [None] * GROUPS
+
+    def send_transit(after):
+        after, first_transit = lax.optimization_barrier((after, transit[0]))
         return pl.pallas_call(
             code_kernel,
-            out_shape=code_shape,
+            out_shape=struct((8 * 128 + 16, 128), BF16),
             compiler_params=params(8),
+            cost_estimate=cost(300_000_000),
             name="code",
-        )(value)
-
-    moved_shape = struct((heads, 2 * CHUNK, 128))
-    if shard_bits > 1:
-        transit_code = [encoded(x) for x in transit]
-    if shard_bits < 2:
-        for group in range(GROUPS):
-            ask(group)
+        )(first_transit, *transit[1:])
+
+    shifts = [heads * group for group in range(GROUPS)]
+    passing = [[]] * GROUPS
     for level in range(shard_bits - 1):
         keeps = level < shard_bits - 2
+
+        def wanted(target):
+            return keeps or target >> (level + 1) > 0
+
+        if level:
+            fanned = [fan(x, level, wanted) for x in transit_codes]
+        elif keeps:
+            fanned = [fan(send_transit(after), level, wanted)] * GROUPS
         following = []
         for group in range(GROUPS):
-            transit_arrived = fan(
-                transit_code[group], level, lambda target: keeps or target >> (level + 1) > 0
-            )
             shapes = [code_shape]
             operands = list(arrived[group])
             if keeps:
                 shapes += [struct(square), struct(square), code_shape]
-                operands += transit_arrived
+                operands += fanned[group]
+            after, state_here = lax.optimization_barrier((after, state[group]))
             joined = pl.pallas_call(
-                functools.partial(join_kernel, level, len(arrived[group]), keeps),
+                functools.partial(
+                    join_kernel, level, len(arrived[group]), keeps, shifts[group]
+                ),
                 out_shape=shapes,
                 compiler_params=params(12),
-                cost_estimate=cost(300_000_000),
+                cost_estimate=cost(4_000_000_000),
                 name="join",
-            )(*operands, state[group], transit[group])
+            )(*operands, state_here, transit[group])
+            after = joined[0]
+            if level == 0 and group == 0:
+                if not keeps:
+                    fanned = [fan(send_transit(after), level, wanted)] * GROUPS
             following.append(fan(joined[0], level + 1, lambda target: True))
             if keeps:
-                state[group], transit[group], transit_code[group] = joined[1:]
-            if level == 0:
-                ask(group)
-            arrivals = len(arrived[group])
-            out, move = pl.pallas_call(
+                state[group], transit[group], transit_codes[group] = joined[1:]
+        arrivals = len(arrived[0])
+        if level == 0:
+            after, small_here = lax.optimization_barrier((after, small))
+            operands = [x for group in range(GROUPS) for x in arrived[group]]
+            operands += [query_half, query_other, query_taps_half, halo_one, halo_two]
+            operands += [small_here, small_other, *upper[:3]]
+            for group in sorted({group for group, _ in pending}):
+                made = local[group]
+                operands += [*made[:3], made[3], made[5]]
+            for group in range(GROUPS):
+                for out, move in zip(outs[group], moved[group]):
+                    operands += [out, move]
+            results = pl.pallas_call(
                 functools.partial(
-                    absorb_kernel,
+                    tail_kernel,
                     level,
                     32 + 16 * (near + 1 + level),
-                    group,
+                    GROUPS,
                     heads,
+                    count,
+                    tuple(pending),
+                    near,
                     arrivals,
-                    len(outs[group]),
                 ),
-                out_shape=[moved_shape, moved_shape],
-                compiler_params=params(12),
-                cost_estimate=cost(800_000_000),
-                name="absorb",
-            )(
-                *arrived[group],
-                *transit_arrived,
-                small,
-                small_other,
-                *outs[group],
-                *moved[group],
-            )
-            outs[group], moved[group] = [out], [move]
+                out_shape=[moved_shape] * (2 * GROUPS),
+                scratch_shapes=[pltpu.VMEM((8 + CHUNK, count * 128), F32)] * 2
+                + [pltpu.VMEM((count, 2 * CHUNK, 128), F32)] * (2 * len(pending)),
+                compiler_params=params(24),
+                cost_estimate=cost(1_000_000),
+                name="tail",
+            )(*operands)
+            pending.clear()
+            for group in range(GROUPS):
+                outs[group], moved[group] = [results[2 * group]], [results[2 * group + 1]]
+        else:
+            for group in range(GROUPS):
+                out, move = pl.pallas_call(
+                    functools.partial(
+                        absorb_kernel,
+                        level,
+                        32 + 16 * (near + 1 + level),
+                        group,
+                        heads,
+                        arrivals,
+                        len(passing[group]),
+                        len(outs[group]),
+                    ),
+                    out_shape=[moved_shape, moved_shape],
+                    compiler_params=params(12),
+                    cost_estimate=cost(800_000_000),
+                    name="absorb",
+                )(
+                    *arrived[group],
+                    *passing[group],
+                    small,
+                    small_other,
+                    *outs[group],
+                    *moved[group],
+                )
+                outs[group], moved[group] = [out], [move]
         arrived = following
+        passing = fanned
+        shifts = [0] * GROUPS
+    while pending:
+        after = ask(after)
 
     level = max(shard_bits - 1, 0)
-    gain = norm_gain.reshape(1, 128)
     stays = []
     comes = []
     for group in range(GROUPS):
@@ -784,6 +1014,7 @@
                 group,
                 heads,
                 len(arrived[group]),
+                len(passing[group]),
                 len(outs[group]),
             ),
             out_shape=[struct((rows, lanes), BF16)] * 2,
@@ -793,6 +1024,7 @@
             name="finish",
         )(
             *arrived[group],
+            *passing[group],
             small,
             small_other,
             gate_half,

time: 52 us -> 44.2 us (0.85)
  the two profiles are of different devices: /device:TPU:17 before, /device:TPU:11 now
where the time goes in v2:
time: 44.2 us; the launch traced here: 43.6 us
  Pallas kernels  22.8 us (52%)
  starting transfers between devices  18.7 us (42%)
  waiting for transfers between devices  1.8 us (4%)
    ppermute x7, starting transfers between devices, fan(): results.append(lax.ppermute(value, 'seq', route))  9.78 us
    pallas_call x2, Pallas kernels, per_device(): pl.pallas_call(functools.partial(lower_kernel, group, heads), out_shape=h...  7.34 us
    pallas_call x1, Pallas kernels, per_device(): pl.pallas_call(functools.partial(tail_kernel, level, 32 + 16 * (near + 1...  6.66 us
    pallas_call x1, Pallas kernels, per_device(): pl.pallas_call(upper_kernel, out_shape=held(8) + [struct((8, 128, 128))]...  4.75 us
    ppermute x1, starting transfers between devices, per_device(): lax.ppermute(halo, 'seq', [(i, i + 2) for i in range(1, size - 1, 2)])  3.2 us
    ppermute x1, starting transfers between devices, per_device(): lax.ppermute(halo, 'seq', [(i, i + 1) for i in range(1, size - 1, 2)])  3.1 us
    pallas_call x1, Pallas kernels, per_device(): pl.pallas_call(prepare_kernel, in_specs=[pl.BlockSpec(memory_space=pltpu....  1.53 us
    ppermute x2, waiting for transfers between devices, per_device(): comes.append(lax.ppermute(leave, 'seq', cores))  1.28 us
  transfers between devices with their start and end apart: 16, of which 3 were waited for; matrix products, arithmetic and copies ran while one was open for 0% of the time, Pallas kernels for 42%

profile of v2, /device:TPU:11, one launch (start us, length us, event | category | flops | bytes accessed | tf_op | source)
XLA Modules:
  0.0 43.6 jit_solution(41984806042636267)
XLA Ops:
  0.0 0.7 %collective-permute-start = (bf16[128,2048]{1,0:T(8,128)(2,1)}, bf16[128,2048]{1,0:T(8,128)(2,1)S(1)}, u32[]{:S(2)}, u32[]{:S(2)}) collective-permute-start(bf16[128,2048]{1,0:T(8,128)(2,1)} %key.1), channel_id=1, source_target_pairs={{0,1},{1,0},{2,3},{3,2},{4,5},{5,4},{6,7},{7,6},{8,9},{9,8},{10,11... | collective-permute-start | bytes 1572872 | tf_op jit(solution)/shard_map/ppermute | solution.py:736
  0.7 1.5 %prepare.1 = (bf16[128,1024]{1,0:T(8,128)(2,1)S(1)}, bf16[128,1024]{1,0:T(8,128)(2,1)S(1)}, bf16[128,1024]{1,0:T(8,128)(2,1)S(1)}, bf16[128,1024]{1,0:T(8,128)(2...) custom-call(bf16[128,2048]{1,0:T(8,128)(2,1)} %query.1, ...), custom_call_target="tpu_custom_call" | custom-call | tf_op jit(solution)/shard_map/prepare/pallas_call | solution.py:751
  2.2 0.6 %collective-permute-start.2 = (f32[208,128]{1,0:T(8,128)S(1)}, f32[208,128]{1,0:T(8,128)S(1)}, u32[]{:S(2)}, u32[]{:S(2)}) collective-permute-start(f32[208,128]{1,0:T(8,128)S(1)} %get-tuple-element.79.small_own.refs_7_.refs_3_), channel_id=1, source_target_pairs={{0,1},{1,0},{2,3},{3,2},{4,5},{5,4},{6,7},{7,6},{8,9},{9,8},{10,11... | collective-permute-start | bytes 319496 | tf_op jit(solution)/shard_map/ppermute | solution.py:778
  2.8 3.1 %collective-permute-start.3 = (bf16[16,2048]{1,0:T(8,128)(2,1)S(1)}, bf16[16,2048]{1,0:T(8,128)(2,1)S(1)}, u32[]{:S(2)}, u32[]{:S(2)}) collective-permute-start(bf16[16,2048]{1,0:T(8,128)(2,1)S(1)} %get-tuple-element.59), channel_id=1, source_target_pairs={{1,2},{3,4},{5,6},{9,10},{11,12},{13,14},{17,18},{19,20},{21,22},{... | collective-permute-start | bytes 196616 | tf_op jit(solution)/shard_map/ppermute | solution.py:779
  5.9 3.2 %collective-permute-start.4 = (bf16[16,2048]{1,0:T(8,128)(2,1)S(1)}, bf16[16,2048]{1,0:T(8,128)(2,1)S(1)}, u32[]{:S(2)}, u32[]{:S(2)}) collective-permute-start(bf16[16,2048]{1,0:T(8,128)(2,1)S(1)} %get-tuple-element.59), channel_id=1, source_target_pairs={{1,3},{3,5},{5,7},{9,11},{11,13},{13,15},{17,19},{19,21},{21,23},{... | collective-permute-start | bytes 196616 | tf_op jit(solution)/shard_map/ppermute | solution.py:780
  9.1 4.8 %upper.1 = (bf16[8,2,128,128]{3,2,1,0:T(8,128)(2,1)S(1)}, bf16[8,2,128,128]{3,2,1,0:T(8,128)(2,1)S(1)}, bf16[8,2,128,256]{3,2,1,0:T(8,128)(2,1)S(1)}, f32[8,128,128]{2,1,0:T(8,128)S(1)}, f32[8,128,128]{2,1,0:T(8,128)S(1)}) custom-call(bf16[128,1024]{1,0:T(8,128)(2,1)S(1)} %get-tuple-element.53.key_own, bf16[128,2048]{1,0:T(8,128)(2,1)S(1)} %collective-permute-done.key_other, ...), custom_call_target="tpu_custom_call" | custom-call | flops 4000000000 | bytes 1000000 | tf_op jit(solution)/shard_map/upper/pallas_call | solution.py:803
  13.9 3.7 %lower.2 = (bf16[4,2,128,128]{3,2,1,0:T(8,128)(2,1)S(1)}, bf16[4,2,128,128]{3,2,1,0:T(8,128)(2,1)S(1)}, bf16[4,2,128,256]{3,2,1,0:T(8,128)(2,1)S(1)}, f32[4,128,...) custom-call(bf16[128,1024]{1,0:T(8,128)(2,1)S(1)} %get-tuple-element, ...), custom_call_target="tpu_custom_call" | custom-call | flops 2500000000 | bytes 1000000 | tf_op jit(solution)/shard_map/lower/pallas_call | solution.py:825
  17.6 1.4 %collective-permute-start.5 = (bf16[528,128]{1,0:T(8,128)(2,1)S(1)}, bf16[528,128]{1,0:T(8,128)(2,1)S(1)}, u32[]{:S(2)}, u32[]{:S(2)}) collective-permute-start(bf16[528,128]{1,0:T(8,128)(2,1)S(1)} %get-tuple-element.62), channel_id=1, source_target_pairs={{0,2},{1,3},{4,6},{5,7},{8,10},{9,11},{12,14},{13,15},{16,18},{17,... | collective-permute-start | bytes 405512 | tf_op jit(solution)/shard_map/ppermute | solution.py:791
  19.1 3.7 %lower.3 = (bf16[4,2,128,128]{3,2,1,0:T(8,128)(2,1)S(1)}, bf16[4,2,128,128]{3,2,1,0:T(8,128)(2,1)S(1)}, bf16[4,2,128,256]{3,2,1,0:T(8,128)(2,1)S(1)}, f32[4,128,...) custom-call(bf16[128,1024]{1,0:T(8,128)(2,1)S(1)} %get-tuple-element, ...), custom_call_target="tpu_custom_call" | custom-call | flops 2500000000 | bytes 1000000 | tf_op jit(solution)/shard_map/lower/pallas_call | solution.py:825
  22.7 1.3 %collective-permute-start.11 = (bf16[528,128]{1,0:T(8,128)(2,1)S(1)}, bf16[528,128]{1,0:T(8,128)(2,1)S(1)}, u32[]{:S(2)}, u32[]{:S(2)}) collective-permute-start(bf16[528,128]{1,0:T(8,128)(2,1)S(1)} %get-tuple-element.69), channel_id=1, source_target_pairs={{0,2},{1,3},{4,6},{5,7},{8,10},{9,11},{12,14},{13,15},{16,18},{17,... | collective-permute-start | bytes 405512 | tf_op jit(solution)/shard_map/ppermute | solution.py:791
  24.1 0.5 %collective-permute-start.10 = (bf16[128,2048]{1,0:T(8,128)(2,1)S(1)}, bf16[128,2048]{1,0:T(8,128)(2,1)S(1)}, u32[]{:S(2)}, u32[]{:S(2)}) collective-permute-start(bf16[128,2048]{1,0:T(8,128)(2,1)S(1)} %copy-done.1), channel_id=1, source_target_pairs={{0,1},{1,0},{2,3},{3,2},{4,5},{5,4},{6,7},{7,6},{8,9},{9,8},{10,11... | collective-permute-start | bytes 1572872 | tf_op jit(solution)/shard_map/ppermute | solution.py:852
  24.6 0.4 join.2
  25.0 1.3 %collective-permute-start.6 = (bf16[528,128]{1,0:T(8,128)(2,1)S(1)}, bf16[528,128]{1,0:T(8,128)(2,1)S(1)}, u32[]{:S(2)}, u32[]{:S(2)}) collective-permute-start(bf16[528,128]{1,0:T(8,128)(2,1)S(1)} %join.2), channel_id=1, source_target_pairs={{2,6},{3,7},{10,14},{11,15},{18,22},{19,23},{26,30},{27,31}} | collective-permute-start | bytes 405512 | tf_op jit(solution)/shard_map/ppermute | solution.py:791
  26.3 1.5 %collective-permute-start.7 = (bf16[528,128]{1,0:T(8,128)(2,1)S(1)}, bf16[528,128]{1,0:T(8,128)(2,1)S(1)}, u32[]{:S(2)}, u32[]{:S(2)}) collective-permute-start(bf16[528,128]{1,0:T(8,128)(2,1)S(1)} %join.2), channel_id=1, source_target_pairs={{2,4},{3,5},{10,12},{11,13},{18,20},{19,21},{26,28},{27,29}} | collective-permute-start | bytes 405512 | tf_op jit(solution)/shard_map/ppermute | solution.py:791
  28.0 0.5 %collective-permute-done.11.refs_0_.refs_1_ = bf16[528,128]{1,0:T(8,128)(2,1)S(1)} collective-permute-done((bf16[528,128]{1,0:T(8,128)(2,1)S(1)}, bf16[528,128]{1,0:T(8,128)(2,1)S(1)}, u32[]{:S(2)}, u32[]{:S(2)}) %collective-permute-start.11) | collective-permute-done | bytes 135200 | tf_op jit(solution)/shard_map/ppermute | solution.py:791
  28.5 0.7 %collective-permute-start.8 = (bf16[1040,128]{1,0:T(8,128)(2,1)S(1)}, bf16[1040,128]{1,0:T(8,128)(2,1)S(1)}, u32[]{:S(2)}, u32[]{:S(2)}) collective-permute-start(bf16[1040,128]{1,0:T(8,128)(2,1)S(1)} %code.1), channel_id=1, source_target_pairs={{4,6},{5,7},{12,14},{13,15},{20,22},{21,23},{28,30},{29,31}} | collective-permute-start | bytes 798728 | tf_op jit(solution)/shard_map/ppermute | solution.py:791
  29.2 0.4 join.3
  29.6 2.0 %collective-permute-start.12 = (bf16[528,128]{1,0:T(8,128)(2,1)S(1)}, bf16[528,128]{1,0:T(8,128)(2,1)S(1)}, u32[]{:S(2)}, u32[]{:S(2)}) collective-permute-start(bf16[528,128]{1,0:T(8,128)(2,1)S(1)} %join.3), channel_id=1, source_target_pairs={{2,6},{3,7},{10,14},{11,15},{18,22},{19,23},{26,30},{27,31}} | collective-permute-start | bytes 405512 | tf_op jit(solution)/shard_map/ppermute | solution.py:791
  31.7 1.6 %collective-permute-start.13 = (bf16[528,128]{1,0:T(8,128)(2,1)S(1)}, bf16[528,128]{1,0:T(8,128)(2,1)S(1)}, u32[]{:S(2)}, u32[]{:S(2)}) collective-permute-start(bf16[528,128]{1,0:T(8,128)(2,1)S(1)} %join.3), channel_id=1, source_target_pairs={{2,4},{3,5},{10,12},{11,13},{18,20},{19,21},{26,28},{27,29}} | collective-permute-start | bytes 405512 | tf_op jit(solution)/shard_map/ppermute | solution.py:791
  33.2 6.7 %tail.1 = (f32[4,256,128]{2,1,0:T(8,128)S(1)}, f32[4,256,128]{2,1,0:T(8,128)S(1)}, f32[4,256,128]{2,1,0:T(8,128)S(1)}, f32[4,256,128]{2,1,0:T(8,128)S(1)}) custom-call(bf16[528,128]{1,0:T(8,128)(2,1)S(1)} %collective-permute-done.5.refs_0_, bf16[528,128]{1,0:T(8,128)(2,1)S(1)} %collective-permute-done.11.refs_0_.refs_1_, ...), custom_call_target="tpu_custom_call" | custom-call | flops 1000000 | bytes 1000000 | tf_op jit(solution)/shard_map/tail/pallas_call | solution.py:951
  40.3 0.7 %collective-permute-start.14 = (bf16[128,512]{1,0:T(8,128)(2,1)S(1)}, bf16[128,512]{1,0:T(8,128)(2,1)S(1)}, u32[]{:S(2)}, u32[]{:S(2)}) collective-permute-start(bf16[128,512]{1,0:T(8,128)(2,1)S(1)} %get-tuple-element.99), channel_id=1, source_target_pairs={{0,1},{1,0},{2,3},{3,2},{4,5},{5,4},{6,7},{7,6},{8,9},{9,8},{10,11... | collective-permute-start | bytes 393224 | tf_op jit(solution)/shard_map/ppermute | solution.py:1037
  41.4 0.5 %collective-permute-done.14.refs_2_ = bf16[128,512]{1,0:T(8,128)(2,1)S(1)} collective-permute-done((bf16[128,512]{1,0:T(8,128)(2,1)S(1)}, bf16[128,512]{1,0:T(8,128)(2,1)S(1)}, u32[]{:S(2)}, u32[]{:S(2)}) %collective-permute-start.14) | collective-permute-done | bytes 131104 | tf_op jit(solution)/shard_map/ppermute | solution.py:1037
  42.0 0.8 %collective-permute-done.15.refs_3_ = bf16[128,512]{1,0:T(8,128)(2,1)S(1)} collective-permute-done((bf16[128,512]{1,0:T(8,128)(2,1)S(1)}, bf16[128,512]{1,0:T(8,128)(2,1)S(1)}, u32[]{:S(2)}, u32[]{:S(2)}) %collective-permute-start.15) | collective-permute-done | bytes 131104 | tf_op jit(solution)/shard_map/ppermute | solution.py:1037
  42.7 0.8 %swap.1 = bf16[128,2048]{1,0:T(8,128)(2,1)} custom-call(bf16[128,512]{1,0:T(8,128)(2,1)S(1)} %get-tuple-element.95.refs_0_, bf16[128,512]{1,0:T(8,128)(2,1)S(1)} %get-tuple-element.98.refs_1_, bf16[128,512]{1,0:T(8,128)(2,1)S(1)} %collective-permute-done.14.refs_2_, bf16[128,512]{1,0:T(8,128)(2,1)S(1)} %collective-permute-done.15.refs_3_), custom_call_target="tpu_custom_call" | custom-call | tf_op jit(solution)/shard_map/swap/pallas_call | solution.py:1038
  (23 shorter events, 1.1 us)
Async XLA Ops:
  0.0 9.1 %collective-permute-start = (bf16[128,2048]{1,0:T(8,128)(2,1)}, bf16[128,2048]{1,0:T(8,128)(2,1)S(1)}, u32[]{:S(2)}, u32[]{:S(2)}) collective-permute-start(bf16[128,2048]{1,0:T(8,128)(2,1)} %key.1), channel_id=1, source_target_pairs={{0,1},{1,0},{2,3},{3,2},{4,5},{5,4},{6,7},{7,6},{8,9},{9,8},{10,11... | collective-permute-start | bytes 1572872 | tf_op jit(solution)/shard_map/ppermute | solution.py:736
  0.7 8.5 %collective-permute-start.1 = (bf16[128,2048]{1,0:T(8,128)(2,1)}, bf16[128,2048]{1,0:T(8,128)(2,1)S(1)}, u32[]{:S(2)}, u32[]{:S(2)}) collective-permute-start(bf16[128,2048]{1,0:T(8,128)(2,1)} %value.1), channel_id=1, source_target_pairs={{0,1},{1,0},{2,3},{3,2},{4,5},{5,4},{6,7},{7,6},{8,9},{9,8},{10,11... | collective-permute-start | bytes 1572872 | tf_op jit(solution)/shard_map/ppermute | solution.py:737
  2.2 6.9 %collective-permute-start.2 = (f32[208,128]{1,0:T(8,128)S(1)}, f32[208,128]{1,0:T(8,128)S(1)}, u32[]{:S(2)}, u32[]{:S(2)}) collective-permute-start(f32[208,128]{1,0:T(8,128)S(1)} %get-tuple-element.79.small_own.refs_7_.refs_3_), channel_id=1, source_target_pairs={{0,1},{1,0},{2,3},{3,2},{4,5},{5,4},{6,7},{7,6},{8,9},{9,8},{10,11... | collective-permute-start | bytes 319496 | tf_op jit(solution)/shard_map/ppermute | solution.py:778
  2.8 11.1 %collective-permute-start.3 = (bf16[16,2048]{1,0:T(8,128)(2,1)S(1)}, bf16[16,2048]{1,0:T(8,128)(2,1)S(1)}, u32[]{:S(2)}, u32[]{:S(2)}) collective-permute-start(bf16[16,2048]{1,0:T(8,128)(2,1)S(1)} %get-tuple-element.59), channel_id=1, source_target_pairs={{1,2},{3,4},{5,6},{9,10},{11,12},{13,14},{17,18},{19,20},{21,22},{... | collective-permute-start | bytes 196616 | tf_op jit(solution)/shard_map/ppermute | solution.py:779
  5.9 8.0 %collective-permute-start.4 = (bf16[16,2048]{1,0:T(8,128)(2,1)S(1)}, bf16[16,2048]{1,0:T(8,128)(2,1)S(1)}, u32[]{:S(2)}, u32[]{:S(2)}) collective-permute-start(bf16[16,2048]{1,0:T(8,128)(2,1)S(1)} %get-tuple-element.59), channel_id=1, source_target_pairs={{1,3},{3,5},{5,7},{9,11},{11,13},{13,15},{17,19},{19,21},{21,23},{... | collective-permute-start | bytes 196616 | tf_op jit(solution)/shard_map/ppermute | solution.py:780
  17.6 6.4 %copy-start = (bf16[128,2048]{1,0:T(8,128)(2,1)S(1)}, bf16[128,2048]{1,0:T(8,128)(2,1)}, u32[]{:S(2)}) copy-start(bf16[128,2048]{1,0:T(8,128)(2,1)} %query.1) | copy-start | bytes 1572868
  17.6 6.5 %copy-start.1 = (bf16[128,2048]{1,0:T(8,128)(2,1)S(1)}, bf16[128,2048]{1,0:T(8,128)(2,1)}, u32[]{:S(2)}) copy-start(bf16[128,2048]{1,0:T(8,128)(2,1)} %gate.1) | copy-start | bytes 1572868
  17.6 7.0 %collective-permute-start.5 = (bf16[528,128]{1,0:T(8,128)(2,1)S(1)}, bf16[528,128]{1,0:T(8,128)(2,1)S(1)}, u32[]{:S(2)}, u32[]{:S(2)}) collective-permute-start(bf16[528,128]{1,0:T(8,128)(2,1)S(1)} %get-tuple-element.62), channel_id=1, source_target_pairs={{0,2},{1,3},{4,6},{5,7},{8,10},{9,11},{12,14},{13,15},{16,18},{17,... | collective-permute-start | bytes 405512 | tf_op jit(solution)/shard_map/ppermute | solution.py:791
  22.7 5.8 %collective-permute-start.11 = (bf16[528,128]{1,0:T(8,128)(2,1)S(1)}, bf16[528,128]{1,0:T(8,128)(2,1)S(1)}, u32[]{:S(2)}, u32[]{:S(2)}) collective-permute-start(bf16[528,128]{1,0:T(8,128)(2,1)S(1)} %get-tuple-element.69), channel_id=1, source_target_pairs={{0,2},{1,3},{4,6},{5,7},{8,10},{9,11},{12,14},{13,15},{16,18},{17,... | collective-permute-start | bytes 405512 | tf_op jit(solution)/shard_map/ppermute | solution.py:791
  24.1 5.5 %collective-permute-start.9 = (bf16[128,2048]{1,0:T(8,128)(2,1)S(1)}, bf16[128,2048]{1,0:T(8,128)(2,1)S(1)}, u32[]{:S(2)}, u32[]{:S(2)}) collective-permute-start(bf16[128,2048]{1,0:T(8,128)(2,1)S(1)} %copy-done), channel_id=1, source_target_pairs={{0,1},{1,0},{2,3},{3,2},{4,5},{5,4},{6,7},{7,6},{8,9},{9,8},{10,11... | collective-permute-start | bytes 1572872 | tf_op jit(solution)/shard_map/ppermute | solution.py:851
  24.1 7.5 %collective-permute-start.10 = (bf16[128,2048]{1,0:T(8,128)(2,1)S(1)}, bf16[128,2048]{1,0:T(8,128)(2,1)S(1)}, u32[]{:S(2)}, u32[]{:S(2)}) collective-permute-start(bf16[128,2048]{1,0:T(8,128)(2,1)S(1)} %copy-done.1), channel_id=1, source_target_pairs={{0,1},{1,0},{2,3},{3,2},{4,5},{5,4},{6,7},{7,6},{8,9},{9,8},{10,11... | collective-permute-start | bytes 1572872 | tf_op jit(solution)/shard_map/ppermute | solution.py:852
  25.0 14.9 %collective-permute-start.6 = (bf16[528,128]{1,0:T(8,128)(2,1)S(1)}, bf16[528,128]{1,0:T(8,128)(2,1)S(1)}, u32[]{:S(2)}, u32[]{:S(2)}) collective-permute-start(bf16[528,128]{1,0:T(8,128)(2,1)S(1)} %join.2), channel_id=1, source_target_pairs={{2,6},{3,7},{10,14},{11,15},{18,22},{19,23},{26,30},{27,31}} | collective-permute-start | bytes 405512 | tf_op jit(solution)/shard_map/ppermute | solution.py:791
  26.3 13.6 %collective-permute-start.7 = (bf16[528,128]{1,0:T(8,128)(2,1)S(1)}, bf16[528,128]{1,0:T(8,128)(2,1)S(1)}, u32[]{:S(2)}, u32[]{:S(2)}) collective-permute-start(bf16[528,128]{1,0:T(8,128)(2,1)S(1)} %join.2), channel_id=1, source_target_pairs={{2,4},{3,5},{10,12},{11,13},{18,20},{19,21},{26,28},{27,29}} | collective-permute-start | bytes 405512 | tf_op jit(solution)/shard_map/ppermute | solution.py:791
  28.5 11.4 %collective-permute-start.8 = (bf16[1040,128]{1,0:T(8,128)(2,1)S(1)}, bf16[1040,128]{1,0:T(8,128)(2,1)S(1)}, u32[]{:S(2)}, u32[]{:S(2)}) collective-permute-start(bf16[1040,128]{1,0:T(8,128)(2,1)S(1)} %code.1), channel_id=1, source_target_pairs={{4,6},{5,7},{12,14},{13,15},{20,22},{21,23},{28,30},{29,31}} | collective-permute-start | bytes 798728 | tf_op jit(solution)/shard_map/ppermute | solution.py:791
  29.6 11.4 %collective-permute-start.12 = (bf16[528,128]{1,0:T(8,128)(2,1)S(1)}, bf16[528,128]{1,0:T(8,128)(2,1)S(1)}, u32[]{:S(2)}, u32[]{:S(2)}) collective-permute-start(bf16[528,128]{1,0:T(8,128)(2,1)S(1)} %join.3), channel_id=1, source_target_pairs={{2,6},{3,7},{10,14},{11,15},{18,22},{19,23},{26,30},{27,31}} | collective-permute-start | bytes 405512 | tf_op jit(solution)/shard_map/ppermute | solution.py:791
  31.7 9.3 %collective-permute-start.13 = (bf16[528,128]{1,0:T(8,128)(2,1)S(1)}, bf16[528,128]{1,0:T(8,128)(2,1)S(1)}, u32[]{:S(2)}, u32[]{:S(2)}) collective-permute-start(bf16[528,128]{1,0:T(8,128)(2,1)S(1)} %join.3), channel_id=1, source_target_pairs={{2,4},{3,5},{10,12},{11,13},{18,20},{19,21},{26,28},{27,29}} | collective-permute-start | bytes 405512 | tf_op jit(solution)/shard_map/ppermute | solution.py:791
  40.3 1.7 %collective-permute-start.14 = (bf16[128,512]{1,0:T(8,128)(2,1)S(1)}, bf16[128,512]{1,0:T(8,128)(2,1)S(1)}, u32[]{:S(2)}, u32[]{:S(2)}) collective-permute-start(bf16[128,512]{1,0:T(8,128)(2,1)S(1)} %get-tuple-element.99), channel_id=1, source_target_pairs={{0,1},{1,0},{2,3},{3,2},{4,5},{5,4},{6,7},{7,6},{8,9},{9,8},{10,11... | collective-permute-start | bytes 393224 | tf_op jit(solution)/shard_map/ppermute | solution.py:1037
  41.3 1.4 %collective-permute-start.15 = (bf16[128,512]{1,0:T(8,128)(2,1)S(1)}, bf16[128,512]{1,0:T(8,128)(2,1)S(1)}, u32[]{:S(2)}, u32[]{:S(2)}) collective-permute-start(bf16[128,512]{1,0:T(8,128)(2,1)S(1)} %get-tuple-element.100), channel_id=1, source_target_pairs={{0,1},{1,0},{2,3},{3,2},{4,5},{5,4},{6,7},{7,6},{8,9},{9,8},{10,11... | collective-permute-start | bytes 393224 | tf_op jit(solution)/shard_map/ppermute | solution.py:1037

commit v3 on v2

--- a/solution.py
+++ b/solution.py
@@ -30,7 +30,7 @@
 
 def mm(a, b):
     width = b[0].shape[1]
-    if width > 128:
+    if b[0].shape[0] <= 128 and (width > 128 or a[0].shape[0] <= 128):
         both = jnp.concatenate([b[0], b[0]], axis=0)
         return dot(jnp.concatenate(a, axis=1), both) + dot(a[0], b[1])
     out = dot(jnp.concatenate(a, axis=1), wide(b))
@@ -476,7 +476,8 @@
     code_out[head * 128 : head * 128 + 16, :] = pack_rows(scales)
 
 
-def join_kernel(level, arrivals, with_transit, shift, *refs):
+def join_kernel(level, arrivals, with_transit, shift, waits, *refs):
+    refs = refs[waits:]
     state_in = refs[:arrivals]
     refs = refs[arrivals:]
     transit_in = ()
@@ -489,7 +490,13 @@
     _, node = place()
     upper = (node >> level) % 2 == 1
     if not with_transit:
-        upper = upper & ((node >> (level + 1)) % 2 == 0)
+        late = (node >> (level + 1)) % 2 == 1
+        riding = late & jnp.logical_not(upper)
+        upper = upper & jnp.logical_not(late)
+
+        @pl.when(riding)
+        def _():
+            encode_all([transit[head] for head in range(heads)], code_out)
 
     @pl.when(upper)
     def _():
@@ -619,10 +626,10 @@
         )
 
 
-def finish_kernel(level, weight_row, group, heads, arrivals, passed, pieces, *refs):
+def finish_kernel(level, weight_row, group, heads, arrivals, pieces, *refs):
+    refs = refs[min(group, 1) :]
     state_in = refs[:arrivals]
-    transit_in = refs[arrivals : arrivals + passed]
-    refs = refs[arrivals + passed :]
+    refs = refs[arrivals:]
     small_own, small_other, gate_own, gate_other, gain = refs[:5]
     outs_in = refs[5 : 5 + pieces]
     moved_in = refs[5 + pieces : 5 + 2 * pieces]
@@ -631,33 +638,33 @@
     upper = (node >> level) % 2 == 1
     each = heads // pieces
 
-    def add(through):
-        states = [received(state_in, head) for head in range(heads)]
-        if through:
-            shift = group * heads if level == 1 else 0
-            states = [
-                mm(split(received(transit_in, shift + head)), split(states[head]))
-                for head in range(heads)
-            ]
+    def add(states, transits):
         for head in range(heads):
+            found = split(received(states, head))
+            if transits is not None:
+                found = split(mm(split(received(transits, head)), found))
             row = weight_row + 8 * core + heads * group + head
             weight = level_weight(small_own, small_other, row, core)
-            extra = mm(split(moved_in[head // each][head % each]), split(states[head]))
+            extra = mm(split(moved_in[head // each][head % each]), found)
             total[head] = outs_in[head // each][head % each] + weight * extra
 
-    through = jnp.bool_(False)
-    if passed:
+    if level:
         through = (node >> (level - 1)) % 2 == 1
-
-    @pl.when(upper & jnp.logical_not(through))
-    def _():
-        add(False)
-
-    if passed:
+        far, close = state_in[: arrivals // 2], state_in[arrivals // 2 :]
 
         @pl.when(upper & through)
         def _():
-            add(True)
+            add(far, close)
+
+        @pl.when(upper & jnp.logical_not(through))
+        def _():
+            add(close, None)
+
+    else:
+
+        @pl.when(upper)
+        def _():
+            add(state_in, None)
 
     @pl.when(jnp.logical_not(upper))
     def _():
@@ -779,14 +786,17 @@
     halo_one = lax.ppermute(halo, "seq", [(i, i + 1) for i in range(1, size - 1, 2)])
     halo_two = lax.ppermute(halo, "seq", [(i, i + 2) for i in range(1, size - 1, 2)])
 
-    def fan(value, level, keep):
+    def fan(value, level, riders=False):
         span = 1 << level
         results = []
         for offset in reversed(range(span)):
             route = []
             for low in range(0, nodes, 2 * span):
-                source, target = low + span - 1, low + span + offset
-                if keep(target):
+                hops = [(low + span - 1, low + span + offset)]
+                if riders and 2 * offset < span:
+                    middle = low + span + span // 2
+                    hops.append((middle - 1, middle + offset))
+                for source, target in hops:
                     route += [(2 * source + c, 2 * target + c) for c in range(2)]
             results.append(lax.ppermute(value, "seq", route))
         return results
@@ -846,11 +856,13 @@
         )
         local.append(made)
         after = made[7]
-        arrived.append(fan(made[7], 0, lambda target: True) if shard_bits else [])
-    after, query_late, gate_late = lax.optimization_barrier((after, query_rows, output_gate))
-    query_other = lax.ppermute(query_late, "seq", cores)
-    gate_other = lax.ppermute(gate_late, "seq", cores)
-    after, query_other, gate_other = lax.optimization_barrier((after, query_other, gate_other))
+        arrived.append(fan(made[7], 0) if shard_bits else [])
+
+    def swap_rows(after):
+        _, query_late, gate_late = lax.optimization_barrier((after, query_rows, output_gate))
+        return lax.ppermute(query_late, "seq", cores), lax.ppermute(gate_late, "seq", cores)
+
+    query_other, gate_other = swap_rows(local[0][7])
     state = [x[4] for x in local]
     transit = [x[6] for x in local]
     count = heads // PIECES
@@ -890,28 +902,25 @@
     moved_shape = struct((heads, 2 * CHUNK, 128))
     transit_codes = [None] * GROUPS
 
-    def send_transit(after):
-        after, first_transit = lax.optimization_barrier((after, transit[0]))
+    def send_transit():
         return pl.pallas_call(
             code_kernel,
             out_shape=struct((8 * 128 + 16, 128), BF16),
             compiler_params=params(8),
-            cost_estimate=cost(300_000_000),
+            cost_estimate=cost(1_000_000),
             name="code",
-        )(first_transit, *transit[1:])
+        )(*transit)
 
     shifts = [heads * group for group in range(GROUPS)]
     passing = [[]] * GROUPS
     for level in range(shard_bits - 1):
         keeps = level < shard_bits - 2
 
-        def wanted(target):
-            return keeps or target >> (level + 1) > 0
-
-        if level:
-            fanned = [fan(x, level, wanted) for x in transit_codes]
+        fanned = [[]] * GROUPS
+        if keeps and level == 0:
+            fanned = [fan(send_transit(), level)] * GROUPS
         elif keeps:
-            fanned = [fan(send_transit(after), level, wanted)] * GROUPS
+            fanned = [fan(x, level) for x in transit_codes]
         following = []
         for group in range(GROUPS):
             shapes = [code_shape]
@@ -919,21 +928,22 @@
             if keeps:
                 shapes += [struct(square), struct(square), code_shape]
                 operands += fanned[group]
-            after, state_here = lax.optimization_barrier((after, state[group]))
+            waits = [after]
+            if level == 0 and group == GROUPS - 1:
+                waits += [query_other, gate_other]
             joined = pl.pallas_call(
                 functools.partial(
-                    join_kernel, level, len(arrived[group]), keeps, shifts[group]
+                    join_kernel, level, len(arrived[group]), keeps, shifts[group], len(waits)
                 ),
+                in_specs=[pl.BlockSpec(memory_space=pl.ANY)] * len(waits)
+                + [pl.BlockSpec(memory_space=pltpu.VMEM)] * (len(operands) + 2),
                 out_shape=shapes,
                 compiler_params=params(12),
                 cost_estimate=cost(4_000_000_000),
                 name="join",
-            )(*operands, state_here, transit[group])
+            )(*waits, *operands, state[group], transit[group])
             after = joined[0]
-            if level == 0 and group == 0:
-                if not keeps:
-                    fanned = [fan(send_transit(after), level, wanted)] * GROUPS
-            following.append(fan(joined[0], level + 1, lambda target: True))
+            following.append(fan(joined[0], level + 1, not keeps))
             if keeps:
                 state[group], transit[group], transit_codes[group] = joined[1:]
         arrivals = len(arrived[0])
@@ -1006,6 +1016,20 @@
     stays = []
     comes = []
     for group in range(GROUPS):
+        operands = [
+            *arrived[group],
+            small,
+            small_other,
+            gate_half,
+            gate_other,
+            gain,
+            *outs[group],
+            *moved[group],
+        ]
+        specs = [pl.BlockSpec(memory_space=pltpu.VMEM)] * len(operands)
+        if group:
+            operands = [stays[-1]] + operands
+            specs = [pl.BlockSpec(memory_space=pl.ANY)] + specs
         stay, leave = pl.pallas_call(
             functools.partial(
                 finish_kernel,
@@ -1014,25 +1038,15 @@
                 group,
                 heads,
                 len(arrived[group]),
-                len(passing[group]),
                 len(outs[group]),
             ),
+            in_specs=specs,
             out_shape=[struct((rows, lanes), BF16)] * 2,
             scratch_shapes=[pltpu.VMEM((heads, 2 * CHUNK, 128), F32)],
             compiler_params=params(12),
-            cost_estimate=cost(600_000_000),
+            cost_estimate=cost(1_000_000),
             name="finish",
-        )(
-            *arrived[group],
-            *passing[group],
-            small,
-            small_other,
-            gate_half,
-            gate_other,
-            gain,
-            *outs[group],
-            *moved[group],
-        )
+        )(*operands)
         stays.append(stay)
         comes.append(lax.ppermute(leave, "seq", cores))
     return pl.pallas_call(

time: 44.2 us -> 42.4 us (0.959); the launches traced: 43.6 us -> 42.2 us
  Pallas kernels: 22.8 us -> 21.6 us
  starting transfers between devices: 18.7 us -> 18.2 us
    ppermute x1, starting transfers between devices: 3.1 us -> 1.29 us  [per_device(): lax.ppermute(halo, 'seq', [(i, i + 1) for i in range(1, size - 1, 2)])]
    ppermute x2, starting transfers between devices: 0.81 us -> 1.57 us  [per_device(): comes.append(lax.ppermute(leave, 'seq', cores))]
    ppermute x7 -> x6, starting transfers between devices: 9.78 us -> 10.3 us  [fan(): results.append(lax.ppermute(value, 'seq', route))]
    pallas_call x2, Pallas kernels: 7.34 us -> 6.86 us  [per_device(): pl.pallas_call(functools.partial(lower_kernel, group, heads), out_shape=h...]
    ppermute x7 -> x6, waiting for transfers between devices: 0.5 us -> 0.89 us  [fan(): results.append(lax.ppermute(value, 'seq', route))]
  transfers between devices with their start and end apart: 16 -> 15, of which waited for: 3 -> 3; matrix products, arithmetic and copies ran while one was open for 0% -> 0% of each run, Pallas kernels for 42% -> 41%
where the time goes in v3:
time: 42.4 us; the launch traced here: 42.2 us
  Pallas kernels  21.6 us (51%)
  starting transfers between devices  18.2 us (43%)
  waiting for transfers between devices  2.19 us (5%)
    ppermute x6, starting transfers between devices, fan(): results.append(lax.ppermute(value, 'seq', route))  10.3 us
    pallas_call x2, Pallas kernels, per_device(): pl.pallas_call(functools.partial(lower_kernel, group, heads), out_shape=h...  6.86 us
    pallas_call x1, Pallas kernels, per_device(): pl.pallas_call(functools.partial(tail_kernel, level, 32 + 16 * (near + 1...  6.54 us
    pallas_call x1, Pallas kernels, per_device(): pl.pallas_call(upper_kernel, out_shape=held(8) + [struct((8, 128, 128))]...  4.34 us
    ppermute x1, starting transfers between devices, per_device(): lax.ppermute(halo, 'seq', [(i, i + 2) for i in range(1, size - 1, 2)])  3.19 us
    ppermute x2, starting transfers between devices, per_device(): comes.append(lax.ppermute(leave, 'seq', cores))  1.57 us
    pallas_call x1, Pallas kernels, per_device(): pl.pallas_call(prepare_kernel, in_specs=[pl.BlockSpec(memory_space=pltpu....  1.53 us
    ppermute x1, starting transfers between devices, per_device(): lax.ppermute(halo, 'seq', [(i, i + 1) for i in range(1, size - 1, 2)])  1.29 us
  transfers between devices with their start and end apart: 15, of which 3 were waited for; matrix products, arithmetic and copies ran while one was open for 0% of the time, Pallas kernels for 41%

profile of v3, /device:TPU:11, one launch (start us, length us, event | category | flops | bytes accessed | tf_op | source)
XLA Modules:
  0.0 42.2 jit_solution(4690956694536692776)
XLA Ops:
  0.0 0.7 %collective-permute-start = (bf16[128,2048]{1,0:T(8,128)(2,1)}, bf16[128,2048]{1,0:T(8,128)(2,1)S(1)}, u32[]{:S(2)}, u32[]{:S(2)}) collective-permute-start(bf16[128,2048]{1,0:T(8,128)(2,1)} %key.1), channel_id=1, source_target_pairs={{0,1},{1,0},{2,3},{3,2},{4,5},{5,4},{6,7},{7,6},{8,9},{9,8},{10,11... | collective-permute-start | bytes 1572872 | tf_op jit(solution)/shard_map/ppermute | solution.py:743
  0.7 1.5 %prepare.1 = (bf16[128,1024]{1,0:T(8,128)(2,1)S(1)}, bf16[128,1024]{1,0:T(8,128)(2,1)S(1)}, bf16[128,1024]{1,0:T(8,128)(2,1)S(1)}, bf16[128,1024]{1,0:T(8,128)(2...) custom-call(bf16[128,2048]{1,0:T(8,128)(2,1)} %query.1, ...), custom_call_target="tpu_custom_call" | custom-call | tf_op jit(solution)/shard_map/prepare/pallas_call | solution.py:758
  2.2 0.6 %collective-permute-start.2 = (f32[208,128]{1,0:T(8,128)S(1)}, f32[208,128]{1,0:T(8,128)S(1)}, u32[]{:S(2)}, u32[]{:S(2)}) collective-permute-start(f32[208,128]{1,0:T(8,128)S(1)} %get-tuple-element.71.small_own.refs_7_.refs_2_.refs_3_), channel_id=1, source_target_pairs={{0,1},{1,0},{2,3},{3,2},{4,5},{5,4},{6,7},{7,6},{8,9},{9,8},{10,11... | collective-permute-start | bytes 319496 | tf_op jit(solution)/shard_map/ppermute | solution.py:785
  2.8 3.2 %collective-permute-start.4 = (bf16[16,2048]{1,0:T(8,128)(2,1)S(1)}, bf16[16,2048]{1,0:T(8,128)(2,1)S(1)}, u32[]{:S(2)}, u32[]{:S(2)}) collective-permute-start(bf16[16,2048]{1,0:T(8,128)(2,1)S(1)} %get-tuple-element.55), channel_id=1, source_target_pairs={{1,3},{3,5},{5,7},{9,11},{11,13},{13,15},{17,19},{19,21},{21,23},{... | collective-permute-start | bytes 196616 | tf_op jit(solution)/shard_map/ppermute | solution.py:787
  6.0 1.3 %collective-permute-start.3 = (bf16[16,2048]{1,0:T(8,128)(2,1)S(1)}, bf16[16,2048]{1,0:T(8,128)(2,1)S(1)}, u32[]{:S(2)}, u32[]{:S(2)}) collective-permute-start(bf16[16,2048]{1,0:T(8,128)(2,1)S(1)} %get-tuple-element.55), channel_id=1, source_target_pairs={{1,2},{3,4},{5,6},{9,10},{11,12},{13,14},{17,18},{19,20},{21,22},{... | collective-permute-start | bytes 196616 | tf_op jit(solution)/shard_map/ppermute | solution.py:786
  7.3 4.3 %upper.1 = (bf16[8,2,128,128]{3,2,1,0:T(8,128)(2,1)S(1)}, bf16[8,2,128,128]{3,2,1,0:T(8,128)(2,1)S(1)}, bf16[8,2,128,256]{3,2,1,0:T(8,128)(2,1)S(1)}, f32[8,128,128]{2,1,0:T(8,128)S(1)}, f32[8,128,128]{2,1,0:T(8,128)S(1)}) custom-call(bf16[128,1024]{1,0:T(8,128)(2,1)S(1)} %get-tuple-element.49.key_own, bf16[128,2048]{1,0:T(8,128)(2,1)S(1)} %collective-permute-done.key_other, ...), custom_call_target="tpu_custom_call" | custom-call | flops 4000000000 | bytes 1000000 | tf_op jit(solution)/shard_map/upper/pallas_call | solution.py:813
  11.7 3.4 %lower.2 = (bf16[4,2,128,128]{3,2,1,0:T(8,128)(2,1)S(1)}, bf16[4,2,128,128]{3,2,1,0:T(8,128)(2,1)S(1)}, bf16[4,2,128,256]{3,2,1,0:T(8,128)(2,1)S(1)}, f32[4,128,...) custom-call(bf16[128,1024]{1,0:T(8,128)(2,1)S(1)} %get-tuple-element, ...), custom_call_target="tpu_custom_call" | custom-call | flops 2500000000 | bytes 1000000 | tf_op jit(solution)/shard_map/lower/pallas_call | solution.py:835
  15.2 1.3 %collective-permute-start.5 = (bf16[528,128]{1,0:T(8,128)(2,1)S(1)}, bf16[528,128]{1,0:T(8,128)(2,1)S(1)}, u32[]{:S(2)}, u32[]{:S(2)}) collective-permute-start(bf16[528,128]{1,0:T(8,128)(2,1)S(1)} %get-tuple-element.58), channel_id=1, source_target_pairs={{0,2},{1,3},{4,6},{5,7},{8,10},{9,11},{12,14},{13,15},{16,18},{17,... | collective-permute-start | bytes 405512 | tf_op jit(solution)/shard_map/ppermute | solution.py:801
  16.6 0.5 %collective-permute-start.10 = (bf16[128,2048]{1,0:T(8,128)(2,1)S(1)}, bf16[128,2048]{1,0:T(8,128)(2,1)S(1)}, u32[]{:S(2)}, u32[]{:S(2)}) collective-permute-start(bf16[128,2048]{1,0:T(8,128)(2,1)S(1)} %copy-done.1), channel_id=1, source_target_pairs={{0,1},{1,0},{2,3},{3,2},{4,5},{5,4},{6,7},{7,6},{8,9},{9,8},{10,11... | collective-permute-start | bytes 1572872 | tf_op jit(solution)/shard_map/ppermute | solution.py:863
  17.1 3.4 %lower.3 = (bf16[4,2,128,128]{3,2,1,0:T(8,128)(2,1)S(1)}, bf16[4,2,128,128]{3,2,1,0:T(8,128)(2,1)S(1)}, bf16[4,2,128,256]{3,2,1,0:T(8,128)(2,1)S(1)}, f32[4,128,...) custom-call(bf16[128,1024]{1,0:T(8,128)(2,1)S(1)} %get-tuple-element, ...), custom_call_target="tpu_custom_call" | custom-call | flops 2500000000 | bytes 1000000 | tf_op jit(solution)/shard_map/lower/pallas_call | solution.py:835
  20.5 1.3 %collective-permute-start.9 = (bf16[528,128]{1,0:T(8,128)(2,1)S(1)}, bf16[528,128]{1,0:T(8,128)(2,1)S(1)}, u32[]{:S(2)}, u32[]{:S(2)}) collective-permute-start(bf16[528,128]{1,0:T(8,128)(2,1)S(1)} %get-tuple-element.60.refs_0_), channel_id=1, source_target_pairs={{0,2},{1,3},{4,6},{5,7},{8,10},{9,11},{12,14},{13,15},{16,18},{17,... | collective-permute-start | bytes 405512 | tf_op jit(solution)/shard_map/ppermute | solution.py:801
  21.8 0.4 join.2.refs_0_
  22.2 3.0 %collective-permute-start.7 = (bf16[528,128]{1,0:T(8,128)(2,1)S(1)}, bf16[528,128]{1,0:T(8,128)(2,1)S(1)}, u32[]{:S(2)}, u32[]{:S(2)}) collective-permute-start(bf16[528,128]{1,0:T(8,128)(2,1)S(1)} %join.2.refs_0_), channel_id=1, source_target_pairs={{2,4},{3,5},{4,6},{5,7},{10,12},{11,13},{12,14},{13,15},{18,20},{1... | collective-permute-start | bytes 405512 | tf_op jit(solution)/shard_map/ppermute | solution.py:801
  25.2 1.5 %collective-permute-start.6 = (bf16[528,128]{1,0:T(8,128)(2,1)S(1)}, bf16[528,128]{1,0:T(8,128)(2,1)S(1)}, u32[]{:S(2)}, u32[]{:S(2)}) collective-permute-start(bf16[528,128]{1,0:T(8,128)(2,1)S(1)} %join.2.refs_0_), channel_id=1, source_target_pairs={{2,6},{3,7},{10,14},{11,15},{18,22},{19,23},{26,30},{27,31}} | collective-permute-start | bytes 405512 | tf_op jit(solution)/shard_map/ppermute | solution.py:801
  26.7 0.9 %collective-permute-done.9.refs_3_.refs_1_ = bf16[528,128]{1,0:T(8,128)(2,1)S(1)} collective-permute-done((bf16[528,128]{1,0:T(8,128)(2,1)S(1)}, bf16[528,128]{1,0:T(8,128)(2,1)S(1)}, u32[]{:S(2)}, u32[]{:S(2)}) %collective-permute-start.9) | collective-permute-done | bytes 135200 | tf_op jit(solution)/shard_map/ppermute | solution.py:801
  27.5 0.4 join.3
  27.9 1.3 %collective-permute-start.12 = (bf16[528,128]{1,0:T(8,128)(2,1)S(1)}, bf16[528,128]{1,0:T(8,128)(2,1)S(1)}, u32[]{:S(2)}, u32[]{:S(2)}) collective-permute-start(bf16[528,128]{1,0:T(8,128)(2,1)S(1)} %join.3), channel_id=1, source_target_pairs={{2,4},{3,5},{4,6},{5,7},{10,12},{11,13},{12,14},{13,15},{18,20},{1... | collective-permute-start | bytes 405512 | tf_op jit(solution)/shard_map/ppermute | solution.py:801
  29.2 2.0 %collective-permute-start.11 = (bf16[528,128]{1,0:T(8,128)(2,1)S(1)}, bf16[528,128]{1,0:T(8,128)(2,1)S(1)}, u32[]{:S(2)}, u32[]{:S(2)}) collective-permute-start(bf16[528,128]{1,0:T(8,128)(2,1)S(1)} %join.3), channel_id=1, source_target_pairs={{2,6},{3,7},{10,14},{11,15},{18,22},{19,23},{26,30},{27,31}} | collective-permute-start | bytes 405512 | tf_op jit(solution)/shard_map/ppermute | solution.py:801
  31.3 6.5 %tail.1 = (f32[4,256,128]{2,1,0:T(8,128)S(1)}, f32[4,256,128]{2,1,0:T(8,128)S(1)}, f32[4,256,128]{2,1,0:T(8,128)S(1)}, f32[4,256,128]{2,1,0:T(8,128)S(1)}) custom-call(bf16[528,128]{1,0:T(8,128)(2,1)S(1)} %collective-permute-done.5.refs_1_.refs_0_, bf16[528,128]{1,0:T(8,128)(2,1)S(1)} %collective-permute-done.9.refs_3_.refs_1_, ...), custom_call_target="tpu_custom_call" | custom-call | flops 1000000 | bytes 1000000 | tf_op jit(solution)/shard_map/tail/pallas_call | solution.py:961
  37.8 0.4 finish.2
  38.2 1.4 %collective-permute-start.13 = (bf16[128,512]{1,0:T(8,128)(2,1)S(1)}, bf16[128,512]{1,0:T(8,128)(2,1)S(1)}, u32[]{:S(2)}, u32[]{:S(2)}) collective-permute-start(bf16[128,512]{1,0:T(8,128)(2,1)S(1)} %get-tuple-element.91), channel_id=1, source_target_pairs={{0,1},{1,0},{2,3},{3,2},{4,5},{5,4},{6,7},{7,6},{8,9},{9,8},{10,11... | collective-permute-start | bytes 393224 | tf_op jit(solution)/shard_map/ppermute | solution.py:1051
  40.1 0.5 %collective-permute-done.13.refs_2_ = bf16[128,512]{1,0:T(8,128)(2,1)S(1)} collective-permute-done((bf16[128,512]{1,0:T(8,128)(2,1)S(1)}, bf16[128,512]{1,0:T(8,128)(2,1)S(1)}, u32[]{:S(2)}, u32[]{:S(2)}) %collective-permute-start.13) | collective-permute-done | bytes 131104 | tf_op jit(solution)/shard_map/ppermute | solution.py:1051
  40.6 0.8 %collective-permute-done.14.refs_3_ = bf16[128,512]{1,0:T(8,128)(2,1)S(1)} collective-permute-done((bf16[128,512]{1,0:T(8,128)(2,1)S(1)}, bf16[128,512]{1,0:T(8,128)(2,1)S(1)}, u32[]{:S(2)}, u32[]{:S(2)}) %collective-permute-start.14) | collective-permute-done | bytes 131104 | tf_op jit(solution)/shard_map/ppermute | solution.py:1051
  41.4 0.8 %swap.1 = bf16[128,2048]{1,0:T(8,128)(2,1)} custom-call(bf16[128,512]{1,0:T(8,128)(2,1)S(1)} %get-tuple-element.87.refs_0_, bf16[128,512]{1,0:T(8,128)(2,1)S(1)} %get-tuple-element.90.refs_1_, bf16[128,512]{1,0:T(8,128)(2,1)S(1)} %collective-permute-done.13.refs_2_, bf16[128,512]{1,0:T(8,128)(2,1)S(1)} %collective-permute-done.14.refs_3_), custom_call_target="tpu_custom_call" | custom-call | tf_op jit(solution)/shard_map/swap/pallas_call | solution.py:1052
  (20 shorter events, 0.6 us)
Async XLA Ops:
  0.0 7.3 %collective-permute-start = (bf16[128,2048]{1,0:T(8,128)(2,1)}, bf16[128,2048]{1,0:T(8,128)(2,1)S(1)}, u32[]{:S(2)}, u32[]{:S(2)}) collective-permute-start(bf16[128,2048]{1,0:T(8,128)(2,1)} %key.1), channel_id=1, source_target_pairs={{0,1},{1,0},{2,3},{3,2},{4,5},{5,4},{6,7},{7,6},{8,9},{9,8},{10,11... | collective-permute-start | bytes 1572872 | tf_op jit(solution)/shard_map/ppermute | solution.py:743
  0.7 6.6 %collective-permute-start.1 = (bf16[128,2048]{1,0:T(8,128)(2,1)}, bf16[128,2048]{1,0:T(8,128)(2,1)S(1)}, u32[]{:S(2)}, u32[]{:S(2)}) collective-permute-start(bf16[128,2048]{1,0:T(8,128)(2,1)} %value.1), channel_id=1, source_target_pairs={{0,1},{1,0},{2,3},{3,2},{4,5},{5,4},{6,7},{7,6},{8,9},{9,8},{10,11... | collective-permute-start | bytes 1572872 | tf_op jit(solution)/shard_map/ppermute | solution.py:744
  2.2 5.1 %collective-permute-start.2 = (f32[208,128]{1,0:T(8,128)S(1)}, f32[208,128]{1,0:T(8,128)S(1)}, u32[]{:S(2)}, u32[]{:S(2)}) collective-permute-start(f32[208,128]{1,0:T(8,128)S(1)} %get-tuple-element.71.small_own.refs_7_.refs_2_.refs_3_), channel_id=1, source_target_pairs={{0,1},{1,0},{2,3},{3,2},{4,5},{5,4},{6,7},{7,6},{8,9},{9,8},{10,11... | collective-permute-start | bytes 319496 | tf_op jit(solution)/shard_map/ppermute | solution.py:785
  2.8 8.9 %collective-permute-start.4 = (bf16[16,2048]{1,0:T(8,128)(2,1)S(1)}, bf16[16,2048]{1,0:T(8,128)(2,1)S(1)}, u32[]{:S(2)}, u32[]{:S(2)}) collective-permute-start(bf16[16,2048]{1,0:T(8,128)(2,1)S(1)} %get-tuple-element.55), channel_id=1, source_target_pairs={{1,3},{3,5},{5,7},{9,11},{11,13},{13,15},{17,19},{19,21},{21,23},{... | collective-permute-start | bytes 196616 | tf_op jit(solution)/shard_map/ppermute | solution.py:787
  6.0 5.7 %collective-permute-start.3 = (bf16[16,2048]{1,0:T(8,128)(2,1)S(1)}, bf16[16,2048]{1,0:T(8,128)(2,1)S(1)}, u32[]{:S(2)}, u32[]{:S(2)}) collective-permute-start(bf16[16,2048]{1,0:T(8,128)(2,1)S(1)} %get-tuple-element.55), channel_id=1, source_target_pairs={{1,2},{3,4},{5,6},{9,10},{11,12},{13,14},{17,18},{19,20},{21,22},{... | collective-permute-start | bytes 196616 | tf_op jit(solution)/shard_map/ppermute | solution.py:786
  11.7 4.8 %copy-start = (bf16[128,2048]{1,0:T(8,128)(2,1)S(1)}, bf16[128,2048]{1,0:T(8,128)(2,1)}, u32[]{:S(2)}) copy-start(bf16[128,2048]{1,0:T(8,128)(2,1)} %gate.1) | copy-start | bytes 1572868
  11.7 4.8 %copy-start.1 = (bf16[128,2048]{1,0:T(8,128)(2,1)S(1)}, bf16[128,2048]{1,0:T(8,128)(2,1)}, u32[]{:S(2)}) copy-start(bf16[128,2048]{1,0:T(8,128)(2,1)} %query.1) | copy-start | bytes 1572868
  15.2 6.6 %collective-permute-start.5 = (bf16[528,128]{1,0:T(8,128)(2,1)S(1)}, bf16[528,128]{1,0:T(8,128)(2,1)S(1)}, u32[]{:S(2)}, u32[]{:S(2)}) collective-permute-start(bf16[528,128]{1,0:T(8,128)(2,1)S(1)} %get-tuple-element.58), channel_id=1, source_target_pairs={{0,2},{1,3},{4,6},{5,7},{8,10},{9,11},{12,14},{13,15},{16,18},{17,... | collective-permute-start | bytes 405512 | tf_op jit(solution)/shard_map/ppermute | solution.py:801
  16.5 11.1 %collective-permute-start.8 = (bf16[128,2048]{1,0:T(8,128)(2,1)S(1)}, bf16[128,2048]{1,0:T(8,128)(2,1)S(1)}, u32[]{:S(2)}, u32[]{:S(2)}) collective-permute-start(bf16[128,2048]{1,0:T(8,128)(2,1)S(1)} %copy-done), channel_id=1, source_target_pairs={{0,1},{1,0},{2,3},{3,2},{4,5},{5,4},{6,7},{7,6},{8,9},{9,8},{10,11... | collective-permute-start | bytes 1572872 | tf_op jit(solution)/shard_map/ppermute | solution.py:863
  16.6 11.0 %collective-permute-start.10 = (bf16[128,2048]{1,0:T(8,128)(2,1)S(1)}, bf16[128,2048]{1,0:T(8,128)(2,1)S(1)}, u32[]{:S(2)}, u32[]{:S(2)}) collective-permute-start(bf16[128,2048]{1,0:T(8,128)(2,1)S(1)} %copy-done.1), channel_id=1, source_target_pairs={{0,1},{1,0},{2,3},{3,2},{4,5},{5,4},{6,7},{7,6},{8,9},{9,8},{10,11... | collective-permute-start | bytes 1572872 | tf_op jit(solution)/shard_map/ppermute | solution.py:863
  20.5 7.0 %collective-permute-start.9 = (bf16[528,128]{1,0:T(8,128)(2,1)S(1)}, bf16[528,128]{1,0:T(8,128)(2,1)S(1)}, u32[]{:S(2)}, u32[]{:S(2)}) collective-permute-start(bf16[528,128]{1,0:T(8,128)(2,1)S(1)} %get-tuple-element.60.refs_0_), channel_id=1, source_target_pairs={{0,2},{1,3},{4,6},{5,7},{8,10},{9,11},{12,14},{13,15},{16,18},{17,... | collective-permute-start | bytes 405512 | tf_op jit(solution)/shard_map/ppermute | solution.py:801
  22.2 15.6 %collective-permute-start.7 = (bf16[528,128]{1,0:T(8,128)(2,1)S(1)}, bf16[528,128]{1,0:T(8,128)(2,1)S(1)}, u32[]{:S(2)}, u32[]{:S(2)}) collective-permute-start(bf16[528,128]{1,0:T(8,128)(2,1)S(1)} %join.2.refs_0_), channel_id=1, source_target_pairs={{2,4},{3,5},{4,6},{5,7},{10,12},{11,13},{12,14},{13,15},{18,20},{1... | collective-permute-start | bytes 405512 | tf_op jit(solution)/shard_map/ppermute | solution.py:801
  25.2 12.6 %collective-permute-start.6 = (bf16[528,128]{1,0:T(8,128)(2,1)S(1)}, bf16[528,128]{1,0:T(8,128)(2,1)S(1)}, u32[]{:S(2)}, u32[]{:S(2)}) collective-permute-start(bf16[528,128]{1,0:T(8,128)(2,1)S(1)} %join.2.refs_0_), channel_id=1, source_target_pairs={{2,6},{3,7},{10,14},{11,15},{18,22},{19,23},{26,30},{27,31}} | collective-permute-start | bytes 405512 | tf_op jit(solution)/shard_map/ppermute | solution.py:801
  27.9 11.7 %collective-permute-start.12 = (bf16[528,128]{1,0:T(8,128)(2,1)S(1)}, bf16[528,128]{1,0:T(8,128)(2,1)S(1)}, u32[]{:S(2)}, u32[]{:S(2)}) collective-permute-start(bf16[528,128]{1,0:T(8,128)(2,1)S(1)} %join.3), channel_id=1, source_target_pairs={{2,4},{3,5},{4,6},{5,7},{10,12},{11,13},{12,14},{13,15},{18,20},{1... | collective-permute-start | bytes 405512 | tf_op jit(solution)/shard_map/ppermute | solution.py:801
  29.2 10.4 %collective-permute-start.11 = (bf16[528,128]{1,0:T(8,128)(2,1)S(1)}, bf16[528,128]{1,0:T(8,128)(2,1)S(1)}, u32[]{:S(2)}, u32[]{:S(2)}) collective-permute-start(bf16[528,128]{1,0:T(8,128)(2,1)S(1)} %join.3), channel_id=1, source_target_pairs={{2,6},{3,7},{10,14},{11,15},{18,22},{19,23},{26,30},{27,31}} | collective-permute-start | bytes 405512 | tf_op jit(solution)/shard_map/ppermute | solution.py:801
  38.2 2.4 %collective-permute-start.13 = (bf16[128,512]{1,0:T(8,128)(2,1)S(1)}, bf16[128,512]{1,0:T(8,128)(2,1)S(1)}, u32[]{:S(2)}, u32[]{:S(2)}) collective-permute-start(bf16[128,512]{1,0:T(8,128)(2,1)S(1)} %get-tuple-element.91), channel_id=1, source_target_pairs={{0,1},{1,0},{2,3},{3,2},{4,5},{5,4},{6,7},{7,6},{8,9},{9,8},{10,11... | collective-permute-start | bytes 393224 | tf_op jit(solution)/shard_map/ppermute | solution.py:1051
  39.9 1.4 %collective-permute-start.14 = (bf16[128,512]{1,0:T(8,128)(2,1)S(1)}, bf16[128,512]{1,0:T(8,128)(2,1)S(1)}, u32[]{:S(2)}, u32[]{:S(2)}) collective-permute-start(bf16[128,512]{1,0:T(8,128)(2,1)S(1)} %get-tuple-element.92), channel_id=1, source_target_pairs={{0,1},{1,0},{2,3},{3,2},{4,5},{5,4},{6,7},{7,6},{8,9},{9,8},{10,11... | collective-permute-start | bytes 393224 | tf_op jit(solution)/shard_map/ppermute | solution.py:1051

commit v4 on v3

--- a/solution.py
+++ b/solution.py
@@ -37,8 +37,13 @@
     return out[:, :width] + out[:, width:]
 
 
+def mm_three(a, b):
+    return (dot(a[1], b[0]) + dot(a[0], b[1])) + dot(a[0], b[0])
+
+
 def silu(u):
-    return u / (1.0 + jnp.exp(-u))
+    half = 0.5 * u
+    return half + half * jnp.tanh(half)
 
 
 def encode(state):
@@ -67,11 +72,11 @@
     return index % 2, index // 2
 
 
-def fill(scratch, own, other, before, core, chunk, first_lane):
+def fill(scratch, own, other, before, core, chunk, first_lane, packed=False):
     lanes = scratch.shape[1]
     start = pl.multiple_of(core * 8 * HEAD_DIM + first_lane, 128)
     mine = own[:, first_lane : first_lane + lanes]
-    theirs = other[:, pl.ds(start, lanes)]
+    theirs = other[:, first_lane : first_lane + lanes] if packed else other[:, pl.ds(start, lanes)]
     if before is None:
         last = jnp.where(core == 1, theirs[CHUNK - 16 :], mine[CHUNK - 16 :]).astype(F32)[13:16]
     else:
@@ -175,7 +180,8 @@
 
 def prepare_kernel(query, key, value, gate, log_alpha, strength, mixture, query_taps, key_taps,
                    value_taps, gain, query_half, key_half, value_half, gate_half, query_taps_half,
-                   key_taps_half, value_taps_half, halo, small, gain_out, tails, sems):
+                   key_taps_half, value_taps_half, halo, small, gain_out, message_out,
+                   tails, sems):
     core, _ = place()
     rows, half = query_half.shape
     lanes = pl.ds(pl.multiple_of(core * half, half), half)
@@ -202,6 +208,9 @@
     ):
         copy(x.at[:, lanes], y)
     copy(gain, gain_out)
+    away = pl.ds(pl.multiple_of((1 - core) * half, half), half)
+    copy(query.at[:, away], message_out.at[:, 0:half])
+    copy(gate.at[:, away], message_out.at[:, half : 2 * half])
     for made in copies:
         made.wait()
     message = [tails[i][13:16, :].astype(F32) for i in range(3)]
@@ -399,8 +408,8 @@
 ):
     core, _ = place()
     start = group * heads + first
-    fill(scratch_one, query_own, query_other, (halo_one, halo_two, 0), core, 0, start * 128)
-    fill(scratch_two, query_own, query_other, None, core, 1, start * 128)
+    fill(scratch_one, query_own, query_other, (halo_one, halo_two, 0), core, 0, start * 128, True)
+    fill(scratch_two, query_own, query_other, None, core, 1, start * 128, True)
     t, j = iotas(CHUNK, CHUNK)
     apart = t ^ j
     parts = [(head, chunk) for head in range(count) for chunk in range(2)]
@@ -447,6 +456,10 @@
             effective = mm(pair, split(transit_one[first + head]))
         out[head, rows, :] = within
         moved[head, rows, :] = effective
+
+
+def asked_kernel(group, heads, first, count, near, after, *refs):
+    queries_kernel(group, heads, first, count, near, *refs)
 
 
 def received(refs, head):
@@ -645,7 +658,7 @@
                 found = split(mm(split(received(transits, head)), found))
             row = weight_row + 8 * core + heads * group + head
             weight = level_weight(small_own, small_other, row, core)
-            extra = mm(split(moved_in[head // each][head % each]), found)
+            extra = mm_three(split(moved_in[head // each][head % each]), found)
             total[head] = outs_in[head // each][head % each] + weight * extra
 
     if level:
@@ -672,10 +685,10 @@
             total[head] = outs_in[head // each][head % each]
 
     lanes_all = heads * 128
-    start = pl.multiple_of(core * 8 * HEAD_DIM + group * lanes_all, lanes_all)
+    at = gate_other.shape[1] // 2 + group * lanes_all
     gates = (
         gate_own[:, group * lanes_all : (group + 1) * lanes_all],
-        gate_other[:, pl.ds(start, lanes_all)],
+        gate_other[:, at : at + lanes_all],
     )
     for head in range(heads):
         lanes = slice(head * 128, head * 128 + 128)
@@ -688,16 +701,20 @@
 
 
 def swap_kernel(*refs):
-    out = refs[-1]
-    count = (len(refs) - 1) // 2
+    out, sems = refs[-2:]
+    count = (len(refs) - 2) // 2
     core, _ = place()
     half = out.shape[1] // 2
     width = half // count
+    copies = []
     for i in range(count):
-        start = pl.multiple_of(core * half + i * width, width)
-        out[:, pl.ds(start, width)] = refs[i][...]
-        start = pl.multiple_of((1 - core) * half + i * width, width)
-        out[:, pl.ds(start, width)] = refs[count + i][...]
+        for j, side in ((i, core), (count + i, 1 - core)):
+            start = pl.multiple_of(side * half + i * width, width)
+            made = pltpu.make_async_copy(refs[j], out.at[:, pl.ds(start, width)], sems.at[j])
+            made.start()
+            copies.append(made)
+    for made in copies:
+        made.wait()
 
 
 def struct(shape, dtype=F32):
@@ -755,13 +772,15 @@
         halo,
         small,
         gain,
+        message,
     ) = pl.pallas_call(
         prepare_kernel,
         in_specs=[pl.BlockSpec(memory_space=pltpu.HBM)] * 11,
         out_shape=[half_shape] * 4
         + [taps_shape] * 3
-        + [struct((16, width), BF16), struct((small_rows, 128)), struct((1, 128))],
-        scratch_shapes=[pltpu.VMEM((3, 16, width), BF16), pltpu.SemaphoreType.DMA((14,))],
+        + [struct((16, width), BF16), struct((small_rows, 128)), struct((1, 128))]
+        + [struct((rows, width), BF16)],
+        scratch_shapes=[pltpu.VMEM((3, 16, width), BF16), pltpu.SemaphoreType.DMA((16,))],
         compiler_params=params(8),
         name="prepare",
     )(
@@ -858,11 +877,8 @@
         after = made[7]
         arrived.append(fan(made[7], 0) if shard_bits else [])
 
-    def swap_rows(after):
-        _, query_late, gate_late = lax.optimization_barrier((after, query_rows, output_gate))
-        return lax.ppermute(query_late, "seq", cores), lax.ppermute(gate_late, "seq", cores)
-
-    query_other, gate_other = swap_rows(local[0][7])
+    _, late_message = lax.optimization_barrier((local[0][7], message))
+    query_other = gate_other = lax.ppermute(late_message, "seq", cores)
     state = [x[4] for x in local]
     transit = [x[6] for x in local]
     count = heads // PIECES
@@ -874,27 +890,29 @@
         group, piece = pending.pop(0)
         made = local[group]
         shape = struct((count, 2 * CHUNK, 128))
-        after, small_here = lax.optimization_barrier((after, small))
-        out, move = pl.pallas_call(
-            functools.partial(queries_kernel, group, heads, piece * count, count, near),
-            out_shape=[shape, shape],
-            scratch_shapes=[pltpu.VMEM((8 + CHUNK, count * 128), F32)] * 2,
-            compiler_params=params(16),
-            cost_estimate=cost(4_000_000_000),
-            name="queries",
-        )(
+        operands = [
             query_half,
             query_other,
             query_taps_half,
             halo_one,
             halo_two,
-            small_here,
+            small,
             small_other,
             *made[:3],
             *upper[:3],
             made[3],
             made[5],
-        )
+        ]
+        out, move = pl.pallas_call(
+            functools.partial(asked_kernel, group, heads, piece * count, count, near),
+            in_specs=[pl.BlockSpec(memory_space=pl.ANY)]
+            + [pl.BlockSpec(memory_space=pltpu.VMEM)] * len(operands),
+            out_shape=[shape, shape],
+            scratch_shapes=[pltpu.VMEM((8 + CHUNK, count * 128), F32)] * 2,
+            compiler_params=params(16),
+            cost_estimate=cost(1_000_000),
+            name="queries",
+        )(after, *operands)
         outs[group].append(out)
         moved[group].append(move)
         return out
@@ -930,7 +948,7 @@
                 operands += fanned[group]
             waits = [after]
             if level == 0 and group == GROUPS - 1:
-                waits += [query_other, gate_other]
+                waits += [query_other]
             joined = pl.pallas_call(
                 functools.partial(
                     join_kernel, level, len(arrived[group]), keeps, shifts[group], len(waits)
@@ -1051,7 +1069,10 @@
         comes.append(lax.ppermute(leave, "seq", cores))
     return pl.pallas_call(
         swap_kernel,
+        in_specs=[pl.BlockSpec(memory_space=pltpu.VMEM)] * (2 * GROUPS),
+        out_specs=pl.BlockSpec(memory_space=pltpu.HBM),
         out_shape=struct((rows, width), BF16),
+        scratch_shapes=[pltpu.SemaphoreType.DMA((2 * GROUPS,))],
         compiler_params=params(4),
         name="swap",
     )(*stays, *comes)

time: 42.4 us -> 42.3 us (level)
  waiting for transfers between devices: 2.19 us -> 1.61 us
    ppermute x6, starting transfers between devices: 10.3 us -> 11.3 us  [fan(): results.append(lax.ppermute(value, 'seq', route))]
    ppermute x6, waiting for transfers between devices: 0.89 us -> 0.31 us  [fan(): results.append(lax.ppermute(value, 'seq', route))]
    ppermute x2 -> x1, starting transfers between devices: 0.56 us -> 0.07 us  [per_device(): query_other = gate_other = lax.ppermute(late_message, 'seq', cores)]
  transfers between devices with their start and end apart: 15 -> 14, of which waited for: 3 -> 3; matrix products, arithmetic and copies ran while one was open for 0% -> 0% of each run, Pallas kernels for 41% -> 41%
where the time goes in v4:
time: 42.3 us; the launch traced here: 42.1 us
  Pallas kernels  21.6 us (51%)
  starting transfers between devices  18.5 us (44%)
  waiting for transfers between devices  1.61 us (4%)
    ppermute x6, starting transfers between devices, fan(): results.append(lax.ppermute(value, 'seq', route))  11.3 us
    pallas_call x2, Pallas kernels, per_device(): pl.pallas_call(functools.partial(lower_kernel, group, heads), out_shape=h...  6.86 us
    pallas_call x1, Pallas kernels, per_device(): pl.pallas_call(functools.partial(tail_kernel, level, 32 + 16 * (near + 1...  6.5 us
    pallas_call x1, Pallas kernels, per_device(): pl.pallas_call(upper_kernel, out_shape=held(8) + [struct((8, 128, 128))]...  4.32 us
    ppermute x1, starting transfers between devices, per_device(): lax.ppermute(halo, 'seq', [(i, i + 2) for i in range(1, size - 1, 2)])  3.19 us
    pallas_call x1, Pallas kernels, per_device(): pl.pallas_call(prepare_kernel, in_specs=[pl.BlockSpec(memory_space=pltpu....  1.71 us
    ppermute x2, starting transfers between devices, per_device(): comes.append(lax.ppermute(leave, 'seq', cores))  1.46 us
    ppermute x1, starting transfers between devices, per_device(): lax.ppermute(halo, 'seq', [(i, i + 1) for i in range(1, size - 1, 2)])  1.29 us
  transfers between devices with their start and end apart: 14, of which 3 were waited for; matrix products, arithmetic and copies ran while one was open for 0% of the time, Pallas kernels for 41%

profile of v4, /device:TPU:11, one launch (start us, length us, event | category | flops | bytes accessed | tf_op | source)
XLA Modules:
  0.0 42.1 jit_solution(12811155703186621106)
XLA Ops:
  0.0 0.7 %collective-permute-start = (bf16[128,2048]{1,0:T(8,128)(2,1)}, bf16[128,2048]{1,0:T(8,128)(2,1)S(1)}, u32[]{:S(2)}, u32[]{:S(2)}) collective-permute-start(bf16[128,2048]{1,0:T(8,128)(2,1)} %key.1), channel_id=1, source_target_pairs={{0,1},{1,0},{2,3},{3,2},{4,5},{5,4},{6,7},{7,6},{8,9},{9,8},{10,11... | collective-permute-start | bytes 1572872 | tf_op jit(solution)/shard_map/ppermute | solution.py:760
  0.7 1.7 %prepare.1 = (bf16[128,1024]{1,0:T(8,128)(2,1)S(1)}, bf16[128,1024]{1,0:T(8,128)(2,1)S(1)}, bf16[128,1024]{1,0:T(8,128)(2,1)S(1)}, bf16[128,1024]{1,0:T(8,128)(2...) custom-call(bf16[128,2048]{1,0:T(8,128)(2,1)} %query.1, ...), custom_call_target="tpu_custom_call" | custom-call | tf_op jit(solution)/shard_map/prepare/pallas_call | solution.py:776
  2.4 0.6 %collective-permute-start.2 = (f32[208,128]{1,0:T(8,128)S(1)}, f32[208,128]{1,0:T(8,128)S(1)}, u32[]{:S(2)}, u32[]{:S(2)}) collective-permute-start(f32[208,128]{1,0:T(8,128)S(1)} %get-tuple-element.71.small_own.refs_7_.refs_2_.refs_3_), channel_id=1, source_target_pairs={{0,1},{1,0},{2,3},{3,2},{4,5},{5,4},{6,7},{7,6},{8,9},{9,8},{10,11... | collective-permute-start | bytes 319496 | tf_op jit(solution)/shard_map/ppermute | solution.py:804
  3.0 3.2 %collective-permute-start.4 = (bf16[16,2048]{1,0:T(8,128)(2,1)S(1)}, bf16[16,2048]{1,0:T(8,128)(2,1)S(1)}, u32[]{:S(2)}, u32[]{:S(2)}) collective-permute-start(bf16[16,2048]{1,0:T(8,128)(2,1)S(1)} %get-tuple-element.55), channel_id=1, source_target_pairs={{1,3},{3,5},{5,7},{9,11},{11,13},{13,15},{17,19},{19,21},{21,23},{... | collective-permute-start | bytes 196616 | tf_op jit(solution)/shard_map/ppermute | solution.py:806
  6.2 1.3 %collective-permute-start.3 = (bf16[16,2048]{1,0:T(8,128)(2,1)S(1)}, bf16[16,2048]{1,0:T(8,128)(2,1)S(1)}, u32[]{:S(2)}, u32[]{:S(2)}) collective-permute-start(bf16[16,2048]{1,0:T(8,128)(2,1)S(1)} %get-tuple-element.55), channel_id=1, source_target_pairs={{1,2},{3,4},{5,6},{9,10},{11,12},{13,14},{17,18},{19,20},{21,22},{... | collective-permute-start | bytes 196616 | tf_op jit(solution)/shard_map/ppermute | solution.py:805
  7.5 4.3 %upper.1 = (bf16[8,2,128,128]{3,2,1,0:T(8,128)(2,1)S(1)}, bf16[8,2,128,128]{3,2,1,0:T(8,128)(2,1)S(1)}, bf16[8,2,128,256]{3,2,1,0:T(8,128)(2,1)S(1)}, f32[8,128,128]{2,1,0:T(8,128)S(1)}, f32[8,128,128]{2,1,0:T(8,128)S(1)}) custom-call(bf16[128,1024]{1,0:T(8,128)(2,1)S(1)} %get-tuple-element.49.key_own, bf16[128,2048]{1,0:T(8,128)(2,1)S(1)} %collective-permute-done.key_other, ...), custom_call_target="tpu_custom_call" | custom-call | flops 4000000000 | bytes 1000000 | tf_op jit(solution)/shard_map/upper/pallas_call | solution.py:832
  11.8 3.4 %lower.2 = (bf16[4,2,128,128]{3,2,1,0:T(8,128)(2,1)S(1)}, bf16[4,2,128,128]{3,2,1,0:T(8,128)(2,1)S(1)}, bf16[4,2,128,256]{3,2,1,0:T(8,128)(2,1)S(1)}, f32[4,128,...) custom-call(bf16[128,1024]{1,0:T(8,128)(2,1)S(1)} %get-tuple-element, ...), custom_call_target="tpu_custom_call" | custom-call | flops 2500000000 | bytes 1000000 | tf_op jit(solution)/shard_map/lower/pallas_call | solution.py:854
  15.3 1.3 %collective-permute-start.5 = (bf16[528,128]{1,0:T(8,128)(2,1)S(1)}, bf16[528,128]{1,0:T(8,128)(2,1)S(1)}, u32[]{:S(2)}, u32[]{:S(2)}) collective-permute-start(bf16[528,128]{1,0:T(8,128)(2,1)S(1)} %get-tuple-element.58), channel_id=1, source_target_pairs={{0,2},{1,3},{4,6},{5,7},{8,10},{9,11},{12,14},{13,15},{16,18},{17,... | collective-permute-start | bytes 405512 | tf_op jit(solution)/shard_map/ppermute | solution.py:820
  16.7 3.4 %lower.3 = (bf16[4,2,128,128]{3,2,1,0:T(8,128)(2,1)S(1)}, bf16[4,2,128,128]{3,2,1,0:T(8,128)(2,1)S(1)}, bf16[4,2,128,256]{3,2,1,0:T(8,128)(2,1)S(1)}, f32[4,128,...) custom-call(bf16[128,1024]{1,0:T(8,128)(2,1)S(1)} %get-tuple-element, ...), custom_call_target="tpu_custom_call" | custom-call | flops 2500000000 | bytes 1000000 | tf_op jit(solution)/shard_map/lower/pallas_call | solution.py:854
  20.1 1.3 %collective-permute-start.9 = (bf16[528,128]{1,0:T(8,128)(2,1)S(1)}, bf16[528,128]{1,0:T(8,128)(2,1)S(1)}, u32[]{:S(2)}, u32[]{:S(2)}) collective-permute-start(bf16[528,128]{1,0:T(8,128)(2,1)S(1)} %get-tuple-element.60.refs_0_), channel_id=1, source_target_pairs={{0,2},{1,3},{4,6},{5,7},{8,10},{9,11},{12,14},{13,15},{16,18},{17,... | collective-permute-start | bytes 405512 | tf_op jit(solution)/shard_map/ppermute | solution.py:820
  21.4 0.4 join.2.refs_0_
  21.8 3.2 %collective-permute-start.7 = (bf16[528,128]{1,0:T(8,128)(2,1)S(1)}, bf16[528,128]{1,0:T(8,128)(2,1)S(1)}, u32[]{:S(2)}, u32[]{:S(2)}) collective-permute-start(bf16[528,128]{1,0:T(8,128)(2,1)S(1)} %join.2.refs_0_), channel_id=1, source_target_pairs={{2,4},{3,5},{4,6},{5,7},{10,12},{11,13},{12,14},{13,15},{18,20},{1... | collective-permute-start | bytes 405512 | tf_op jit(solution)/shard_map/ppermute | solution.py:820
  25.1 1.3 %collective-permute-start.6 = (bf16[528,128]{1,0:T(8,128)(2,1)S(1)}, bf16[528,128]{1,0:T(8,128)(2,1)S(1)}, u32[]{:S(2)}, u32[]{:S(2)}) collective-permute-start(bf16[528,128]{1,0:T(8,128)(2,1)S(1)} %join.2.refs_0_), channel_id=1, source_target_pairs={{2,6},{3,7},{10,14},{11,15},{18,22},{19,23},{26,30},{27,31}} | collective-permute-start | bytes 405512 | tf_op jit(solution)/shard_map/ppermute | solution.py:820
  26.4 0.3 collective-permute-done.9.refs_2_.refs_1_
  26.7 0.4 join.3
  27.1 1.3 %collective-permute-start.11 = (bf16[528,128]{1,0:T(8,128)(2,1)S(1)}, bf16[528,128]{1,0:T(8,128)(2,1)S(1)}, u32[]{:S(2)}, u32[]{:S(2)}) collective-permute-start(bf16[528,128]{1,0:T(8,128)(2,1)S(1)} %join.3), channel_id=1, source_target_pairs={{2,4},{3,5},{4,6},{5,7},{10,12},{11,13},{12,14},{13,15},{18,20},{1... | collective-permute-start | bytes 405512 | tf_op jit(solution)/shard_map/ppermute | solution.py:820
  28.4 2.8 %collective-permute-start.10 = (bf16[528,128]{1,0:T(8,128)(2,1)S(1)}, bf16[528,128]{1,0:T(8,128)(2,1)S(1)}, u32[]{:S(2)}, u32[]{:S(2)}) collective-permute-start(bf16[528,128]{1,0:T(8,128)(2,1)S(1)} %join.3), channel_id=1, source_target_pairs={{2,6},{3,7},{10,14},{11,15},{18,22},{19,23},{26,30},{27,31}} | collective-permute-start | bytes 405512 | tf_op jit(solution)/shard_map/ppermute | solution.py:820
  31.2 6.5 %tail.1 = (f32[4,256,128]{2,1,0:T(8,128)S(1)}, f32[4,256,128]{2,1,0:T(8,128)S(1)}, f32[4,256,128]{2,1,0:T(8,128)S(1)}, f32[4,256,128]{2,1,0:T(8,128)S(1)}) custom-call(bf16[528,128]{1,0:T(8,128)(2,1)S(1)} %collective-permute-done.5.refs_1_.refs_0_, bf16[528,128]{1,0:T(8,128)(2,1)S(1)} %collective-permute-done.9.refs_2_.refs_1_, ...), custom_call_target="tpu_custom_call" | custom-call | flops 1000000 | bytes 1000000 | tf_op jit(solution)/shard_map/tail/pallas_call | solution.py:979
  37.7 0.3 finish.2
  38.0 1.3 %collective-permute-start.12 = (bf16[128,512]{1,0:T(8,128)(2,1)S(1)}, bf16[128,512]{1,0:T(8,128)(2,1)S(1)}, u32[]{:S(2)}, u32[]{:S(2)}) collective-permute-start(bf16[128,512]{1,0:T(8,128)(2,1)S(1)} %get-tuple-element.91), channel_id=1, source_target_pairs={{0,1},{1,0},{2,3},{3,2},{4,5},{5,4},{6,7},{7,6},{8,9},{9,8},{10,11... | collective-permute-start | bytes 393224 | tf_op jit(solution)/shard_map/ppermute | solution.py:1069
  39.4 0.3 finish.3
  39.8 0.6 %collective-permute-done.12.refs_2_ = bf16[128,512]{1,0:T(8,128)(2,1)S(1)} collective-permute-done((bf16[128,512]{1,0:T(8,128)(2,1)S(1)}, bf16[128,512]{1,0:T(8,128)(2,1)S(1)}, u32[]{:S(2)}, u32[]{:S(2)}) %collective-permute-start.12) | collective-permute-done | bytes 131104 | tf_op jit(solution)/shard_map/ppermute | solution.py:1069
  40.4 0.7 %collective-permute-done.13.refs_3_ = bf16[128,512]{1,0:T(8,128)(2,1)S(1)} collective-permute-done((bf16[128,512]{1,0:T(8,128)(2,1)S(1)}, bf16[128,512]{1,0:T(8,128)(2,1)S(1)}, u32[]{:S(2)}, u32[]{:S(2)}) %collective-permute-start.13) | collective-permute-done | bytes 131104 | tf_op jit(solution)/shard_map/ppermute | solution.py:1069
  41.1 0.8 %swap.1 = bf16[128,2048]{1,0:T(8,128)(2,1)} custom-call(bf16[128,512]{1,0:T(8,128)(2,1)S(1)} %get-tuple-element.87.refs_0_, bf16[128,512]{1,0:T(8,128)(2,1)S(1)} %get-tuple-element.90.refs_1_, bf16[128,512]{1,0:T(8,128)(2,1)S(1)} %collective-permute-done.12.refs_2_, bf16[128,512]{1,0:T(8,128)(2,1)S(1)} %collective-permute-done.13.refs_3_), custom_call_target="tpu_custom_call" | custom-call | tf_op jit(solution)/shard_map/swap/pallas_call | solution.py:1070
  (14 shorter events, 0.2 us)
Async XLA Ops:
  0.0 7.5 %collective-permute-start = (bf16[128,2048]{1,0:T(8,128)(2,1)}, bf16[128,2048]{1,0:T(8,128)(2,1)S(1)}, u32[]{:S(2)}, u32[]{:S(2)}) collective-permute-start(bf16[128,2048]{1,0:T(8,128)(2,1)} %key.1), channel_id=1, source_target_pairs={{0,1},{1,0},{2,3},{3,2},{4,5},{5,4},{6,7},{7,6},{8,9},{9,8},{10,11... | collective-permute-start | bytes 1572872 | tf_op jit(solution)/shard_map/ppermute | solution.py:760
  0.7 6.8 %collective-permute-start.1 = (bf16[128,2048]{1,0:T(8,128)(2,1)}, bf16[128,2048]{1,0:T(8,128)(2,1)S(1)}, u32[]{:S(2)}, u32[]{:S(2)}) collective-permute-start(bf16[128,2048]{1,0:T(8,128)(2,1)} %value.1), channel_id=1, source_target_pairs={{0,1},{1,0},{2,3},{3,2},{4,5},{5,4},{6,7},{7,6},{8,9},{9,8},{10,11... | collective-permute-start | bytes 1572872 | tf_op jit(solution)/shard_map/ppermute | solution.py:761
  2.4 5.1 %collective-permute-start.2 = (f32[208,128]{1,0:T(8,128)S(1)}, f32[208,128]{1,0:T(8,128)S(1)}, u32[]{:S(2)}, u32[]{:S(2)}) collective-permute-start(f32[208,128]{1,0:T(8,128)S(1)} %get-tuple-element.71.small_own.refs_7_.refs_2_.refs_3_), channel_id=1, source_target_pairs={{0,1},{1,0},{2,3},{3,2},{4,5},{5,4},{6,7},{7,6},{8,9},{9,8},{10,11... | collective-permute-start | bytes 319496 | tf_op jit(solution)/shard_map/ppermute | solution.py:804
  3.0 8.9 %collective-permute-start.4 = (bf16[16,2048]{1,0:T(8,128)(2,1)S(1)}, bf16[16,2048]{1,0:T(8,128)(2,1)S(1)}, u32[]{:S(2)}, u32[]{:S(2)}) collective-permute-start(bf16[16,2048]{1,0:T(8,128)(2,1)S(1)} %get-tuple-element.55), channel_id=1, source_target_pairs={{1,3},{3,5},{5,7},{9,11},{11,13},{13,15},{17,19},{19,21},{21,23},{... | collective-permute-start | bytes 196616 | tf_op jit(solution)/shard_map/ppermute | solution.py:806
  6.2 5.7 %collective-permute-start.3 = (bf16[16,2048]{1,0:T(8,128)(2,1)S(1)}, bf16[16,2048]{1,0:T(8,128)(2,1)S(1)}, u32[]{:S(2)}, u32[]{:S(2)}) collective-permute-start(bf16[16,2048]{1,0:T(8,128)(2,1)S(1)} %get-tuple-element.55), channel_id=1, source_target_pairs={{1,2},{3,4},{5,6},{9,10},{11,12},{13,14},{17,18},{19,20},{21,22},{... | collective-permute-start | bytes 196616 | tf_op jit(solution)/shard_map/ppermute | solution.py:805
  15.3 6.1 %collective-permute-start.5 = (bf16[528,128]{1,0:T(8,128)(2,1)S(1)}, bf16[528,128]{1,0:T(8,128)(2,1)S(1)}, u32[]{:S(2)}, u32[]{:S(2)}) collective-permute-start(bf16[528,128]{1,0:T(8,128)(2,1)S(1)} %get-tuple-element.58), channel_id=1, source_target_pairs={{0,2},{1,3},{4,6},{5,7},{8,10},{9,11},{12,14},{13,15},{16,18},{17,... | collective-permute-start | bytes 405512 | tf_op jit(solution)/shard_map/ppermute | solution.py:820
  16.6 10.1 %collective-permute-start.8 = (bf16[128,2048]{1,0:T(8,128)(2,1)S(1)}, bf16[128,2048]{1,0:T(8,128)(2,1)S(1)}, u32[]{:S(2)}, u32[]{:S(2)}) collective-permute-start(bf16[128,2048]{1,0:T(8,128)(2,1)S(1)} %get-tuple-element.65), channel_id=1, source_target_pairs={{0,1},{1,0},{2,3},{3,2},{4,5},{5,4},{6,7},{7,6},{8,9},{9,8},{10,11... | collective-permute-start | bytes 1572872 | tf_op jit(solution)/shard_map/ppermute | solution.py:881
  20.1 6.6 %collective-permute-start.9 = (bf16[528,128]{1,0:T(8,128)(2,1)S(1)}, bf16[528,128]{1,0:T(8,128)(2,1)S(1)}, u32[]{:S(2)}, u32[]{:S(2)}) collective-permute-start(bf16[528,128]{1,0:T(8,128)(2,1)S(1)} %get-tuple-element.60.refs_0_), channel_id=1, source_target_pairs={{0,2},{1,3},{4,6},{5,7},{8,10},{9,11},{12,14},{13,15},{16,18},{17,... | collective-permute-start | bytes 405512 | tf_op jit(solution)/shard_map/ppermute | solution.py:820
  21.8 15.9 %collective-permute-start.7 = (bf16[528,128]{1,0:T(8,128)(2,1)S(1)}, bf16[528,128]{1,0:T(8,128)(2,1)S(1)}, u32[]{:S(2)}, u32[]{:S(2)}) collective-permute-start(bf16[528,128]{1,0:T(8,128)(2,1)S(1)} %join.2.refs_0_), channel_id=1, source_target_pairs={{2,4},{3,5},{4,6},{5,7},{10,12},{11,13},{12,14},{13,15},{18,20},{1... | collective-permute-start | bytes 405512 | tf_op jit(solution)/shard_map/ppermute | solution.py:820
  25.1 12.6 %collective-permute-start.6 = (bf16[528,128]{1,0:T(8,128)(2,1)S(1)}, bf16[528,128]{1,0:T(8,128)(2,1)S(1)}, u32[]{:S(2)}, u32[]{:S(2)}) collective-permute-start(bf16[528,128]{1,0:T(8,128)(2,1)S(1)} %join.2.refs_0_), channel_id=1, source_target_pairs={{2,6},{3,7},{10,14},{11,15},{18,22},{19,23},{26,30},{27,31}} | collective-permute-start | bytes 405512 | tf_op jit(solution)/shard_map/ppermute | solution.py:820
  27.1 12.3 %collective-permute-start.11 = (bf16[528,128]{1,0:T(8,128)(2,1)S(1)}, bf16[528,128]{1,0:T(8,128)(2,1)S(1)}, u32[]{:S(2)}, u32[]{:S(2)}) collective-permute-start(bf16[528,128]{1,0:T(8,128)(2,1)S(1)} %join.3), channel_id=1, source_target_pairs={{2,4},{3,5},{4,6},{5,7},{10,12},{11,13},{12,14},{13,15},{18,20},{1... | collective-permute-start | bytes 405512 | tf_op jit(solution)/shard_map/ppermute | solution.py:820
  28.4 11.0 %collective-permute-start.10 = (bf16[528,128]{1,0:T(8,128)(2,1)S(1)}, bf16[528,128]{1,0:T(8,128)(2,1)S(1)}, u32[]{:S(2)}, u32[]{:S(2)}) collective-permute-start(bf16[528,128]{1,0:T(8,128)(2,1)S(1)} %join.3), channel_id=1, source_target_pairs={{2,6},{3,7},{10,14},{11,15},{18,22},{19,23},{26,30},{27,31}} | collective-permute-start | bytes 405512 | tf_op jit(solution)/shard_map/ppermute | solution.py:820
  38.0 2.3 %collective-permute-start.12 = (bf16[128,512]{1,0:T(8,128)(2,1)S(1)}, bf16[128,512]{1,0:T(8,128)(2,1)S(1)}, u32[]{:S(2)}, u32[]{:S(2)}) collective-permute-start(bf16[128,512]{1,0:T(8,128)(2,1)S(1)} %get-tuple-element.91), channel_id=1, source_target_pairs={{0,1},{1,0},{2,3},{3,2},{4,5},{5,4},{6,7},{7,6},{8,9},{9,8},{10,11... | collective-permute-start | bytes 393224 | tf_op jit(solution)/shard_map/ppermute | solution.py:1069
  39.7 1.4 %collective-permute-start.13 = (bf16[128,512]{1,0:T(8,128)(2,1)S(1)}, bf16[128,512]{1,0:T(8,128)(2,1)S(1)}, u32[]{:S(2)}, u32[]{:S(2)}) collective-permute-start(bf16[128,512]{1,0:T(8,128)(2,1)S(1)} %get-tuple-element.92), channel_id=1, source_target_pairs={{0,1},{1,0},{2,3},{3,2},{4,5},{5,4},{6,7},{7,6},{8,9},{9,8},{10,11... | collective-permute-start | bytes 393224 | tf_op jit(solution)/shard_map/ppermute | solution.py:1069

commit v5 on v4

--- a/solution.py
+++ b/solution.py
@@ -730,7 +730,7 @@
 
 
 GROUPS = 2
-PIECES = 1
+PIECES = 2
 
 
 def per_device(
@@ -946,6 +946,8 @@
             if keeps:
                 shapes += [struct(square), struct(square), code_shape]
                 operands += fanned[group]
+            if level == 0 and group == 1:
+                after = ask(after)
             waits = [after]
             if level == 0 and group == GROUPS - 1:
                 waits += [query_other]

time: 42.3 us -> 41.7 us (0.986)
  starting transfers between devices: 18.5 us -> 17.2 us
  Pallas kernels: 21.6 us -> 22.3 us
    pallas_call x0 -> x1, Pallas kernels: none -> 1.56 us  [ask(): pl.pallas_call(functools.partial(asked_kernel, group, heads, piece * coun...]
    ppermute x6, starting transfers between devices: 11.3 us -> 9.93 us  [fan(): results.append(lax.ppermute(value, 'seq', route))]
    pallas_call x1, Pallas kernels: 6.5 us -> 5.64 us  [per_device(): pl.pallas_call(functools.partial(tail_kernel, level, 32 + 16 * (near + 1...]
  transfers between devices with their start and end apart: 14 -> 14, of which waited for: 3 -> 2; matrix products, arithmetic and copies ran while one was open for 0% -> 0% of each run, Pallas kernels for 41% -> 44%
where the time goes in v5:
time: 41.7 us; the launch traced here: 41.2 us
  Pallas kernels  22.3 us (53%)
  starting transfers between devices  17.2 us (41%)
  waiting for transfers between devices  1.32 us (3%)
    ppermute x6, starting transfers between devices, fan(): results.append(lax.ppermute(value, 'seq', route))  9.93 us
    pallas_call x2, Pallas kernels, per_device(): pl.pallas_call(functools.partial(lower_kernel, group, heads), out_shape=h...  6.87 us
    pallas_call x1, Pallas kernels, per_device(): pl.pallas_call(functools.partial(tail_kernel, level, 32 + 16 * (near + 1...  5.64 us
    pallas_call x1, Pallas kernels, per_device(): pl.pallas_call(upper_kernel, out_shape=held(8) + [struct((8, 128, 128))]...  4.32 us
    ppermute x1, starting transfers between devices, per_device(): lax.ppermute(halo, 'seq', [(i, i + 2) for i in range(1, size - 1, 2)])  3.19 us
    pallas_call x1, Pallas kernels, per_device(): pl.pallas_call(prepare_kernel, in_specs=[pl.BlockSpec(memory_space=pltpu....  1.71 us
    pallas_call x1, Pallas kernels, ask(): pl.pallas_call(functools.partial(asked_kernel, group, heads, piece * coun...  1.56 us
    ppermute x2, starting transfers between devices, per_device(): comes.append(lax.ppermute(leave, 'seq', cores))  1.48 us
  transfers between devices with their start and end apart: 14, of which 2 were waited for; matrix products, arithmetic and copies ran while one was open for 0% of the time, Pallas kernels for 44%

profile of v5, /device:TPU:11, one launch (start us, length us, event | category | flops | bytes accessed | tf_op | source)
XLA Modules:
  0.0 41.2 jit_solution(1172870620250218098)
XLA Ops:
  0.0 0.7 %collective-permute-start = (bf16[128,2048]{1,0:T(8,128)(2,1)}, bf16[128,2048]{1,0:T(8,128)(2,1)S(1)}, u32[]{:S(2)}, u32[]{:S(2)}) collective-permute-start(bf16[128,2048]{1,0:T(8,128)(2,1)} %key.1), channel_id=1, source_target_pairs={{0,1},{1,0},{2,3},{3,2},{4,5},{5,4},{6,7},{7,6},{8,9},{9,8},{10,11... | collective-permute-start | bytes 1572872 | tf_op jit(solution)/shard_map/ppermute | solution.py:760
  0.7 1.7 %prepare.1 = (bf16[128,1024]{1,0:T(8,128)(2,1)S(1)}, bf16[128,1024]{1,0:T(8,128)(2,1)S(1)}, bf16[128,1024]{1,0:T(8,128)(2,1)S(1)}, bf16[128,1024]{1,0:T(8,128)(2...) custom-call(bf16[128,2048]{1,0:T(8,128)(2,1)} %query.1, ...), custom_call_target="tpu_custom_call" | custom-call | tf_op jit(solution)/shard_map/prepare/pallas_call | solution.py:776
  2.4 0.6 %collective-permute-start.2 = (f32[208,128]{1,0:T(8,128)S(1)}, f32[208,128]{1,0:T(8,128)S(1)}, u32[]{:S(2)}, u32[]{:S(2)}) collective-permute-start(f32[208,128]{1,0:T(8,128)S(1)} %get-tuple-element.82.small_own.refs_5_.refs_7_.refs_2_.refs_3_), channel_id=1, source_target_pairs={{0,1},{1,0},{2,3},{3,2},{4,5},{5,4},{6,7},{7,6},{8,9},{9,8},{10,11... | collective-permute-start | bytes 319496 | tf_op jit(solution)/shard_map/ppermute | solution.py:804
  3.0 3.2 %collective-permute-start.4 = (bf16[16,2048]{1,0:T(8,128)(2,1)S(1)}, bf16[16,2048]{1,0:T(8,128)(2,1)S(1)}, u32[]{:S(2)}, u32[]{:S(2)}) collective-permute-start(bf16[16,2048]{1,0:T(8,128)(2,1)S(1)} %get-tuple-element.57), channel_id=1, source_target_pairs={{1,3},{3,5},{5,7},{9,11},{11,13},{13,15},{17,19},{19,21},{21,23},{... | collective-permute-start | bytes 196616 | tf_op jit(solution)/shard_map/ppermute | solution.py:806
  6.2 1.3 %collective-permute-start.3 = (bf16[16,2048]{1,0:T(8,128)(2,1)S(1)}, bf16[16,2048]{1,0:T(8,128)(2,1)S(1)}, u32[]{:S(2)}, u32[]{:S(2)}) collective-permute-start(bf16[16,2048]{1,0:T(8,128)(2,1)S(1)} %get-tuple-element.57), channel_id=1, source_target_pairs={{1,2},{3,4},{5,6},{9,10},{11,12},{13,14},{17,18},{19,20},{21,22},{... | collective-permute-start | bytes 196616 | tf_op jit(solution)/shard_map/ppermute | solution.py:805
  7.5 4.3 %upper.1 = (bf16[8,2,128,128]{3,2,1,0:T(8,128)(2,1)S(1)}, bf16[8,2,128,128]{3,2,1,0:T(8,128)(2,1)S(1)}, bf16[8,2,128,256]{3,2,1,0:T(8,128)(2,1)S(1)}, f32[8,128,128]{2,1,0:T(8,128)S(1)}, f32[8,128,128]{2,1,0:T(8,128)S(1)}) custom-call(bf16[128,1024]{1,0:T(8,128)(2,1)S(1)} %get-tuple-element.51.key_own, bf16[128,2048]{1,0:T(8,128)(2,1)S(1)} %collective-permute-done.key_other, ...), custom_call_target="tpu_custom_call" | custom-call | flops 4000000000 | bytes 1000000 | tf_op jit(solution)/shard_map/upper/pallas_call | solution.py:832
  11.8 3.4 %lower.2 = (bf16[4,2,128,128]{3,2,1,0:T(8,128)(2,1)S(1)}, bf16[4,2,128,128]{3,2,1,0:T(8,128)(2,1)S(1)}, bf16[4,2,128,256]{3,2,1,0:T(8,128)(2,1)S(1)}, f32[4,128,...) custom-call(bf16[128,1024]{1,0:T(8,128)(2,1)S(1)} %get-tuple-element, ...), custom_call_target="tpu_custom_call" | custom-call | flops 2500000000 | bytes 1000000 | tf_op jit(solution)/shard_map/lower/pallas_call | solution.py:854
  15.3 1.3 %collective-permute-start.5 = (bf16[528,128]{1,0:T(8,128)(2,1)S(1)}, bf16[528,128]{1,0:T(8,128)(2,1)S(1)}, u32[]{:S(2)}, u32[]{:S(2)}) collective-permute-start(bf16[528,128]{1,0:T(8,128)(2,1)S(1)} %get-tuple-element.60), channel_id=1, source_target_pairs={{0,2},{1,3},{4,6},{5,7},{8,10},{9,11},{12,14},{13,15},{16,18},{17,... | collective-permute-start | bytes 405512 | tf_op jit(solution)/shard_map/ppermute | solution.py:820
  16.7 3.4 %lower.3 = (bf16[4,2,128,128]{3,2,1,0:T(8,128)(2,1)S(1)}, bf16[4,2,128,128]{3,2,1,0:T(8,128)(2,1)S(1)}, bf16[4,2,128,256]{3,2,1,0:T(8,128)(2,1)S(1)}, f32[4,128,...) custom-call(bf16[128,1024]{1,0:T(8,128)(2,1)S(1)} %get-tuple-element, ...), custom_call_target="tpu_custom_call" | custom-call | flops 2500000000 | bytes 1000000 | tf_op jit(solution)/shard_map/lower/pallas_call | solution.py:854
  20.1 1.3 %collective-permute-start.9 = (bf16[528,128]{1,0:T(8,128)(2,1)S(1)}, bf16[528,128]{1,0:T(8,128)(2,1)S(1)}, u32[]{:S(2)}, u32[]{:S(2)}) collective-permute-start(bf16[528,128]{1,0:T(8,128)(2,1)S(1)} %get-tuple-element.62.refs_0_), channel_id=1, source_target_pairs={{0,2},{1,3},{4,6},{5,7},{8,10},{9,11},{12,14},{13,15},{16,18},{17,... | collective-permute-start | bytes 405512 | tf_op jit(solution)/shard_map/ppermute | solution.py:820
  21.4 0.4 join.2.after
  21.8 3.2 %collective-permute-start.7 = (bf16[528,128]{1,0:T(8,128)(2,1)S(1)}, bf16[528,128]{1,0:T(8,128)(2,1)S(1)}, u32[]{:S(2)}, u32[]{:S(2)}) collective-permute-start(bf16[528,128]{1,0:T(8,128)(2,1)S(1)} %join.2.after), channel_id=1, source_target_pairs={{2,4},{3,5},{4,6},{5,7},{10,12},{11,13},{12,14},{13,15},{18,20},{1... | collective-permute-start | bytes 405512 | tf_op jit(solution)/shard_map/ppermute | solution.py:820
  25.1 1.5 %collective-permute-start.6 = (bf16[528,128]{1,0:T(8,128)(2,1)S(1)}, bf16[528,128]{1,0:T(8,128)(2,1)S(1)}, u32[]{:S(2)}, u32[]{:S(2)}) collective-permute-start(bf16[528,128]{1,0:T(8,128)(2,1)S(1)} %join.2.after), channel_id=1, source_target_pairs={{2,6},{3,7},{10,14},{11,15},{18,22},{19,23},{26,30},{27,31}} | collective-permute-start | bytes 405512 | tf_op jit(solution)/shard_map/ppermute | solution.py:820
  26.6 1.6 %queries.1 = (f32[2,256,128]{2,1,0:T(8,128)S(1)}, f32[2,256,128]{2,1,0:T(8,128)S(1)}) custom-call(bf16[528,128]{1,0:T(8,128)(2,1)S(1)} %join.2.after, bf16[128,1024]{1,0:T(8,128)(2,1)S(1)} %get-tuple-element.69.refs_0_.refs_2_, bf16[128,2048]{1,0:T(8,128)(2,1)S(1)} %collective-permute-done.8.refs_1_.refs_3_.refs_5_.refs_6_, ...), custom_call_target="tpu_custom_call" | custom-call | flops 1000000 | bytes 1000000 | tf_op jit(solution)/shard_map/queries/pallas_call | solution.py:906
  28.2 0.4 join.3
  28.6 1.3 %collective-permute-start.11 = (bf16[528,128]{1,0:T(8,128)(2,1)S(1)}, bf16[528,128]{1,0:T(8,128)(2,1)S(1)}, u32[]{:S(2)}, u32[]{:S(2)}) collective-permute-start(bf16[528,128]{1,0:T(8,128)(2,1)S(1)} %join.3), channel_id=1, source_target_pairs={{2,4},{3,5},{4,6},{5,7},{10,12},{11,13},{12,14},{13,15},{18,20},{1... | collective-permute-start | bytes 405512 | tf_op jit(solution)/shard_map/ppermute | solution.py:820
  29.9 1.3 %collective-permute-start.10 = (bf16[528,128]{1,0:T(8,128)(2,1)S(1)}, bf16[528,128]{1,0:T(8,128)(2,1)S(1)}, u32[]{:S(2)}, u32[]{:S(2)}) collective-permute-start(bf16[528,128]{1,0:T(8,128)(2,1)S(1)} %join.3), channel_id=1, source_target_pairs={{2,6},{3,7},{10,14},{11,15},{18,22},{19,23},{26,30},{27,31}} | collective-permute-start | bytes 405512 | tf_op jit(solution)/shard_map/ppermute | solution.py:820
  31.2 5.6 %tail.1 = (f32[4,256,128]{2,1,0:T(8,128)S(1)}, f32[4,256,128]{2,1,0:T(8,128)S(1)}, f32[4,256,128]{2,1,0:T(8,128)S(1)}, f32[4,256,128]{2,1,0:T(8,128)S(1)}) custom-call(bf16[528,128]{1,0:T(8,128)(2,1)S(1)} %collective-permute-done.5.refs_1_.refs_0_, bf16[528,128]{1,0:T(8,128)(2,1)S(1)} %collective-permute-done.9.refs_2_.refs_1_, ...), custom_call_target="tpu_custom_call" | custom-call | flops 1000000 | bytes 1000000 | tf_op jit(solution)/shard_map/tail/pallas_call | solution.py:981
  36.9 0.3 finish.2
  37.2 1.4 %collective-permute-start.12 = (bf16[128,512]{1,0:T(8,128)(2,1)S(1)}, bf16[128,512]{1,0:T(8,128)(2,1)S(1)}, u32[]{:S(2)}, u32[]{:S(2)}) collective-permute-start(bf16[128,512]{1,0:T(8,128)(2,1)S(1)} %get-tuple-element.95), channel_id=1, source_target_pairs={{0,1},{1,0},{2,3},{3,2},{4,5},{5,4},{6,7},{7,6},{8,9},{9,8},{10,11... | collective-permute-start | bytes 393224 | tf_op jit(solution)/shard_map/ppermute | solution.py:1071
  38.5 0.3 finish.3
  39.0 0.6 %collective-permute-done.12.refs_2_ = bf16[128,512]{1,0:T(8,128)(2,1)S(1)} collective-permute-done((bf16[128,512]{1,0:T(8,128)(2,1)S(1)}, bf16[128,512]{1,0:T(8,128)(2,1)S(1)}, u32[]{:S(2)}, u32[]{:S(2)}) %collective-permute-start.12) | collective-permute-done | bytes 131104 | tf_op jit(solution)/shard_map/ppermute | solution.py:1071
  39.5 0.7 %collective-permute-done.13.refs_3_ = bf16[128,512]{1,0:T(8,128)(2,1)S(1)} collective-permute-done((bf16[128,512]{1,0:T(8,128)(2,1)S(1)}, bf16[128,512]{1,0:T(8,128)(2,1)S(1)}, u32[]{:S(2)}, u32[]{:S(2)}) %collective-permute-start.13) | collective-permute-done | bytes 131104 | tf_op jit(solution)/shard_map/ppermute | solution.py:1071
  40.3 0.8 %swap.1 = bf16[128,2048]{1,0:T(8,128)(2,1)} custom-call(bf16[128,512]{1,0:T(8,128)(2,1)S(1)} %get-tuple-element.91.refs_0_, bf16[128,512]{1,0:T(8,128)(2,1)S(1)} %get-tuple-element.94.refs_1_, bf16[128,512]{1,0:T(8,128)(2,1)S(1)} %collective-permute-done.12.refs_2_, bf16[128,512]{1,0:T(8,128)(2,1)S(1)} %collective-permute-done.13.refs_3_), custom_call_target="tpu_custom_call" | custom-call | tf_op jit(solution)/shard_map/swap/pallas_call | solution.py:1072
  (15 shorter events, 0.2 us)
Async XLA Ops:
  0.0 7.5 %collective-permute-start = (bf16[128,2048]{1,0:T(8,128)(2,1)}, bf16[128,2048]{1,0:T(8,128)(2,1)S(1)}, u32[]{:S(2)}, u32[]{:S(2)}) collective-permute-start(bf16[128,2048]{1,0:T(8,128)(2,1)} %key.1), channel_id=1, source_target_pairs={{0,1},{1,0},{2,3},{3,2},{4,5},{5,4},{6,7},{7,6},{8,9},{9,8},{10,11... | collective-permute-start | bytes 1572872 | tf_op jit(solution)/shard_map/ppermute | solution.py:760
  0.7 6.8 %collective-permute-start.1 = (bf16[128,2048]{1,0:T(8,128)(2,1)}, bf16[128,2048]{1,0:T(8,128)(2,1)S(1)}, u32[]{:S(2)}, u32[]{:S(2)}) collective-permute-start(bf16[128,2048]{1,0:T(8,128)(2,1)} %value.1), channel_id=1, source_target_pairs={{0,1},{1,0},{2,3},{3,2},{4,5},{5,4},{6,7},{7,6},{8,9},{9,8},{10,11... | collective-permute-start | bytes 1572872 | tf_op jit(solution)/shard_map/ppermute | solution.py:761
  2.4 5.1 %collective-permute-start.2 = (f32[208,128]{1,0:T(8,128)S(1)}, f32[208,128]{1,0:T(8,128)S(1)}, u32[]{:S(2)}, u32[]{:S(2)}) collective-permute-start(f32[208,128]{1,0:T(8,128)S(1)} %get-tuple-element.82.small_own.refs_5_.refs_7_.refs_2_.refs_3_), channel_id=1, source_target_pairs={{0,1},{1,0},{2,3},{3,2},{4,5},{5,4},{6,7},{7,6},{8,9},{9,8},{10,11... | collective-permute-start | bytes 319496 | tf_op jit(solution)/shard_map/ppermute | solution.py:804
  3.0 8.9 %collective-permute-start.4 = (bf16[16,2048]{1,0:T(8,128)(2,1)S(1)}, bf16[16,2048]{1,0:T(8,128)(2,1)S(1)}, u32[]{:S(2)}, u32[]{:S(2)}) collective-permute-start(bf16[16,2048]{1,0:T(8,128)(2,1)S(1)} %get-tuple-element.57), channel_id=1, source_target_pairs={{1,3},{3,5},{5,7},{9,11},{11,13},{13,15},{17,19},{19,21},{21,23},{... | collective-permute-start | bytes 196616 | tf_op jit(solution)/shard_map/ppermute | solution.py:806
  6.2 5.7 %collective-permute-start.3 = (bf16[16,2048]{1,0:T(8,128)(2,1)S(1)}, bf16[16,2048]{1,0:T(8,128)(2,1)S(1)}, u32[]{:S(2)}, u32[]{:S(2)}) collective-permute-start(bf16[16,2048]{1,0:T(8,128)(2,1)S(1)} %get-tuple-element.57), channel_id=1, source_target_pairs={{1,2},{3,4},{5,6},{9,10},{11,12},{13,14},{17,18},{19,20},{21,22},{... | collective-permute-start | bytes 196616 | tf_op jit(solution)/shard_map/ppermute | solution.py:805
  15.3 6.1 %collective-permute-start.5 = (bf16[528,128]{1,0:T(8,128)(2,1)S(1)}, bf16[528,128]{1,0:T(8,128)(2,1)S(1)}, u32[]{:S(2)}, u32[]{:S(2)}) collective-permute-start(bf16[528,128]{1,0:T(8,128)(2,1)S(1)} %get-tuple-element.60), channel_id=1, source_target_pairs={{0,2},{1,3},{4,6},{5,7},{8,10},{9,11},{12,14},{13,15},{16,18},{17,... | collective-permute-start | bytes 405512 | tf_op jit(solution)/shard_map/ppermute | solution.py:820
  16.6 10.0 %collective-permute-start.8 = (bf16[128,2048]{1,0:T(8,128)(2,1)S(1)}, bf16[128,2048]{1,0:T(8,128)(2,1)S(1)}, u32[]{:S(2)}, u32[]{:S(2)}) collective-permute-start(bf16[128,2048]{1,0:T(8,128)(2,1)S(1)} %get-tuple-element.67), channel_id=1, source_target_pairs={{0,1},{1,0},{2,3},{3,2},{4,5},{5,4},{6,7},{7,6},{8,9},{9,8},{10,11... | collective-permute-start | bytes 1572872 | tf_op jit(solution)/shard_map/ppermute | solution.py:881
  20.1 8.0 %collective-permute-start.9 = (bf16[528,128]{1,0:T(8,128)(2,1)S(1)}, bf16[528,128]{1,0:T(8,128)(2,1)S(1)}, u32[]{:S(2)}, u32[]{:S(2)}) collective-permute-start(bf16[528,128]{1,0:T(8,128)(2,1)S(1)} %get-tuple-element.62.refs_0_), channel_id=1, source_target_pairs={{0,2},{1,3},{4,6},{5,7},{8,10},{9,11},{12,14},{13,15},{16,18},{17,... | collective-permute-start | bytes 405512 | tf_op jit(solution)/shard_map/ppermute | solution.py:820
  21.8 15.0 %collective-permute-start.7 = (bf16[528,128]{1,0:T(8,128)(2,1)S(1)}, bf16[528,128]{1,0:T(8,128)(2,1)S(1)}, u32[]{:S(2)}, u32[]{:S(2)}) collective-permute-start(bf16[528,128]{1,0:T(8,128)(2,1)S(1)} %join.2.after), channel_id=1, source_target_pairs={{2,4},{3,5},{4,6},{5,7},{10,12},{11,13},{12,14},{13,15},{18,20},{1... | collective-permute-start | bytes 405512 | tf_op jit(solution)/shard_map/ppermute | solution.py:820
  25.1 11.8 %collective-permute-start.6 = (bf16[528,128]{1,0:T(8,128)(2,1)S(1)}, bf16[528,128]{1,0:T(8,128)(2,1)S(1)}, u32[]{:S(2)}, u32[]{:S(2)}) collective-permute-start(bf16[528,128]{1,0:T(8,128)(2,1)S(1)} %join.2.after), channel_id=1, source_target_pairs={{2,6},{3,7},{10,14},{11,15},{18,22},{19,23},{26,30},{27,31}} | collective-permute-start | bytes 405512 | tf_op jit(solution)/shard_map/ppermute | solution.py:820
  28.6 10.0 %collective-permute-start.11 = (bf16[528,128]{1,0:T(8,128)(2,1)S(1)}, bf16[528,128]{1,0:T(8,128)(2,1)S(1)}, u32[]{:S(2)}, u32[]{:S(2)}) collective-permute-start(bf16[528,128]{1,0:T(8,128)(2,1)S(1)} %join.3), channel_id=1, source_target_pairs={{2,4},{3,5},{4,6},{5,7},{10,12},{11,13},{12,14},{13,15},{18,20},{1... | collective-permute-start | bytes 405512 | tf_op jit(solution)/shard_map/ppermute | solution.py:820
  29.9 8.7 %collective-permute-start.10 = (bf16[528,128]{1,0:T(8,128)(2,1)S(1)}, bf16[528,128]{1,0:T(8,128)(2,1)S(1)}, u32[]{:S(2)}, u32[]{:S(2)}) collective-permute-start(bf16[528,128]{1,0:T(8,128)(2,1)S(1)} %join.3), channel_id=1, source_target_pairs={{2,6},{3,7},{10,14},{11,15},{18,22},{19,23},{26,30},{27,31}} | collective-permute-start | bytes 405512 | tf_op jit(solution)/shard_map/ppermute | solution.py:820
  37.2 2.3 %collective-permute-start.12 = (bf16[128,512]{1,0:T(8,128)(2,1)S(1)}, bf16[128,512]{1,0:T(8,128)(2,1)S(1)}, u32[]{:S(2)}, u32[]{:S(2)}) collective-permute-start(bf16[128,512]{1,0:T(8,128)(2,1)S(1)} %get-tuple-element.95), channel_id=1, source_target_pairs={{0,1},{1,0},{2,3},{3,2},{4,5},{5,4},{6,7},{7,6},{8,9},{9,8},{10,11... | collective-permute-start | bytes 393224 | tf_op jit(solution)/shard_map/ppermute | solution.py:1071
  38.8 1.4 %collective-permute-start.13 = (bf16[128,512]{1,0:T(8,128)(2,1)S(1)}, bf16[128,512]{1,0:T(8,128)(2,1)S(1)}, u32[]{:S(2)}, u32[]{:S(2)}) collective-permute-start(bf16[128,512]{1,0:T(8,128)(2,1)S(1)} %get-tuple-element.96), channel_id=1, source_target_pairs={{0,1},{1,0},{2,3},{3,2},{4,5},{5,4},{6,7},{7,6},{8,9},{9,8},{10,11... | collective-permute-start | bytes 393224 | tf_op jit(solution)/shard_map/ppermute | solution.py:1071

commit v6 on v5

--- a/solution.py
+++ b/solution.py
@@ -123,22 +123,19 @@
 def invert(coupling, t, j):
     apart = t ^ j
     count = len(coupling)
-    near = [split(jnp.where(apart < 8, -a, 0.0)) for a in coupling]
+    near = [split(jnp.where(apart < 16, -a, 0.0)) for a in coupling]
     eye = (t == j).astype(F32)
-    squared = [mm(n, n) for n in near]
-    grown = []
-    fourth = []
-    for i in range(count):
-        base = eye + near[i][0].astype(F32) + near[i][1].astype(F32)
-        left = split(jnp.concatenate([squared[i], base], axis=0))
-        both = mm(left, split(squared[i]))
-        fourth.append(both[:CHUNK])
-        grown.append(base + both[CHUNK:])
-    inverse = [
-        grown[i] + mm(split(grown[i]), split(fourth[i])) for i in range(count)
-    ]
-    inverse = [split(x) for x in inverse]
-    size = 8
+    powers = [split(mm(n, n)) for n in near]
+    grown = [eye + n[0].astype(F32) + n[1].astype(F32) for n in near]
+    for _ in range(2):
+        for i in range(count):
+            base = split(grown[i])
+            left = tuple(jnp.concatenate([powers[i][k], base[k]], axis=0) for k in range(2))
+            both = mm(left, powers[i])
+            powers[i] = split(both[:CHUNK])
+            grown[i] = grown[i] + both[CHUNK:]
+    inverse = [split(grown[i] + mm(split(grown[i]), powers[i])) for i in range(count)]
+    size = 16
     while size < CHUNK:
         starts = range(size, CHUNK, 2 * size)
 

time: 41.7 us -> 41.5 us (level)
  no operation moved by 1% of the time
where the time goes in v6:
time: 41.5 us; the launch traced here: 41 us
  Pallas kernels  22.1 us (53%)
  starting transfers between devices  17.2 us (41%)
  waiting for transfers between devices  1.32 us (3%)
    ppermute x6, starting transfers between devices, fan(): results.append(lax.ppermute(value, 'seq', route))  9.93 us
    pallas_call x2, Pallas kernels, per_device(): pl.pallas_call(functools.partial(lower_kernel, group, heads), out_shape=h...  6.62 us
    pallas_call x1, Pallas kernels, per_device(): pl.pallas_call(functools.partial(tail_kernel, level, 32 + 16 * (near + 1...  5.65 us
    pallas_call x1, Pallas kernels, per_device(): pl.pallas_call(upper_kernel, out_shape=held(8) + [struct((8, 128, 128))]...  4.32 us
    ppermute x1, starting transfers between devices, per_device(): lax.ppermute(halo, 'seq', [(i, i + 2) for i in range(1, size - 1, 2)])  3.19 us
    pallas_call x1, Pallas kernels, per_device(): pl.pallas_call(prepare_kernel, in_specs=[pl.BlockSpec(memory_space=pltpu....  1.71 us
    pallas_call x1, Pallas kernels, ask(): pl.pallas_call(functools.partial(asked_kernel, group, heads, piece * coun...  1.56 us
    ppermute x2, starting transfers between devices, per_device(): comes.append(lax.ppermute(leave, 'seq', cores))  1.47 us
  transfers between devices with their start and end apart: 14, of which 2 were waited for; matrix products, arithmetic and copies ran while one was open for 0% of the time, Pallas kernels for 44%

profile of v6, /device:TPU:11, one launch (start us, length us, event | category | flops | bytes accessed | tf_op | source)
XLA Modules:
  0.0 41.0 jit_solution(5885028438096894817)
XLA Ops:
  0.0 0.7 %collective-permute-start = (bf16[128,2048]{1,0:T(8,128)(2,1)}, bf16[128,2048]{1,0:T(8,128)(2,1)S(1)}, u32[]{:S(2)}, u32[]{:S(2)}) collective-permute-start(bf16[128,2048]{1,0:T(8,128)(2,1)} %key.1), channel_id=1, source_target_pairs={{0,1},{1,0},{2,3},{3,2},{4,5},{5,4},{6,7},{7,6},{8,9},{9,8},{10,11... | collective-permute-start | bytes 1572872 | tf_op jit(solution)/shard_map/ppermute | solution.py:757
  0.7 1.7 %prepare.1 = (bf16[128,1024]{1,0:T(8,128)(2,1)S(1)}, bf16[128,1024]{1,0:T(8,128)(2,1)S(1)}, bf16[128,1024]{1,0:T(8,128)(2,1)S(1)}, bf16[128,1024]{1,0:T(8,128)(2...) custom-call(bf16[128,2048]{1,0:T(8,128)(2,1)} %query.1, ...), custom_call_target="tpu_custom_call" | custom-call | tf_op jit(solution)/shard_map/prepare/pallas_call | solution.py:773
  2.4 0.6 %collective-permute-start.2 = (f32[208,128]{1,0:T(8,128)S(1)}, f32[208,128]{1,0:T(8,128)S(1)}, u32[]{:S(2)}, u32[]{:S(2)}) collective-permute-start(f32[208,128]{1,0:T(8,128)S(1)} %get-tuple-element.82.small_own.refs_5_.refs_7_.refs_2_.refs_3_), channel_id=1, source_target_pairs={{0,1},{1,0},{2,3},{3,2},{4,5},{5,4},{6,7},{7,6},{8,9},{9,8},{10,11... | collective-permute-start | bytes 319496 | tf_op jit(solution)/shard_map/ppermute | solution.py:801
  3.0 3.2 %collective-permute-start.4 = (bf16[16,2048]{1,0:T(8,128)(2,1)S(1)}, bf16[16,2048]{1,0:T(8,128)(2,1)S(1)}, u32[]{:S(2)}, u32[]{:S(2)}) collective-permute-start(bf16[16,2048]{1,0:T(8,128)(2,1)S(1)} %get-tuple-element.57), channel_id=1, source_target_pairs={{1,3},{3,5},{5,7},{9,11},{11,13},{13,15},{17,19},{19,21},{21,23},{... | collective-permute-start | bytes 196616 | tf_op jit(solution)/shard_map/ppermute | solution.py:803
  6.2 1.3 %collective-permute-start.3 = (bf16[16,2048]{1,0:T(8,128)(2,1)S(1)}, bf16[16,2048]{1,0:T(8,128)(2,1)S(1)}, u32[]{:S(2)}, u32[]{:S(2)}) collective-permute-start(bf16[16,2048]{1,0:T(8,128)(2,1)S(1)} %get-tuple-element.57), channel_id=1, source_target_pairs={{1,2},{3,4},{5,6},{9,10},{11,12},{13,14},{17,18},{19,20},{21,22},{... | collective-permute-start | bytes 196616 | tf_op jit(solution)/shard_map/ppermute | solution.py:802
  7.5 4.3 %upper.1 = (bf16[8,2,128,128]{3,2,1,0:T(8,128)(2,1)S(1)}, bf16[8,2,128,128]{3,2,1,0:T(8,128)(2,1)S(1)}, bf16[8,2,128,256]{3,2,1,0:T(8,128)(2,1)S(1)}, f32[8,128,128]{2,1,0:T(8,128)S(1)}, f32[8,128,128]{2,1,0:T(8,128)S(1)}) custom-call(bf16[128,1024]{1,0:T(8,128)(2,1)S(1)} %get-tuple-element.51.key_own, bf16[128,2048]{1,0:T(8,128)(2,1)S(1)} %collective-permute-done.key_other, ...), custom_call_target="tpu_custom_call" | custom-call | flops 4000000000 | bytes 1000000 | tf_op jit(solution)/shard_map/upper/pallas_call | solution.py:829
  11.8 3.3 %lower.2 = (bf16[4,2,128,128]{3,2,1,0:T(8,128)(2,1)S(1)}, bf16[4,2,128,128]{3,2,1,0:T(8,128)(2,1)S(1)}, bf16[4,2,128,256]{3,2,1,0:T(8,128)(2,1)S(1)}, f32[4,128,...) custom-call(bf16[128,1024]{1,0:T(8,128)(2,1)S(1)} %get-tuple-element, ...), custom_call_target="tpu_custom_call" | custom-call | flops 2500000000 | bytes 1000000 | tf_op jit(solution)/shard_map/lower/pallas_call | solution.py:851
  15.2 1.3 %collective-permute-start.5 = (bf16[528,128]{1,0:T(8,128)(2,1)S(1)}, bf16[528,128]{1,0:T(8,128)(2,1)S(1)}, u32[]{:S(2)}, u32[]{:S(2)}) collective-permute-start(bf16[528,128]{1,0:T(8,128)(2,1)S(1)} %get-tuple-element.60), channel_id=1, source_target_pairs={{0,2},{1,3},{4,6},{5,7},{8,10},{9,11},{12,14},{13,15},{16,18},{17,... | collective-permute-start | bytes 405512 | tf_op jit(solution)/shard_map/ppermute | solution.py:817
  16.5 3.3 %lower.3 = (bf16[4,2,128,128]{3,2,1,0:T(8,128)(2,1)S(1)}, bf16[4,2,128,128]{3,2,1,0:T(8,128)(2,1)S(1)}, bf16[4,2,128,256]{3,2,1,0:T(8,128)(2,1)S(1)}, f32[4,128,...) custom-call(bf16[128,1024]{1,0:T(8,128)(2,1)S(1)} %get-tuple-element, ...), custom_call_target="tpu_custom_call" | custom-call | flops 2500000000 | bytes 1000000 | tf_op jit(solution)/shard_map/lower/pallas_call | solution.py:851
  19.9 1.3 %collective-permute-start.9 = (bf16[528,128]{1,0:T(8,128)(2,1)S(1)}, bf16[528,128]{1,0:T(8,128)(2,1)S(1)}, u32[]{:S(2)}, u32[]{:S(2)}) collective-permute-start(bf16[528,128]{1,0:T(8,128)(2,1)S(1)} %get-tuple-element.62.refs_0_), channel_id=1, source_target_pairs={{0,2},{1,3},{4,6},{5,7},{8,10},{9,11},{12,14},{13,15},{16,18},{17,... | collective-permute-start | bytes 405512 | tf_op jit(solution)/shard_map/ppermute | solution.py:817
  21.2 0.4 join.2.after
  21.6 3.2 %collective-permute-start.7 = (bf16[528,128]{1,0:T(8,128)(2,1)S(1)}, bf16[528,128]{1,0:T(8,128)(2,1)S(1)}, u32[]{:S(2)}, u32[]{:S(2)}) collective-permute-start(bf16[528,128]{1,0:T(8,128)(2,1)S(1)} %join.2.after), channel_id=1, source_target_pairs={{2,4},{3,5},{4,6},{5,7},{10,12},{11,13},{12,14},{13,15},{18,20},{1... | collective-permute-start | bytes 405512 | tf_op jit(solution)/shard_map/ppermute | solution.py:817
  24.8 1.5 %collective-permute-start.6 = (bf16[528,128]{1,0:T(8,128)(2,1)S(1)}, bf16[528,128]{1,0:T(8,128)(2,1)S(1)}, u32[]{:S(2)}, u32[]{:S(2)}) collective-permute-start(bf16[528,128]{1,0:T(8,128)(2,1)S(1)} %join.2.after), channel_id=1, source_target_pairs={{2,6},{3,7},{10,14},{11,15},{18,22},{19,23},{26,30},{27,31}} | collective-permute-start | bytes 405512 | tf_op jit(solution)/shard_map/ppermute | solution.py:817
  26.3 1.6 %queries.1 = (f32[2,256,128]{2,1,0:T(8,128)S(1)}, f32[2,256,128]{2,1,0:T(8,128)S(1)}) custom-call(bf16[528,128]{1,0:T(8,128)(2,1)S(1)} %join.2.after, bf16[128,1024]{1,0:T(8,128)(2,1)S(1)} %get-tuple-element.69.refs_0_.refs_2_, bf16[128,2048]{1,0:T(8,128)(2,1)S(1)} %collective-permute-done.8.refs_1_.refs_3_.refs_5_.refs_6_, ...), custom_call_target="tpu_custom_call" | custom-call | flops 1000000 | bytes 1000000 | tf_op jit(solution)/shard_map/queries/pallas_call | solution.py:903
  27.9 0.4 join.3
  28.3 1.3 %collective-permute-start.11 = (bf16[528,128]{1,0:T(8,128)(2,1)S(1)}, bf16[528,128]{1,0:T(8,128)(2,1)S(1)}, u32[]{:S(2)}, u32[]{:S(2)}) collective-permute-start(bf16[528,128]{1,0:T(8,128)(2,1)S(1)} %join.3), channel_id=1, source_target_pairs={{2,4},{3,5},{4,6},{5,7},{10,12},{11,13},{12,14},{13,15},{18,20},{1... | collective-permute-start | bytes 405512 | tf_op jit(solution)/shard_map/ppermute | solution.py:817
  29.6 1.3 %collective-permute-start.10 = (bf16[528,128]{1,0:T(8,128)(2,1)S(1)}, bf16[528,128]{1,0:T(8,128)(2,1)S(1)}, u32[]{:S(2)}, u32[]{:S(2)}) collective-permute-start(bf16[528,128]{1,0:T(8,128)(2,1)S(1)} %join.3), channel_id=1, source_target_pairs={{2,6},{3,7},{10,14},{11,15},{18,22},{19,23},{26,30},{27,31}} | collective-permute-start | bytes 405512 | tf_op jit(solution)/shard_map/ppermute | solution.py:817
  31.0 5.6 %tail.1 = (f32[4,256,128]{2,1,0:T(8,128)S(1)}, f32[4,256,128]{2,1,0:T(8,128)S(1)}, f32[4,256,128]{2,1,0:T(8,128)S(1)}, f32[4,256,128]{2,1,0:T(8,128)S(1)}) custom-call(bf16[528,128]{1,0:T(8,128)(2,1)S(1)} %collective-permute-done.5.refs_1_.refs_0_, bf16[528,128]{1,0:T(8,128)(2,1)S(1)} %collective-permute-done.9.refs_2_.refs_1_, ...), custom_call_target="tpu_custom_call" | custom-call | flops 1000000 | bytes 1000000 | tf_op jit(solution)/shard_map/tail/pallas_call | solution.py:978
  36.6 0.3 finish.2
  36.9 1.3 %collective-permute-start.12 = (bf16[128,512]{1,0:T(8,128)(2,1)S(1)}, bf16[128,512]{1,0:T(8,128)(2,1)S(1)}, u32[]{:S(2)}, u32[]{:S(2)}) collective-permute-start(bf16[128,512]{1,0:T(8,128)(2,1)S(1)} %get-tuple-element.95), channel_id=1, source_target_pairs={{0,1},{1,0},{2,3},{3,2},{4,5},{5,4},{6,7},{7,6},{8,9},{9,8},{10,11... | collective-permute-start | bytes 393224 | tf_op jit(solution)/shard_map/ppermute | solution.py:1068
  38.3 0.3 finish.3
  38.7 0.6 %collective-permute-done.12.refs_2_ = bf16[128,512]{1,0:T(8,128)(2,1)S(1)} collective-permute-done((bf16[128,512]{1,0:T(8,128)(2,1)S(1)}, bf16[128,512]{1,0:T(8,128)(2,1)S(1)}, u32[]{:S(2)}, u32[]{:S(2)}) %collective-permute-start.12) | collective-permute-done | bytes 131104 | tf_op jit(solution)/shard_map/ppermute | solution.py:1068
  39.3 0.7 %collective-permute-done.13.refs_3_ = bf16[128,512]{1,0:T(8,128)(2,1)S(1)} collective-permute-done((bf16[128,512]{1,0:T(8,128)(2,1)S(1)}, bf16[128,512]{1,0:T(8,128)(2,1)S(1)}, u32[]{:S(2)}, u32[]{:S(2)}) %collective-permute-start.13) | collective-permute-done | bytes 131104 | tf_op jit(solution)/shard_map/ppermute | solution.py:1068
  40.0 0.8 %swap.1 = bf16[128,2048]{1,0:T(8,128)(2,1)} custom-call(bf16[128,512]{1,0:T(8,128)(2,1)S(1)} %get-tuple-element.91.refs_0_, bf16[128,512]{1,0:T(8,128)(2,1)S(1)} %get-tuple-element.94.refs_1_, bf16[128,512]{1,0:T(8,128)(2,1)S(1)} %collective-permute-done.12.refs_2_, bf16[128,512]{1,0:T(8,128)(2,1)S(1)} %collective-permute-done.13.refs_3_), custom_call_target="tpu_custom_call" | custom-call | tf_op jit(solution)/shard_map/swap/pallas_call | solution.py:1069
  (15 shorter events, 0.2 us)
Async XLA Ops:
  0.0 7.5 %collective-permute-start = (bf16[128,2048]{1,0:T(8,128)(2,1)}, bf16[128,2048]{1,0:T(8,128)(2,1)S(1)}, u32[]{:S(2)}, u32[]{:S(2)}) collective-permute-start(bf16[128,2048]{1,0:T(8,128)(2,1)} %key.1), channel_id=1, source_target_pairs={{0,1},{1,0},{2,3},{3,2},{4,5},{5,4},{6,7},{7,6},{8,9},{9,8},{10,11... | collective-permute-start | bytes 1572872 | tf_op jit(solution)/shard_map/ppermute | solution.py:757
  0.7 6.8 %collective-permute-start.1 = (bf16[128,2048]{1,0:T(8,128)(2,1)}, bf16[128,2048]{1,0:T(8,128)(2,1)S(1)}, u32[]{:S(2)}, u32[]{:S(2)}) collective-permute-start(bf16[128,2048]{1,0:T(8,128)(2,1)} %value.1), channel_id=1, source_target_pairs={{0,1},{1,0},{2,3},{3,2},{4,5},{5,4},{6,7},{7,6},{8,9},{9,8},{10,11... | collective-permute-start | bytes 1572872 | tf_op jit(solution)/shard_map/ppermute | solution.py:758
  2.4 5.1 %collective-permute-start.2 = (f32[208,128]{1,0:T(8,128)S(1)}, f32[208,128]{1,0:T(8,128)S(1)}, u32[]{:S(2)}, u32[]{:S(2)}) collective-permute-start(f32[208,128]{1,0:T(8,128)S(1)} %get-tuple-element.82.small_own.refs_5_.refs_7_.refs_2_.refs_3_), channel_id=1, source_target_pairs={{0,1},{1,0},{2,3},{3,2},{4,5},{5,4},{6,7},{7,6},{8,9},{9,8},{10,11... | collective-permute-start | bytes 319496 | tf_op jit(solution)/shard_map/ppermute | solution.py:801
  3.0 8.9 %collective-permute-start.4 = (bf16[16,2048]{1,0:T(8,128)(2,1)S(1)}, bf16[16,2048]{1,0:T(8,128)(2,1)S(1)}, u32[]{:S(2)}, u32[]{:S(2)}) collective-permute-start(bf16[16,2048]{1,0:T(8,128)(2,1)S(1)} %get-tuple-element.57), channel_id=1, source_target_pairs={{1,3},{3,5},{5,7},{9,11},{11,13},{13,15},{17,19},{19,21},{21,23},{... | collective-permute-start | bytes 196616 | tf_op jit(solution)/shard_map/ppermute | solution.py:803
  6.2 5.7 %collective-permute-start.3 = (bf16[16,2048]{1,0:T(8,128)(2,1)S(1)}, bf16[16,2048]{1,0:T(8,128)(2,1)S(1)}, u32[]{:S(2)}, u32[]{:S(2)}) collective-permute-start(bf16[16,2048]{1,0:T(8,128)(2,1)S(1)} %get-tuple-element.57), channel_id=1, source_target_pairs={{1,2},{3,4},{5,6},{9,10},{11,12},{13,14},{17,18},{19,20},{21,22},{... | collective-permute-start | bytes 196616 | tf_op jit(solution)/shard_map/ppermute | solution.py:802
  15.2 6.0 %collective-permute-start.5 = (bf16[528,128]{1,0:T(8,128)(2,1)S(1)}, bf16[528,128]{1,0:T(8,128)(2,1)S(1)}, u32[]{:S(2)}, u32[]{:S(2)}) collective-permute-start(bf16[528,128]{1,0:T(8,128)(2,1)S(1)} %get-tuple-element.60), channel_id=1, source_target_pairs={{0,2},{1,3},{4,6},{5,7},{8,10},{9,11},{12,14},{13,15},{16,18},{17,... | collective-permute-start | bytes 405512 | tf_op jit(solution)/shard_map/ppermute | solution.py:817
  16.5 9.8 %collective-permute-start.8 = (bf16[128,2048]{1,0:T(8,128)(2,1)S(1)}, bf16[128,2048]{1,0:T(8,128)(2,1)S(1)}, u32[]{:S(2)}, u32[]{:S(2)}) collective-permute-start(bf16[128,2048]{1,0:T(8,128)(2,1)S(1)} %get-tuple-element.67), channel_id=1, source_target_pairs={{0,1},{1,0},{2,3},{3,2},{4,5},{5,4},{6,7},{7,6},{8,9},{9,8},{10,11... | collective-permute-start | bytes 1572872 | tf_op jit(solution)/shard_map/ppermute | solution.py:878
  19.9 8.0 %collective-permute-start.9 = (bf16[528,128]{1,0:T(8,128)(2,1)S(1)}, bf16[528,128]{1,0:T(8,128)(2,1)S(1)}, u32[]{:S(2)}, u32[]{:S(2)}) collective-permute-start(bf16[528,128]{1,0:T(8,128)(2,1)S(1)} %get-tuple-element.62.refs_0_), channel_id=1, source_target_pairs={{0,2},{1,3},{4,6},{5,7},{8,10},{9,11},{12,14},{13,15},{16,18},{17,... | collective-permute-start | bytes 405512 | tf_op jit(solution)/shard_map/ppermute | solution.py:817
  21.6 15.0 %collective-permute-start.7 = (bf16[528,128]{1,0:T(8,128)(2,1)S(1)}, bf16[528,128]{1,0:T(8,128)(2,1)S(1)}, u32[]{:S(2)}, u32[]{:S(2)}) collective-permute-start(bf16[528,128]{1,0:T(8,128)(2,1)S(1)} %join.2.after), channel_id=1, source_target_pairs={{2,4},{3,5},{4,6},{5,7},{10,12},{11,13},{12,14},{13,15},{18,20},{1... | collective-permute-start | bytes 405512 | tf_op jit(solution)/shard_map/ppermute | solution.py:817
  24.8 11.8 %collective-permute-start.6 = (bf16[528,128]{1,0:T(8,128)(2,1)S(1)}, bf16[528,128]{1,0:T(8,128)(2,1)S(1)}, u32[]{:S(2)}, u32[]{:S(2)}) collective-permute-start(bf16[528,128]{1,0:T(8,128)(2,1)S(1)} %join.2.after), channel_id=1, source_target_pairs={{2,6},{3,7},{10,14},{11,15},{18,22},{19,23},{26,30},{27,31}} | collective-permute-start | bytes 405512 | tf_op jit(solution)/shard_map/ppermute | solution.py:817
  28.3 10.0 %collective-permute-start.11 = (bf16[528,128]{1,0:T(8,128)(2,1)S(1)}, bf16[528,128]{1,0:T(8,128)(2,1)S(1)}, u32[]{:S(2)}, u32[]{:S(2)}) collective-permute-start(bf16[528,128]{1,0:T(8,128)(2,1)S(1)} %join.3), channel_id=1, source_target_pairs={{2,4},{3,5},{4,6},{5,7},{10,12},{11,13},{12,14},{13,15},{18,20},{1... | collective-permute-start | bytes 405512 | tf_op jit(solution)/shard_map/ppermute | solution.py:817
  29.6 8.7 %collective-permute-start.10 = (bf16[528,128]{1,0:T(8,128)(2,1)S(1)}, bf16[528,128]{1,0:T(8,128)(2,1)S(1)}, u32[]{:S(2)}, u32[]{:S(2)}) collective-permute-start(bf16[528,128]{1,0:T(8,128)(2,1)S(1)} %join.3), channel_id=1, source_target_pairs={{2,6},{3,7},{10,14},{11,15},{18,22},{19,23},{26,30},{27,31}} | collective-permute-start | bytes 405512 | tf_op jit(solution)/shard_map/ppermute | solution.py:817
  36.9 2.3 %collective-permute-start.12 = (bf16[128,512]{1,0:T(8,128)(2,1)S(1)}, bf16[128,512]{1,0:T(8,128)(2,1)S(1)}, u32[]{:S(2)}, u32[]{:S(2)}) collective-permute-start(bf16[128,512]{1,0:T(8,128)(2,1)S(1)} %get-tuple-element.95), channel_id=1, source_target_pairs={{0,1},{1,0},{2,3},{3,2},{4,5},{5,4},{6,7},{7,6},{8,9},{9,8},{10,11... | collective-permute-start | bytes 393224 | tf_op jit(solution)/shard_map/ppermute | solution.py:1068
  38.6 1.4 %collective-permute-start.13 = (bf16[128,512]{1,0:T(8,128)(2,1)S(1)}, bf16[128,512]{1,0:T(8,128)(2,1)S(1)}, u32[]{:S(2)}, u32[]{:S(2)}) collective-permute-start(bf16[128,512]{1,0:T(8,128)(2,1)S(1)} %get-tuple-element.96), channel_id=1, source_target_pairs={{0,1},{1,0},{2,3},{3,2},{4,5},{5,4},{6,7},{7,6},{8,9},{9,8},{10,11... | collective-permute-start | bytes 393224 | tf_op jit(solution)/shard_map/ppermute | solution.py:1068

commit v7 on v6

--- a/solution.py
+++ b/solution.py
@@ -49,7 +49,7 @@
 def encode(state):
     top = jnp.max(jnp.abs(state), axis=0, keepdims=True)
     scale = (top * 1.02 + 1e-30).astype(BF16).astype(F32)
-    grade = jnp.abs(state) / scale
+    grade = jnp.abs(state) * (1.0 / scale)
     level = jnp.exp2(grade * (2.0 * CODE) - CODE)
     return jnp.where(state < 0, -level, level).astype(BF16), scale
 
@@ -258,6 +258,15 @@
         gram = mm(split(keys[head]), pair)
         ratio = decay(columns[:, head : head + 1], run[head], t, j)
         coupling.append(jnp.where(t > j, gram * ratio * beta(head), 0.0))
+    writes = []
+    for head in range(heads):
+        value = conv(value_scratch, value_taps, lanes(head), lanes(first + head))
+        grow = jnp.exp(columns[:, head : head + 1])
+        write = jnp.concatenate([keys[head] * (beta(head) * grow), value * beta(head)], axis=1)
+        write = split(write)
+        write_out[head, 0] = write[0]
+        write_out[head, 1] = write[1]
+        writes.append(write)
     inverse = invert(coupling, t, j)
     mixed = []
     for head in range(heads):
@@ -269,14 +278,8 @@
     transits = []
     states = []
     for head in range(heads):
-        value = conv(value_scratch, value_taps, lanes(head), lanes(first + head))
-        grow = jnp.exp(columns[:, head : head + 1])
-        write = jnp.concatenate([keys[head] * (beta(head) * grow), value * beta(head)], axis=1)
-        write = split(write)
-        write_out[head, 0] = write[0]
-        write_out[head, 1] = write[1]
         last = run[head][:, CHUNK - 1 : CHUNK]
-        both = mm(split(mixed[head]), write)
+        both = mm(split(mixed[head]), writes[head])
         transits.append(jnp.where(t == j, jnp.exp(last), 0.0) - both[:, :128])
         states.append(both[:, 128:])
     return transits, states

time: 41.5 us -> 41.5 us (level)
  no operation moved by 1% of the time
where the time goes in v7:
time: 41.5 us; the launch traced here: 41 us
  Pallas kernels  22.1 us (53%)
  starting transfers between devices  17.2 us (41%)
  waiting for transfers between devices  1.32 us (3%)
    ppermute x6, starting transfers between devices, fan(): results.append(lax.ppermute(value, 'seq', route))  9.92 us
    pallas_call x2, Pallas kernels, per_device(): pl.pallas_call(functools.partial(lower_kernel, group, heads), out_shape=h...  6.6 us
    pallas_call x1, Pallas kernels, per_device(): pl.pallas_call(functools.partial(tail_kernel, level, 32 + 16 * (near + 1...  5.65 us
    pallas_call x1, Pallas kernels, per_device(): pl.pallas_call(upper_kernel, out_shape=held(8) + [struct((8, 128, 128))]...  4.33 us
    ppermute x1, starting transfers between devices, per_device(): lax.ppermute(halo, 'seq', [(i, i + 2) for i in range(1, size - 1, 2)])  3.19 us
    pallas_call x1, Pallas kernels, per_device(): pl.pallas_call(prepare_kernel, in_specs=[pl.BlockSpec(memory_space=pltpu....  1.71 us
    pallas_call x1, Pallas kernels, ask(): pl.pallas_call(functools.partial(asked_kernel, group, heads, piece * coun...  1.56 us
    ppermute x2, starting transfers between devices, per_device(): comes.append(lax.ppermute(leave, 'seq', cores))  1.47 us
  transfers between devices with their start and end apart: 14, of which 2 were waited for; matrix products, arithmetic and copies ran while one was open for 0% of the time, Pallas kernels for 44%

profile of v7, /device:TPU:11, one launch (start us, length us, event | category | flops | bytes accessed | tf_op | source)
XLA Modules:
  0.0 41.0 jit_solution(17574879347765768516)
XLA Ops:
  0.0 0.7 %collective-permute-start = (bf16[128,2048]{1,0:T(8,128)(2,1)}, bf16[128,2048]{1,0:T(8,128)(2,1)S(1)}, u32[]{:S(2)}, u32[]{:S(2)}) collective-permute-start(bf16[128,2048]{1,0:T(8,128)(2,1)} %key.1), channel_id=1, source_target_pairs={{0,1},{1,0},{2,3},{3,2},{4,5},{5,4},{6,7},{7,6},{8,9},{9,8},{10,11... | collective-permute-start | bytes 1572872 | tf_op jit(solution)/shard_map/ppermute | solution.py:760
  0.7 1.7 %prepare.1 = (bf16[128,1024]{1,0:T(8,128)(2,1)S(1)}, bf16[128,1024]{1,0:T(8,128)(2,1)S(1)}, bf16[128,1024]{1,0:T(8,128)(2,1)S(1)}, bf16[128,1024]{1,0:T(8,128)(2...) custom-call(bf16[128,2048]{1,0:T(8,128)(2,1)} %query.1, ...), custom_call_target="tpu_custom_call" | custom-call | tf_op jit(solution)/shard_map/prepare/pallas_call | solution.py:776
  2.4 0.6 %collective-permute-start.2 = (f32[208,128]{1,0:T(8,128)S(1)}, f32[208,128]{1,0:T(8,128)S(1)}, u32[]{:S(2)}, u32[]{:S(2)}) collective-permute-start(f32[208,128]{1,0:T(8,128)S(1)} %get-tuple-element.82.small_own.refs_5_.refs_7_.refs_2_.refs_3_), channel_id=1, source_target_pairs={{0,1},{1,0},{2,3},{3,2},{4,5},{5,4},{6,7},{7,6},{8,9},{9,8},{10,11... | collective-permute-start | bytes 319496 | tf_op jit(solution)/shard_map/ppermute | solution.py:804
  3.0 3.2 %collective-permute-start.4 = (bf16[16,2048]{1,0:T(8,128)(2,1)S(1)}, bf16[16,2048]{1,0:T(8,128)(2,1)S(1)}, u32[]{:S(2)}, u32[]{:S(2)}) collective-permute-start(bf16[16,2048]{1,0:T(8,128)(2,1)S(1)} %get-tuple-element.57), channel_id=1, source_target_pairs={{1,3},{3,5},{5,7},{9,11},{11,13},{13,15},{17,19},{19,21},{21,23},{... | collective-permute-start | bytes 196616 | tf_op jit(solution)/shard_map/ppermute | solution.py:806
  6.2 1.3 %collective-permute-start.3 = (bf16[16,2048]{1,0:T(8,128)(2,1)S(1)}, bf16[16,2048]{1,0:T(8,128)(2,1)S(1)}, u32[]{:S(2)}, u32[]{:S(2)}) collective-permute-start(bf16[16,2048]{1,0:T(8,128)(2,1)S(1)} %get-tuple-element.57), channel_id=1, source_target_pairs={{1,2},{3,4},{5,6},{9,10},{11,12},{13,14},{17,18},{19,20},{21,22},{... | collective-permute-start | bytes 196616 | tf_op jit(solution)/shard_map/ppermute | solution.py:805
  7.5 4.3 %upper.1 = (bf16[8,2,128,128]{3,2,1,0:T(8,128)(2,1)S(1)}, bf16[8,2,128,128]{3,2,1,0:T(8,128)(2,1)S(1)}, bf16[8,2,128,256]{3,2,1,0:T(8,128)(2,1)S(1)}, f32[8,128,128]{2,1,0:T(8,128)S(1)}, f32[8,128,128]{2,1,0:T(8,128)S(1)}) custom-call(bf16[128,1024]{1,0:T(8,128)(2,1)S(1)} %get-tuple-element.51.key_own, bf16[128,2048]{1,0:T(8,128)(2,1)S(1)} %collective-permute-done.key_other, ...), custom_call_target="tpu_custom_call" | custom-call | flops 4000000000 | bytes 1000000 | tf_op jit(solution)/shard_map/upper/pallas_call | solution.py:832
  11.9 3.3 %lower.2 = (bf16[4,2,128,128]{3,2,1,0:T(8,128)(2,1)S(1)}, bf16[4,2,128,128]{3,2,1,0:T(8,128)(2,1)S(1)}, bf16[4,2,128,256]{3,2,1,0:T(8,128)(2,1)S(1)}, f32[4,128,...) custom-call(bf16[128,1024]{1,0:T(8,128)(2,1)S(1)} %get-tuple-element, ...), custom_call_target="tpu_custom_call" | custom-call | flops 2500000000 | bytes 1000000 | tf_op jit(solution)/shard_map/lower/pallas_call | solution.py:854
  15.2 1.3 %collective-permute-start.5 = (bf16[528,128]{1,0:T(8,128)(2,1)S(1)}, bf16[528,128]{1,0:T(8,128)(2,1)S(1)}, u32[]{:S(2)}, u32[]{:S(2)}) collective-permute-start(bf16[528,128]{1,0:T(8,128)(2,1)S(1)} %get-tuple-element.60), channel_id=1, source_target_pairs={{0,2},{1,3},{4,6},{5,7},{8,10},{9,11},{12,14},{13,15},{16,18},{17,... | collective-permute-start | bytes 405512 | tf_op jit(solution)/shard_map/ppermute | solution.py:820
  16.5 3.3 %lower.3 = (bf16[4,2,128,128]{3,2,1,0:T(8,128)(2,1)S(1)}, bf16[4,2,128,128]{3,2,1,0:T(8,128)(2,1)S(1)}, bf16[4,2,128,256]{3,2,1,0:T(8,128)(2,1)S(1)}, f32[4,128,...) custom-call(bf16[128,1024]{1,0:T(8,128)(2,1)S(1)} %get-tuple-element, ...), custom_call_target="tpu_custom_call" | custom-call | flops 2500000000 | bytes 1000000 | tf_op jit(solution)/shard_map/lower/pallas_call | solution.py:854
  19.8 1.3 %collective-permute-start.9 = (bf16[528,128]{1,0:T(8,128)(2,1)S(1)}, bf16[528,128]{1,0:T(8,128)(2,1)S(1)}, u32[]{:S(2)}, u32[]{:S(2)}) collective-permute-start(bf16[528,128]{1,0:T(8,128)(2,1)S(1)} %get-tuple-element.62.refs_0_), channel_id=1, source_target_pairs={{0,2},{1,3},{4,6},{5,7},{8,10},{9,11},{12,14},{13,15},{16,18},{17,... | collective-permute-start | bytes 405512 | tf_op jit(solution)/shard_map/ppermute | solution.py:820
  21.2 0.4 join.2.after
  21.6 3.2 %collective-permute-start.7 = (bf16[528,128]{1,0:T(8,128)(2,1)S(1)}, bf16[528,128]{1,0:T(8,128)(2,1)S(1)}, u32[]{:S(2)}, u32[]{:S(2)}) collective-permute-start(bf16[528,128]{1,0:T(8,128)(2,1)S(1)} %join.2.after), channel_id=1, source_target_pairs={{2,4},{3,5},{4,6},{5,7},{10,12},{11,13},{12,14},{13,15},{18,20},{1... | collective-permute-start | bytes 405512 | tf_op jit(solution)/shard_map/ppermute | solution.py:820
  24.8 1.5 %collective-permute-start.6 = (bf16[528,128]{1,0:T(8,128)(2,1)S(1)}, bf16[528,128]{1,0:T(8,128)(2,1)S(1)}, u32[]{:S(2)}, u32[]{:S(2)}) collective-permute-start(bf16[528,128]{1,0:T(8,128)(2,1)S(1)} %join.2.after), channel_id=1, source_target_pairs={{2,6},{3,7},{10,14},{11,15},{18,22},{19,23},{26,30},{27,31}} | collective-permute-start | bytes 405512 | tf_op jit(solution)/shard_map/ppermute | solution.py:820
  26.3 1.6 %queries.1 = (f32[2,256,128]{2,1,0:T(8,128)S(1)}, f32[2,256,128]{2,1,0:T(8,128)S(1)}) custom-call(bf16[528,128]{1,0:T(8,128)(2,1)S(1)} %join.2.after, bf16[128,1024]{1,0:T(8,128)(2,1)S(1)} %get-tuple-element.69.refs_0_.refs_2_, bf16[128,2048]{1,0:T(8,128)(2,1)S(1)} %collective-permute-done.8.refs_1_.refs_3_.refs_5_.refs_6_, ...), custom_call_target="tpu_custom_call" | custom-call | flops 1000000 | bytes 1000000 | tf_op jit(solution)/shard_map/queries/pallas_call | solution.py:906
  27.9 0.4 join.3
  28.3 1.3 %collective-permute-start.11 = (bf16[528,128]{1,0:T(8,128)(2,1)S(1)}, bf16[528,128]{1,0:T(8,128)(2,1)S(1)}, u32[]{:S(2)}, u32[]{:S(2)}) collective-permute-start(bf16[528,128]{1,0:T(8,128)(2,1)S(1)} %join.3), channel_id=1, source_target_pairs={{2,4},{3,5},{4,6},{5,7},{10,12},{11,13},{12,14},{13,15},{18,20},{1... | collective-permute-start | bytes 405512 | tf_op jit(solution)/shard_map/ppermute | solution.py:820
  29.6 1.3 %collective-permute-start.10 = (bf16[528,128]{1,0:T(8,128)(2,1)S(1)}, bf16[528,128]{1,0:T(8,128)(2,1)S(1)}, u32[]{:S(2)}, u32[]{:S(2)}) collective-permute-start(bf16[528,128]{1,0:T(8,128)(2,1)S(1)} %join.3), channel_id=1, source_target_pairs={{2,6},{3,7},{10,14},{11,15},{18,22},{19,23},{26,30},{27,31}} | collective-permute-start | bytes 405512 | tf_op jit(solution)/shard_map/ppermute | solution.py:820
  30.9 5.6 %tail.1 = (f32[4,256,128]{2,1,0:T(8,128)S(1)}, f32[4,256,128]{2,1,0:T(8,128)S(1)}, f32[4,256,128]{2,1,0:T(8,128)S(1)}, f32[4,256,128]{2,1,0:T(8,128)S(1)}) custom-call(bf16[528,128]{1,0:T(8,128)(2,1)S(1)} %collective-permute-done.5.refs_1_.refs_0_, bf16[528,128]{1,0:T(8,128)(2,1)S(1)} %collective-permute-done.9.refs_2_.refs_1_, ...), custom_call_target="tpu_custom_call" | custom-call | flops 1000000 | bytes 1000000 | tf_op jit(solution)/shard_map/tail/pallas_call | solution.py:981
  36.6 0.3 finish.2
  36.9 1.3 %collective-permute-start.12 = (bf16[128,512]{1,0:T(8,128)(2,1)S(1)}, bf16[128,512]{1,0:T(8,128)(2,1)S(1)}, u32[]{:S(2)}, u32[]{:S(2)}) collective-permute-start(bf16[128,512]{1,0:T(8,128)(2,1)S(1)} %get-tuple-element.95), channel_id=1, source_target_pairs={{0,1},{1,0},{2,3},{3,2},{4,5},{5,4},{6,7},{7,6},{8,9},{9,8},{10,11... | collective-permute-start | bytes 393224 | tf_op jit(solution)/shard_map/ppermute | solution.py:1071
  38.3 0.3 finish.3
  38.7 0.6 %collective-permute-done.12.refs_2_ = bf16[128,512]{1,0:T(8,128)(2,1)S(1)} collective-permute-done((bf16[128,512]{1,0:T(8,128)(2,1)S(1)}, bf16[128,512]{1,0:T(8,128)(2,1)S(1)}, u32[]{:S(2)}, u32[]{:S(2)}) %collective-permute-start.12) | collective-permute-done | bytes 131104 | tf_op jit(solution)/shard_map/ppermute | solution.py:1071
  39.3 0.7 %collective-permute-done.13.refs_3_ = bf16[128,512]{1,0:T(8,128)(2,1)S(1)} collective-permute-done((bf16[128,512]{1,0:T(8,128)(2,1)S(1)}, bf16[128,512]{1,0:T(8,128)(2,1)S(1)}, u32[]{:S(2)}, u32[]{:S(2)}) %collective-permute-start.13) | collective-permute-done | bytes 131104 | tf_op jit(solution)/shard_map/ppermute | solution.py:1071
  40.0 0.8 %swap.1 = bf16[128,2048]{1,0:T(8,128)(2,1)} custom-call(bf16[128,512]{1,0:T(8,128)(2,1)S(1)} %get-tuple-element.91.refs_0_, bf16[128,512]{1,0:T(8,128)(2,1)S(1)} %get-tuple-element.94.refs_1_, bf16[128,512]{1,0:T(8,128)(2,1)S(1)} %collective-permute-done.12.refs_2_, bf16[128,512]{1,0:T(8,128)(2,1)S(1)} %collective-permute-done.13.refs_3_), custom_call_target="tpu_custom_call" | custom-call | tf_op jit(solution)/shard_map/swap/pallas_call | solution.py:1072
  (15 shorter events, 0.2 us)
Async XLA Ops:
  0.0 7.5 %collective-permute-start = (bf16[128,2048]{1,0:T(8,128)(2,1)}, bf16[128,2048]{1,0:T(8,128)(2,1)S(1)}, u32[]{:S(2)}, u32[]{:S(2)}) collective-permute-start(bf16[128,2048]{1,0:T(8,128)(2,1)} %key.1), channel_id=1, source_target_pairs={{0,1},{1,0},{2,3},{3,2},{4,5},{5,4},{6,7},{7,6},{8,9},{9,8},{10,11... | collective-permute-start | bytes 1572872 | tf_op jit(solution)/shard_map/ppermute | solution.py:760
  0.7 6.8 %collective-permute-start.1 = (bf16[128,2048]{1,0:T(8,128)(2,1)}, bf16[128,2048]{1,0:T(8,128)(2,1)S(1)}, u32[]{:S(2)}, u32[]{:S(2)}) collective-permute-start(bf16[128,2048]{1,0:T(8,128)(2,1)} %value.1), channel_id=1, source_target_pairs={{0,1},{1,0},{2,3},{3,2},{4,5},{5,4},{6,7},{7,6},{8,9},{9,8},{10,11... | collective-permute-start | bytes 1572872 | tf_op jit(solution)/shard_map/ppermute | solution.py:761
  2.4 5.1 %collective-permute-start.2 = (f32[208,128]{1,0:T(8,128)S(1)}, f32[208,128]{1,0:T(8,128)S(1)}, u32[]{:S(2)}, u32[]{:S(2)}) collective-permute-start(f32[208,128]{1,0:T(8,128)S(1)} %get-tuple-element.82.small_own.refs_5_.refs_7_.refs_2_.refs_3_), channel_id=1, source_target_pairs={{0,1},{1,0},{2,3},{3,2},{4,5},{5,4},{6,7},{7,6},{8,9},{9,8},{10,11... | collective-permute-start | bytes 319496 | tf_op jit(solution)/shard_map/ppermute | solution.py:804
  3.0 8.9 %collective-permute-start.4 = (bf16[16,2048]{1,0:T(8,128)(2,1)S(1)}, bf16[16,2048]{1,0:T(8,128)(2,1)S(1)}, u32[]{:S(2)}, u32[]{:S(2)}) collective-permute-start(bf16[16,2048]{1,0:T(8,128)(2,1)S(1)} %get-tuple-element.57), channel_id=1, source_target_pairs={{1,3},{3,5},{5,7},{9,11},{11,13},{13,15},{17,19},{19,21},{21,23},{... | collective-permute-start | bytes 196616 | tf_op jit(solution)/shard_map/ppermute | solution.py:806
  6.2 5.7 %collective-permute-start.3 = (bf16[16,2048]{1,0:T(8,128)(2,1)S(1)}, bf16[16,2048]{1,0:T(8,128)(2,1)S(1)}, u32[]{:S(2)}, u32[]{:S(2)}) collective-permute-start(bf16[16,2048]{1,0:T(8,128)(2,1)S(1)} %get-tuple-element.57), channel_id=1, source_target_pairs={{1,2},{3,4},{5,6},{9,10},{11,12},{13,14},{17,18},{19,20},{21,22},{... | collective-permute-start | bytes 196616 | tf_op jit(solution)/shard_map/ppermute | solution.py:805
  15.2 6.0 %collective-permute-start.5 = (bf16[528,128]{1,0:T(8,128)(2,1)S(1)}, bf16[528,128]{1,0:T(8,128)(2,1)S(1)}, u32[]{:S(2)}, u32[]{:S(2)}) collective-permute-start(bf16[528,128]{1,0:T(8,128)(2,1)S(1)} %get-tuple-element.60), channel_id=1, source_target_pairs={{0,2},{1,3},{4,6},{5,7},{8,10},{9,11},{12,14},{13,15},{16,18},{17,... | collective-permute-start | bytes 405512 | tf_op jit(solution)/shard_map/ppermute | solution.py:820
  16.5 9.8 %collective-permute-start.8 = (bf16[128,2048]{1,0:T(8,128)(2,1)S(1)}, bf16[128,2048]{1,0:T(8,128)(2,1)S(1)}, u32[]{:S(2)}, u32[]{:S(2)}) collective-permute-start(bf16[128,2048]{1,0:T(8,128)(2,1)S(1)} %get-tuple-element.67), channel_id=1, source_target_pairs={{0,1},{1,0},{2,3},{3,2},{4,5},{5,4},{6,7},{7,6},{8,9},{9,8},{10,11... | collective-permute-start | bytes 1572872 | tf_op jit(solution)/shard_map/ppermute | solution.py:881
  19.8 8.0 %collective-permute-start.9 = (bf16[528,128]{1,0:T(8,128)(2,1)S(1)}, bf16[528,128]{1,0:T(8,128)(2,1)S(1)}, u32[]{:S(2)}, u32[]{:S(2)}) collective-permute-start(bf16[528,128]{1,0:T(8,128)(2,1)S(1)} %get-tuple-element.62.refs_0_), channel_id=1, source_target_pairs={{0,2},{1,3},{4,6},{5,7},{8,10},{9,11},{12,14},{13,15},{16,18},{17,... | collective-permute-start | bytes 405512 | tf_op jit(solution)/shard_map/ppermute | solution.py:820
  21.6 15.0 %collective-permute-start.7 = (bf16[528,128]{1,0:T(8,128)(2,1)S(1)}, bf16[528,128]{1,0:T(8,128)(2,1)S(1)}, u32[]{:S(2)}, u32[]{:S(2)}) collective-permute-start(bf16[528,128]{1,0:T(8,128)(2,1)S(1)} %join.2.after), channel_id=1, source_target_pairs={{2,4},{3,5},{4,6},{5,7},{10,12},{11,13},{12,14},{13,15},{18,20},{1... | collective-permute-start | bytes 405512 | tf_op jit(solution)/shard_map/ppermute | solution.py:820
  24.8 11.8 %collective-permute-start.6 = (bf16[528,128]{1,0:T(8,128)(2,1)S(1)}, bf16[528,128]{1,0:T(8,128)(2,1)S(1)}, u32[]{:S(2)}, u32[]{:S(2)}) collective-permute-start(bf16[528,128]{1,0:T(8,128)(2,1)S(1)} %join.2.after), channel_id=1, source_target_pairs={{2,6},{3,7},{10,14},{11,15},{18,22},{19,23},{26,30},{27,31}} | collective-permute-start | bytes 405512 | tf_op jit(solution)/shard_map/ppermute | solution.py:820
  28.3 10.0 %collective-permute-start.11 = (bf16[528,128]{1,0:T(8,128)(2,1)S(1)}, bf16[528,128]{1,0:T(8,128)(2,1)S(1)}, u32[]{:S(2)}, u32[]{:S(2)}) collective-permute-start(bf16[528,128]{1,0:T(8,128)(2,1)S(1)} %join.3), channel_id=1, source_target_pairs={{2,4},{3,5},{4,6},{5,7},{10,12},{11,13},{12,14},{13,15},{18,20},{1... | collective-permute-start | bytes 405512 | tf_op jit(solution)/shard_map/ppermute | solution.py:820
  29.6 8.7 %collective-permute-start.10 = (bf16[528,128]{1,0:T(8,128)(2,1)S(1)}, bf16[528,128]{1,0:T(8,128)(2,1)S(1)}, u32[]{:S(2)}, u32[]{:S(2)}) collective-permute-start(bf16[528,128]{1,0:T(8,128)(2,1)S(1)} %join.3), channel_id=1, source_target_pairs={{2,6},{3,7},{10,14},{11,15},{18,22},{19,23},{26,30},{27,31}} | collective-permute-start | bytes 405512 | tf_op jit(solution)/shard_map/ppermute | solution.py:820
  36.9 2.3 %collective-permute-start.12 = (bf16[128,512]{1,0:T(8,128)(2,1)S(1)}, bf16[128,512]{1,0:T(8,128)(2,1)S(1)}, u32[]{:S(2)}, u32[]{:S(2)}) collective-permute-start(bf16[128,512]{1,0:T(8,128)(2,1)S(1)} %get-tuple-element.95), channel_id=1, source_target_pairs={{0,1},{1,0},{2,3},{3,2},{4,5},{5,4},{6,7},{7,6},{8,9},{9,8},{10,11... | collective-permute-start | bytes 393224 | tf_op jit(solution)/shard_map/ppermute | solution.py:1071
  38.6 1.4 %collective-permute-start.13 = (bf16[128,512]{1,0:T(8,128)(2,1)S(1)}, bf16[128,512]{1,0:T(8,128)(2,1)S(1)}, u32[]{:S(2)}, u32[]{:S(2)}) collective-permute-start(bf16[128,512]{1,0:T(8,128)(2,1)S(1)} %get-tuple-element.96), channel_id=1, source_target_pairs={{0,1},{1,0},{2,3},{3,2},{4,5},{5,4},{6,7},{7,6},{8,9},{9,8},{10,11... | collective-permute-start | bytes 393224 | tf_op jit(solution)/shard_map/ppermute | solution.py:1071

commit v8 on v6

--- a/solution.py
+++ b/solution.py
@@ -49,7 +49,7 @@
 def encode(state):
     top = jnp.max(jnp.abs(state), axis=0, keepdims=True)
     scale = (top * 1.02 + 1e-30).astype(BF16).astype(F32)
-    grade = jnp.abs(state) / scale
+    grade = jnp.abs(state) * (1.0 / scale)
     level = jnp.exp2(grade * (2.0 * CODE) - CODE)
     return jnp.where(state < 0, -level, level).astype(BF16), scale
 

time: 41.5 us -> 41.5 us (level)
  no operation moved by 1% of the time
where the time goes in v8:
time: 41.5 us; the launch traced here: 41 us
  Pallas kernels  22.1 us (53%)
  starting transfers between devices  17.2 us (41%)
  waiting for transfers between devices  1.32 us (3%)
    ppermute x6, starting transfers between devices, fan(): results.append(lax.ppermute(value, 'seq', route))  9.93 us
    pallas_call x2, Pallas kernels, per_device(): pl.pallas_call(functools.partial(lower_kernel, group, heads), out_shape=h...  6.62 us
    pallas_call x1, Pallas kernels, per_device(): pl.pallas_call(functools.partial(tail_kernel, level, 32 + 16 * (near + 1...  5.65 us
    pallas_call x1, Pallas kernels, per_device(): pl.pallas_call(upper_kernel, out_shape=held(8) + [struct((8, 128, 128))]...  4.32 us
    ppermute x1, starting transfers between devices, per_device(): lax.ppermute(halo, 'seq', [(i, i + 2) for i in range(1, size - 1, 2)])  3.19 us
    pallas_call x1, Pallas kernels, per_device(): pl.pallas_call(prepare_kernel, in_specs=[pl.BlockSpec(memory_space=pltpu....  1.71 us
    pallas_call x1, Pallas kernels, ask(): pl.pallas_call(functools.partial(asked_kernel, group, heads, piece * coun...  1.56 us
    ppermute x2, starting transfers between devices, per_device(): comes.append(lax.ppermute(leave, 'seq', cores))  1.47 us
  transfers between devices with their start and end apart: 14, of which 2 were waited for; matrix products, arithmetic and copies ran while one was open for 0% of the time, Pallas kernels for 44%

profile of v8, /device:TPU:11, one launch (start us, length us, event | category | flops | bytes accessed | tf_op | source)
XLA Modules:
  0.0 41.0 jit_solution(5885028438096894817)
XLA Ops:
  0.0 0.7 %collective-permute-start = (bf16[128,2048]{1,0:T(8,128)(2,1)}, bf16[128,2048]{1,0:T(8,128)(2,1)S(1)}, u32[]{:S(2)}, u32[]{:S(2)}) collective-permute-start(bf16[128,2048]{1,0:T(8,128)(2,1)} %key.1), channel_id=1, source_target_pairs={{0,1},{1,0},{2,3},{3,2},{4,5},{5,4},{6,7},{7,6},{8,9},{9,8},{10,11... | collective-permute-start | bytes 1572872 | tf_op jit(solution)/shard_map/ppermute | solution.py:757
  0.7 1.7 %prepare.1 = (bf16[128,1024]{1,0:T(8,128)(2,1)S(1)}, bf16[128,1024]{1,0:T(8,128)(2,1)S(1)}, bf16[128,1024]{1,0:T(8,128)(2,1)S(1)}, bf16[128,1024]{1,0:T(8,128)(2...) custom-call(bf16[128,2048]{1,0:T(8,128)(2,1)} %query.1, ...), custom_call_target="tpu_custom_call" | custom-call | tf_op jit(solution)/shard_map/prepare/pallas_call | solution.py:773
  2.4 0.6 %collective-permute-start.2 = (f32[208,128]{1,0:T(8,128)S(1)}, f32[208,128]{1,0:T(8,128)S(1)}, u32[]{:S(2)}, u32[]{:S(2)}) collective-permute-start(f32[208,128]{1,0:T(8,128)S(1)} %get-tuple-element.82.small_own.refs_5_.refs_7_.refs_2_.refs_3_), channel_id=1, source_target_pairs={{0,1},{1,0},{2,3},{3,2},{4,5},{5,4},{6,7},{7,6},{8,9},{9,8},{10,11... | collective-permute-start | bytes 319496 | tf_op jit(solution)/shard_map/ppermute | solution.py:801
  3.0 3.2 %collective-permute-start.4 = (bf16[16,2048]{1,0:T(8,128)(2,1)S(1)}, bf16[16,2048]{1,0:T(8,128)(2,1)S(1)}, u32[]{:S(2)}, u32[]{:S(2)}) collective-permute-start(bf16[16,2048]{1,0:T(8,128)(2,1)S(1)} %get-tuple-element.57), channel_id=1, source_target_pairs={{1,3},{3,5},{5,7},{9,11},{11,13},{13,15},{17,19},{19,21},{21,23},{... | collective-permute-start | bytes 196616 | tf_op jit(solution)/shard_map/ppermute | solution.py:803
  6.2 1.3 %collective-permute-start.3 = (bf16[16,2048]{1,0:T(8,128)(2,1)S(1)}, bf16[16,2048]{1,0:T(8,128)(2,1)S(1)}, u32[]{:S(2)}, u32[]{:S(2)}) collective-permute-start(bf16[16,2048]{1,0:T(8,128)(2,1)S(1)} %get-tuple-element.57), channel_id=1, source_target_pairs={{1,2},{3,4},{5,6},{9,10},{11,12},{13,14},{17,18},{19,20},{21,22},{... | collective-permute-start | bytes 196616 | tf_op jit(solution)/shard_map/ppermute | solution.py:802
  7.5 4.3 %upper.1 = (bf16[8,2,128,128]{3,2,1,0:T(8,128)(2,1)S(1)}, bf16[8,2,128,128]{3,2,1,0:T(8,128)(2,1)S(1)}, bf16[8,2,128,256]{3,2,1,0:T(8,128)(2,1)S(1)}, f32[8,128,128]{2,1,0:T(8,128)S(1)}, f32[8,128,128]{2,1,0:T(8,128)S(1)}) custom-call(bf16[128,1024]{1,0:T(8,128)(2,1)S(1)} %get-tuple-element.51.key_own, bf16[128,2048]{1,0:T(8,128)(2,1)S(1)} %collective-permute-done.key_other, ...), custom_call_target="tpu_custom_call" | custom-call | flops 4000000000 | bytes 1000000 | tf_op jit(solution)/shard_map/upper/pallas_call | solution.py:829
  11.8 3.3 %lower.2 = (bf16[4,2,128,128]{3,2,1,0:T(8,128)(2,1)S(1)}, bf16[4,2,128,128]{3,2,1,0:T(8,128)(2,1)S(1)}, bf16[4,2,128,256]{3,2,1,0:T(8,128)(2,1)S(1)}, f32[4,128,...) custom-call(bf16[128,1024]{1,0:T(8,128)(2,1)S(1)} %get-tuple-element, ...), custom_call_target="tpu_custom_call" | custom-call | flops 2500000000 | bytes 1000000 | tf_op jit(solution)/shard_map/lower/pallas_call | solution.py:851
  15.2 1.3 %collective-permute-start.5 = (bf16[528,128]{1,0:T(8,128)(2,1)S(1)}, bf16[528,128]{1,0:T(8,128)(2,1)S(1)}, u32[]{:S(2)}, u32[]{:S(2)}) collective-permute-start(bf16[528,128]{1,0:T(8,128)(2,1)S(1)} %get-tuple-element.60), channel_id=1, source_target_pairs={{0,2},{1,3},{4,6},{5,7},{8,10},{9,11},{12,14},{13,15},{16,18},{17,... | collective-permute-start | bytes 405512 | tf_op jit(solution)/shard_map/ppermute | solution.py:817
  16.5 3.3 %lower.3 = (bf16[4,2,128,128]{3,2,1,0:T(8,128)(2,1)S(1)}, bf16[4,2,128,128]{3,2,1,0:T(8,128)(2,1)S(1)}, bf16[4,2,128,256]{3,2,1,0:T(8,128)(2,1)S(1)}, f32[4,128,...) custom-call(bf16[128,1024]{1,0:T(8,128)(2,1)S(1)} %get-tuple-element, ...), custom_call_target="tpu_custom_call" | custom-call | flops 2500000000 | bytes 1000000 | tf_op jit(solution)/shard_map/lower/pallas_call | solution.py:851
  19.9 1.3 %collective-permute-start.9 = (bf16[528,128]{1,0:T(8,128)(2,1)S(1)}, bf16[528,128]{1,0:T(8,128)(2,1)S(1)}, u32[]{:S(2)}, u32[]{:S(2)}) collective-permute-start(bf16[528,128]{1,0:T(8,128)(2,1)S(1)} %get-tuple-element.62.refs_0_), channel_id=1, source_target_pairs={{0,2},{1,3},{4,6},{5,7},{8,10},{9,11},{12,14},{13,15},{16,18},{17,... | collective-permute-start | bytes 405512 | tf_op jit(solution)/shard_map/ppermute | solution.py:817
  21.2 0.4 join.2.after
  21.6 3.2 %collective-permute-start.7 = (bf16[528,128]{1,0:T(8,128)(2,1)S(1)}, bf16[528,128]{1,0:T(8,128)(2,1)S(1)}, u32[]{:S(2)}, u32[]{:S(2)}) collective-permute-start(bf16[528,128]{1,0:T(8,128)(2,1)S(1)} %join.2.after), channel_id=1, source_target_pairs={{2,4},{3,5},{4,6},{5,7},{10,12},{11,13},{12,14},{13,15},{18,20},{1... | collective-permute-start | bytes 405512 | tf_op jit(solution)/shard_map/ppermute | solution.py:817
  24.8 1.5 %collective-permute-start.6 = (bf16[528,128]{1,0:T(8,128)(2,1)S(1)}, bf16[528,128]{1,0:T(8,128)(2,1)S(1)}, u32[]{:S(2)}, u32[]{:S(2)}) collective-permute-start(bf16[528,128]{1,0:T(8,128)(2,1)S(1)} %join.2.after), channel_id=1, source_target_pairs={{2,6},{3,7},{10,14},{11,15},{18,22},{19,23},{26,30},{27,31}} | collective-permute-start | bytes 405512 | tf_op jit(solution)/shard_map/ppermute | solution.py:817
  26.3 1.6 %queries.1 = (f32[2,256,128]{2,1,0:T(8,128)S(1)}, f32[2,256,128]{2,1,0:T(8,128)S(1)}) custom-call(bf16[528,128]{1,0:T(8,128)(2,1)S(1)} %join.2.after, bf16[128,1024]{1,0:T(8,128)(2,1)S(1)} %get-tuple-element.69.refs_0_.refs_2_, bf16[128,2048]{1,0:T(8,128)(2,1)S(1)} %collective-permute-done.8.refs_1_.refs_3_.refs_5_.refs_6_, ...), custom_call_target="tpu_custom_call" | custom-call | flops 1000000 | bytes 1000000 | tf_op jit(solution)/shard_map/queries/pallas_call | solution.py:903
  27.9 0.4 join.3
  28.3 1.3 %collective-permute-start.11 = (bf16[528,128]{1,0:T(8,128)(2,1)S(1)}, bf16[528,128]{1,0:T(8,128)(2,1)S(1)}, u32[]{:S(2)}, u32[]{:S(2)}) collective-permute-start(bf16[528,128]{1,0:T(8,128)(2,1)S(1)} %join.3), channel_id=1, source_target_pairs={{2,4},{3,5},{4,6},{5,7},{10,12},{11,13},{12,14},{13,15},{18,20},{1... | collective-permute-start | bytes 405512 | tf_op jit(solution)/shard_map/ppermute | solution.py:817
  29.6 1.3 %collective-permute-start.10 = (bf16[528,128]{1,0:T(8,128)(2,1)S(1)}, bf16[528,128]{1,0:T(8,128)(2,1)S(1)}, u32[]{:S(2)}, u32[]{:S(2)}) collective-permute-start(bf16[528,128]{1,0:T(8,128)(2,1)S(1)} %join.3), channel_id=1, source_target_pairs={{2,6},{3,7},{10,14},{11,15},{18,22},{19,23},{26,30},{27,31}} | collective-permute-start | bytes 405512 | tf_op jit(solution)/shard_map/ppermute | solution.py:817
  31.0 5.6 %tail.1 = (f32[4,256,128]{2,1,0:T(8,128)S(1)}, f32[4,256,128]{2,1,0:T(8,128)S(1)}, f32[4,256,128]{2,1,0:T(8,128)S(1)}, f32[4,256,128]{2,1,0:T(8,128)S(1)}) custom-call(bf16[528,128]{1,0:T(8,128)(2,1)S(1)} %collective-permute-done.5.refs_1_.refs_0_, bf16[528,128]{1,0:T(8,128)(2,1)S(1)} %collective-permute-done.9.refs_2_.refs_1_, ...), custom_call_target="tpu_custom_call" | custom-call | flops 1000000 | bytes 1000000 | tf_op jit(solution)/shard_map/tail/pallas_call | solution.py:978
  36.6 0.3 finish.2
  36.9 1.3 %collective-permute-start.12 = (bf16[128,512]{1,0:T(8,128)(2,1)S(1)}, bf16[128,512]{1,0:T(8,128)(2,1)S(1)}, u32[]{:S(2)}, u32[]{:S(2)}) collective-permute-start(bf16[128,512]{1,0:T(8,128)(2,1)S(1)} %get-tuple-element.95), channel_id=1, source_target_pairs={{0,1},{1,0},{2,3},{3,2},{4,5},{5,4},{6,7},{7,6},{8,9},{9,8},{10,11... | collective-permute-start | bytes 393224 | tf_op jit(solution)/shard_map/ppermute | solution.py:1068
  38.3 0.3 finish.3
  38.7 0.6 %collective-permute-done.12.refs_2_ = bf16[128,512]{1,0:T(8,128)(2,1)S(1)} collective-permute-done((bf16[128,512]{1,0:T(8,128)(2,1)S(1)}, bf16[128,512]{1,0:T(8,128)(2,1)S(1)}, u32[]{:S(2)}, u32[]{:S(2)}) %collective-permute-start.12) | collective-permute-done | bytes 131104 | tf_op jit(solution)/shard_map/ppermute | solution.py:1068
  39.3 0.7 %collective-permute-done.13.refs_3_ = bf16[128,512]{1,0:T(8,128)(2,1)S(1)} collective-permute-done((bf16[128,512]{1,0:T(8,128)(2,1)S(1)}, bf16[128,512]{1,0:T(8,128)(2,1)S(1)}, u32[]{:S(2)}, u32[]{:S(2)}) %collective-permute-start.13) | collective-permute-done | bytes 131104 | tf_op jit(solution)/shard_map/ppermute | solution.py:1068
  40.0 0.8 %swap.1 = bf16[128,2048]{1,0:T(8,128)(2,1)} custom-call(bf16[128,512]{1,0:T(8,128)(2,1)S(1)} %get-tuple-element.91.refs_0_, bf16[128,512]{1,0:T(8,128)(2,1)S(1)} %get-tuple-element.94.refs_1_, bf16[128,512]{1,0:T(8,128)(2,1)S(1)} %collective-permute-done.12.refs_2_, bf16[128,512]{1,0:T(8,128)(2,1)S(1)} %collective-permute-done.13.refs_3_), custom_call_target="tpu_custom_call" | custom-call | tf_op jit(solution)/shard_map/swap/pallas_call | solution.py:1069
  (15 shorter events, 0.2 us)
Async XLA Ops:
  0.0 7.5 %collective-permute-start = (bf16[128,2048]{1,0:T(8,128)(2,1)}, bf16[128,2048]{1,0:T(8,128)(2,1)S(1)}, u32[]{:S(2)}, u32[]{:S(2)}) collective-permute-start(bf16[128,2048]{1,0:T(8,128)(2,1)} %key.1), channel_id=1, source_target_pairs={{0,1},{1,0},{2,3},{3,2},{4,5},{5,4},{6,7},{7,6},{8,9},{9,8},{10,11... | collective-permute-start | bytes 1572872 | tf_op jit(solution)/shard_map/ppermute | solution.py:757
  0.7 6.8 %collective-permute-start.1 = (bf16[128,2048]{1,0:T(8,128)(2,1)}, bf16[128,2048]{1,0:T(8,128)(2,1)S(1)}, u32[]{:S(2)}, u32[]{:S(2)}) collective-permute-start(bf16[128,2048]{1,0:T(8,128)(2,1)} %value.1), channel_id=1, source_target_pairs={{0,1},{1,0},{2,3},{3,2},{4,5},{5,4},{6,7},{7,6},{8,9},{9,8},{10,11... | collective-permute-start | bytes 1572872 | tf_op jit(solution)/shard_map/ppermute | solution.py:758
  2.4 5.1 %collective-permute-start.2 = (f32[208,128]{1,0:T(8,128)S(1)}, f32[208,128]{1,0:T(8,128)S(1)}, u32[]{:S(2)}, u32[]{:S(2)}) collective-permute-start(f32[208,128]{1,0:T(8,128)S(1)} %get-tuple-element.82.small_own.refs_5_.refs_7_.refs_2_.refs_3_), channel_id=1, source_target_pairs={{0,1},{1,0},{2,3},{3,2},{4,5},{5,4},{6,7},{7,6},{8,9},{9,8},{10,11... | collective-permute-start | bytes 319496 | tf_op jit(solution)/shard_map/ppermute | solution.py:801
  3.0 8.9 %collective-permute-start.4 = (bf16[16,2048]{1,0:T(8,128)(2,1)S(1)}, bf16[16,2048]{1,0:T(8,128)(2,1)S(1)}, u32[]{:S(2)}, u32[]{:S(2)}) collective-permute-start(bf16[16,2048]{1,0:T(8,128)(2,1)S(1)} %get-tuple-element.57), channel_id=1, source_target_pairs={{1,3},{3,5},{5,7},{9,11},{11,13},{13,15},{17,19},{19,21},{21,23},{... | collective-permute-start | bytes 196616 | tf_op jit(solution)/shard_map/ppermute | solution.py:803
  6.2 5.7 %collective-permute-start.3 = (bf16[16,2048]{1,0:T(8,128)(2,1)S(1)}, bf16[16,2048]{1,0:T(8,128)(2,1)S(1)}, u32[]{:S(2)}, u32[]{:S(2)}) collective-permute-start(bf16[16,2048]{1,0:T(8,128)(2,1)S(1)} %get-tuple-element.57), channel_id=1, source_target_pairs={{1,2},{3,4},{5,6},{9,10},{11,12},{13,14},{17,18},{19,20},{21,22},{... | collective-permute-start | bytes 196616 | tf_op jit(solution)/shard_map/ppermute | solution.py:802
  15.2 6.0 %collective-permute-start.5 = (bf16[528,128]{1,0:T(8,128)(2,1)S(1)}, bf16[528,128]{1,0:T(8,128)(2,1)S(1)}, u32[]{:S(2)}, u32[]{:S(2)}) collective-permute-start(bf16[528,128]{1,0:T(8,128)(2,1)S(1)} %get-tuple-element.60), channel_id=1, source_target_pairs={{0,2},{1,3},{4,6},{5,7},{8,10},{9,11},{12,14},{13,15},{16,18},{17,... | collective-permute-start | bytes 405512 | tf_op jit(solution)/shard_map/ppermute | solution.py:817
  16.5 9.8 %collective-permute-start.8 = (bf16[128,2048]{1,0:T(8,128)(2,1)S(1)}, bf16[128,2048]{1,0:T(8,128)(2,1)S(1)}, u32[]{:S(2)}, u32[]{:S(2)}) collective-permute-start(bf16[128,2048]{1,0:T(8,128)(2,1)S(1)} %get-tuple-element.67), channel_id=1, source_target_pairs={{0,1},{1,0},{2,3},{3,2},{4,5},{5,4},{6,7},{7,6},{8,9},{9,8},{10,11... | collective-permute-start | bytes 1572872 | tf_op jit(solution)/shard_map/ppermute | solution.py:878
  19.9 8.0 %collective-permute-start.9 = (bf16[528,128]{1,0:T(8,128)(2,1)S(1)}, bf16[528,128]{1,0:T(8,128)(2,1)S(1)}, u32[]{:S(2)}, u32[]{:S(2)}) collective-permute-start(bf16[528,128]{1,0:T(8,128)(2,1)S(1)} %get-tuple-element.62.refs_0_), channel_id=1, source_target_pairs={{0,2},{1,3},{4,6},{5,7},{8,10},{9,11},{12,14},{13,15},{16,18},{17,... | collective-permute-start | bytes 405512 | tf_op jit(solution)/shard_map/ppermute | solution.py:817
  21.6 15.0 %collective-permute-start.7 = (bf16[528,128]{1,0:T(8,128)(2,1)S(1)}, bf16[528,128]{1,0:T(8,128)(2,1)S(1)}, u32[]{:S(2)}, u32[]{:S(2)}) collective-permute-start(bf16[528,128]{1,0:T(8,128)(2,1)S(1)} %join.2.after), channel_id=1, source_target_pairs={{2,4},{3,5},{4,6},{5,7},{10,12},{11,13},{12,14},{13,15},{18,20},{1... | collective-permute-start | bytes 405512 | tf_op jit(solution)/shard_map/ppermute | solution.py:817
  24.8 11.8 %collective-permute-start.6 = (bf16[528,128]{1,0:T(8,128)(2,1)S(1)}, bf16[528,128]{1,0:T(8,128)(2,1)S(1)}, u32[]{:S(2)}, u32[]{:S(2)}) collective-permute-start(bf16[528,128]{1,0:T(8,128)(2,1)S(1)} %join.2.after), channel_id=1, source_target_pairs={{2,6},{3,7},{10,14},{11,15},{18,22},{19,23},{26,30},{27,31}} | collective-permute-start | bytes 405512 | tf_op jit(solution)/shard_map/ppermute | solution.py:817
  28.3 10.0 %collective-permute-start.11 = (bf16[528,128]{1,0:T(8,128)(2,1)S(1)}, bf16[528,128]{1,0:T(8,128)(2,1)S(1)}, u32[]{:S(2)}, u32[]{:S(2)}) collective-permute-start(bf16[528,128]{1,0:T(8,128)(2,1)S(1)} %join.3), channel_id=1, source_target_pairs={{2,4},{3,5},{4,6},{5,7},{10,12},{11,13},{12,14},{13,15},{18,20},{1... | collective-permute-start | bytes 405512 | tf_op jit(solution)/shard_map/ppermute | solution.py:817
  29.6 8.7 %collective-permute-start.10 = (bf16[528,128]{1,0:T(8,128)(2,1)S(1)}, bf16[528,128]{1,0:T(8,128)(2,1)S(1)}, u32[]{:S(2)}, u32[]{:S(2)}) collective-permute-start(bf16[528,128]{1,0:T(8,128)(2,1)S(1)} %join.3), channel_id=1, source_target_pairs={{2,6},{3,7},{10,14},{11,15},{18,22},{19,23},{26,30},{27,31}} | collective-permute-start | bytes 405512 | tf_op jit(solution)/shard_map/ppermute | solution.py:817
  36.9 2.3 %collective-permute-start.12 = (bf16[128,512]{1,0:T(8,128)(2,1)S(1)}, bf16[128,512]{1,0:T(8,128)(2,1)S(1)}, u32[]{:S(2)}, u32[]{:S(2)}) collective-permute-start(bf16[128,512]{1,0:T(8,128)(2,1)S(1)} %get-tuple-element.95), channel_id=1, source_target_pairs={{0,1},{1,0},{2,3},{3,2},{4,5},{5,4},{6,7},{7,6},{8,9},{9,8},{10,11... | collective-permute-start | bytes 393224 | tf_op jit(solution)/shard_map/ppermute | solution.py:1068
  38.6 1.4 %collective-permute-start.13 = (bf16[128,512]{1,0:T(8,128)(2,1)S(1)}, bf16[128,512]{1,0:T(8,128)(2,1)S(1)}, u32[]{:S(2)}, u32[]{:S(2)}) collective-permute-start(bf16[128,512]{1,0:T(8,128)(2,1)S(1)} %get-tuple-element.96), channel_id=1, source_target_pairs={{0,1},{1,0},{2,3},{3,2},{4,5},{5,4},{6,7},{7,6},{8,9},{9,8},{10,11... | collective-permute-start | bytes 393224 | tf_op jit(solution)/shard_map/ppermute | solution.py:1068
